TPU v7x, 32 devices: a whole 2x2x4 slice. The times are simulated.
32 devices in a mesh: fsdp: 2 (over y), ctx: 4 (over z), tp: 4 (over x, core).
Axes of the slice: x: 2, y: 2, z: 4, core: 2. Of those that a mesh axis runs over, the one named last changes fastest.
Arguments:
- layer_input: bfloat16 [4, 2048, 2048], P('fsdp', 'ctx'), may hold values from -6 to 6
- segment_ids: int32 [4, 2048], P('fsdp', 'ctx'), may hold values from 0 to 15, never falling along the last dimension, each value on 1 to 1536 neighbouring positions
- qkv_weight: bfloat16 [2048, 3, 2048], P('fsdp', None, 'tp'), may hold values from -0.125 to 0.125
- qv_bias: bfloat16 [2, 2048], P(None, 'tp'), may hold values from -1.1953125 to 1.1953125
- out_weight: bfloat16 [2048, 2048], P('tp', 'fsdp'), may hold values from -1.5 to 1.5
- out_bias: bfloat16 [2048], replicated, may hold values from -1.1953125 to 1.1953125
- norm1_gain: bfloat16 [2048], replicated, may hold values from 0.5 to 1.5
- norm1_bias: bfloat16 [2048], replicated, may hold values from -1.1953125 to 1.1953125
- up_weight: bfloat16 [2048, 8192], P('fsdp', 'tp'), may hold values from -0.125 to 0.125
- up_bias: bfloat16 [8192], P('tp'), may hold values from -1.1953125 to 1.1953125
- down_weight: bfloat16 [8192, 2048], P('tp', 'fsdp'), may hold values from -0.0625 to 0.0625
- down_bias: bfloat16 [2048], replicated, may hold values from -1.1953125 to 1.1953125
- norm2_gain: bfloat16 [2048], replicated, may hold values from 0.5 to 1.5
- norm2_bias: bfloat16 [2048], replicated, may hold values from -1.1953125 to 1.1953125
- out_grad: bfloat16 [4, 2048, 2048], P('fsdp', 'ctx'), may hold values from -6 to 6
Outputs:
- layer_output: bfloat16 [4, 2048, 2048], P('fsdp', 'ctx')
- input_grad: float32 [4, 2048, 2048], P('fsdp', 'ctx')
- qkv_weight_grad: float32 [2048, 3, 2048], P('fsdp', None, 'tp')
- qv_bias_grad: float32 [2, 2048], P(None, 'tp')
- out_weight_grad: float32 [2048, 2048], P('tp', 'fsdp')
- out_bias_grad: float32 [2048], replicated
- norm1_gain_grad: float32 [2048], replicated
- norm1_bias_grad: float32 [2048], replicated
- up_weight_grad: float32 [2048, 8192], P('fsdp', 'tp')
- up_bias_grad: float32 [8192], P('tp')
- down_weight_grad: float32 [8192, 2048], P('tp', 'fsdp')
- down_bias_grad: float32 [2048], replicated
- norm2_gain_grad: float32 [2048], replicated
- norm2_bias_grad: float32 [2048], replicated
Inputs may be any that keep to these rules, and one draw needn't show every extreme that they name: `segment_ids`: along each row the ids never fall, and each id names 1 to 1536 tokens in a row; in every row one id names exactly 1536 tokens.
All inputs are finite; a program needn't handle non-finite values.
Results may differ from a plain program's by a relative error of at most 0.013.
Values may be sent and summed in bfloat16 or wider, within the bound.
No kernel may reach another device: no remote copies, remote signals or barrier semaphores. Data moves between devices by JAX's collectives and lax.ppermute only.
A program may use at most 320 MiB of HBM per device.

v0:
```python
import math

import jax
import jax.numpy as jnp
from jax import lax
from jax.sharding import PartitionSpec as P

HEAD = 128


EPSILON = 1e-12
NEGATIVE = -1e30


def layer_norm(hidden, gain, shift):
    center = hidden - jnp.mean(hidden, axis=-1, keepdims=True)
    spread = jnp.mean(center * center, axis=-1, keepdims=True)
    return center * lax.rsqrt(spread + EPSILON) * gain + shift


def gelu_tanh(pre):
    return 0.5 * pre * (1.0 + jnp.tanh(0.7978845608028654 * (pre + 0.044715 * pre * pre * pre)))


def contract_rows(left, right):
    return lax.dot_general(
        left, right, (((0,), (0,)), ((), ())), preferred_element_type=jnp.float32
    )


def contract_cols(left, right):
    return lax.dot_general(
        left, right, (((1,), (1,)), ((), ())), preferred_element_type=jnp.float32
    )


def row_blocks(seg_query, seg_key):
    length = seg_key.shape[0]
    block_width = min(512, length)
    blocks = []
    for begin in range(0, length, block_width):
        same = seg_query[:, None] == seg_key[begin : begin + block_width][None, :]
        blocks.append((begin, block_width, jnp.any(same), same))
    return blocks


def row_scores(query_row, key_row, blocks):
    scale = 1.0 / math.sqrt(HEAD)
    pieces = []
    for begin, block_width, live, same in blocks:
        key_block = key_row[begin : begin + block_width]

        def row_compute():
            raw = (
                jnp.einsum("qhd,khd->hqk", query_row, key_block, preferred_element_type=jnp.float32)
                * scale
            )
            return jnp.where(same[None], raw, NEGATIVE)

        def row_skipped():
            return jnp.full(
                (query_row.shape[1], query_row.shape[0], block_width), NEGATIVE, jnp.float32
            )

        pieces.append(lax.cond(live, row_compute, row_skipped))
    return jnp.concatenate(pieces, axis=-1)


def attend_row(operands):
    query_row, key_row, value_row, seg_query, seg_key = operands
    blocks = row_blocks(seg_query, seg_key)
    scores = row_scores(query_row, key_row, blocks)
    top = jnp.max(scores, axis=-1, keepdims=True)
    log_total = top + jnp.log(jnp.sum(jnp.exp(scores - top), axis=-1, keepdims=True))
    probs_low = jnp.exp(scores - log_total).astype(jnp.bfloat16)
    mixed = jnp.zeros(query_row.shape, jnp.float32)
    for begin, block_width, live, same in blocks:
        prob_piece = probs_low[:, :, begin : begin + block_width]
        value_block = value_row[begin : begin + block_width]
        mixed = mixed + lax.cond(
            live,
            lambda: jnp.einsum(
                "hqk,khd->qhd", prob_piece, value_block, preferred_element_type=jnp.float32
            ),
            lambda: jnp.zeros(query_row.shape, jnp.float32),
        )
    rows_here = query_row.shape[0]
    return (mixed.astype(jnp.bfloat16).reshape(rows_here, -1), log_total[:, :, 0])


def attend_back_row(operands):
    query_row, key_row, value_row, seg_query, seg_key, log_total, grad_row = operands
    scale = 1.0 / math.sqrt(HEAD)
    blocks = row_blocks(seg_query, seg_key)
    scores = row_scores(query_row, key_row, blocks)
    probs = jnp.exp(scores - log_total[:, :, None])
    probs_low = probs.astype(jnp.bfloat16)
    heads_here = query_row.shape[1]
    rows_here = query_row.shape[0]
    d_pieces = []
    for begin, block_width, live, same in blocks:
        value_block = value_row[begin : begin + block_width]
        d_pieces.append(
            lax.cond(
                live,
                lambda: jnp.einsum(
                    "qhd,khd->hqk", grad_row, value_block, preferred_element_type=jnp.float32
                ),
                lambda: jnp.zeros((heads_here, rows_here, block_width), jnp.float32),
            )
        )
    d_probs = jnp.concatenate(d_pieces, axis=-1)
    weighted = jnp.sum(probs * d_probs, axis=-1, keepdims=True)
    d_scores = (probs * (d_probs - weighted)).astype(jnp.bfloat16)
    d_query = jnp.zeros(query_row.shape, jnp.float32)
    key_parts = []
    value_parts = []
    for begin, block_width, live, same in blocks:
        key_block = key_row[begin : begin + block_width]
        score_piece = d_scores[:, :, begin : begin + block_width]
        prob_piece = probs_low[:, :, begin : begin + block_width]

        def attend_compute():
            return (
                jnp.einsum(
                    "hqk,khd->qhd", score_piece, key_block, preferred_element_type=jnp.float32
                ),
                jnp.einsum(
                    "hqk,qhd->khd", score_piece, query_row, preferred_element_type=jnp.float32
                ),
                jnp.einsum(
                    "hqk,qhd->khd", prob_piece, grad_row, preferred_element_type=jnp.float32
                ),
            )

        def attend_skipped():
            return (
                jnp.zeros(query_row.shape, jnp.float32),
                jnp.zeros((block_width, heads_here, HEAD), jnp.float32),
                jnp.zeros((block_width, heads_here, HEAD), jnp.float32),
            )

        query_part, key_part, value_part = lax.cond(live, attend_compute, attend_skipped)
        d_query = d_query + query_part
        key_parts.append(key_part)
        value_parts.append(value_part)
    length = key_row.shape[0]
    d_keys = (jnp.concatenate(key_parts, axis=0) * scale).reshape(length, heads_here * HEAD)
    d_values = jnp.concatenate(value_parts, axis=0).reshape(length, heads_here * HEAD)
    return ((d_query * scale).reshape(rows_here, heads_here * HEAD), d_keys, d_values)


def local(
    layer_input,
    segment_ids,
    qkv_weight,
    qv_bias,
    out_weight,
    out_bias,
    norm1_gain,
    norm1_bias,
    up_weight,
    up_bias,
    down_weight,
    down_bias,
    norm2_gain,
    norm2_bias,
    out_grad,
):
    rows, local_len, width = layer_input.shape
    tokens = rows * local_len
    flat_input = layer_input.reshape(tokens, width)
    joint_weight, output_weight, upward_weight, downward_weight = (
        lax.all_gather(qkv_weight, "fsdp", axis=0, tiled=True),
        lax.all_gather(out_weight, "fsdp", axis=1, tiled=True),
        lax.all_gather(up_weight, "fsdp", axis=0, tiled=True),
        lax.all_gather(down_weight, "fsdp", axis=1, tiled=True),
    )
    local_width = joint_weight.shape[2]
    heads_here = local_width // HEAD
    joint_flat = joint_weight.reshape(width, 3 * local_width)
    projections = jnp.dot(flat_input, joint_flat, preferred_element_type=jnp.float32).reshape(
        tokens, 3, local_width
    )
    bias_pair = qv_bias.astype(jnp.float32)
    queries = (projections[:, 0] + bias_pair[0]).astype(jnp.bfloat16)
    keys_low = projections[:, 1].astype(jnp.bfloat16)
    values_low = (projections[:, 2] + bias_pair[1]).astype(jnp.bfloat16)
    all_keys, all_values, all_segments = (
        lax.all_gather(keys_low.reshape(rows, local_len, local_width), "ctx", axis=1, tiled=True),
        lax.all_gather(values_low.reshape(rows, local_len, local_width), "ctx", axis=1, tiled=True),
        lax.all_gather(segment_ids, "ctx", axis=1, tiled=True),
    )
    full_len = all_keys.shape[1]
    query_rows = queries.reshape(rows, local_len, heads_here, HEAD)
    key_rows = all_keys.reshape(rows, full_len, heads_here, HEAD)
    value_rows = all_values.reshape(rows, full_len, heads_here, HEAD)
    attended_rows, log_totals = lax.map(
        attend_row, (query_rows, key_rows, value_rows, segment_ids, all_segments)
    )
    attended = attended_rows.reshape(tokens, local_width)
    attn_out = lax.psum(
        jnp.dot(attended, output_weight, preferred_element_type=jnp.float32), "tp"
    ) + out_bias.astype(jnp.float32)
    gain_one = norm1_gain.astype(jnp.float32)
    shift_one = norm1_bias.astype(jnp.float32)
    gain_two = norm2_gain.astype(jnp.float32)
    shift_two = norm2_bias.astype(jnp.float32)
    norm_one, norm_one_pull = jax.vjp(
        layer_norm, flat_input.astype(jnp.float32) + attn_out, gain_one, shift_one
    )
    norm_one_low = norm_one.astype(jnp.bfloat16)
    pre_act = jnp.dot(
        norm_one_low, upward_weight, preferred_element_type=jnp.float32
    ) + up_bias.astype(jnp.float32)
    activation, gelu_pull = jax.vjp(gelu_tanh, pre_act)
    act_low = activation.astype(jnp.bfloat16)
    mlp_out = lax.psum(
        jnp.dot(act_low, downward_weight, preferred_element_type=jnp.float32), "tp"
    ) + down_bias.astype(jnp.float32)
    normed, norm_two_pull = jax.vjp(layer_norm, norm_one + mlp_out, gain_two, shift_two)
    layer_output = normed.astype(jnp.bfloat16).reshape(rows, local_len, width)
    d_normed = out_grad.reshape(tokens, width).astype(jnp.float32)
    d_second, gain_two_grad, shift_two_grad = norm_two_pull(d_normed)
    d_mlp_low = d_second.astype(jnp.bfloat16)
    down_bias_grad = jnp.sum(d_mlp_low, axis=0, dtype=jnp.float32)
    down_weight_grad = contract_rows(act_low, d_mlp_low)
    (d_pre,) = gelu_pull(contract_cols(d_mlp_low, downward_weight))
    d_pre_low = d_pre.astype(jnp.bfloat16)
    up_bias_grad = jnp.sum(d_pre_low, axis=0, dtype=jnp.float32)
    up_weight_grad = contract_rows(norm_one_low, d_pre_low)
    d_norm_one = d_second + lax.psum(contract_cols(d_pre_low, upward_weight), "tp")
    d_first, gain_one_grad, shift_one_grad = norm_one_pull(d_norm_one)
    d_attn_low = d_first.astype(jnp.bfloat16)
    out_bias_grad = jnp.sum(d_attn_low, axis=0, dtype=jnp.float32)
    out_weight_grad = contract_rows(attended, d_attn_low)
    d_attended = contract_cols(d_attn_low, output_weight).astype(jnp.bfloat16)
    d_query, d_key_rows, d_value_rows = lax.map(
        attend_back_row,
        (
            query_rows,
            key_rows,
            value_rows,
            segment_ids,
            all_segments,
            log_totals,
            d_attended.reshape(rows, local_len, heads_here, HEAD),
        ),
    )
    key_share, value_share = (
        lax.psum_scatter(d_key_rows, "ctx", scatter_dimension=1, tiled=True),
        lax.psum_scatter(d_value_rows, "ctx", scatter_dimension=1, tiled=True),
    )
    d_query_low = d_query.reshape(tokens, local_width).astype(jnp.bfloat16)
    d_key_low = key_share.reshape(tokens, local_width).astype(jnp.bfloat16)
    d_value_low = value_share.reshape(tokens, local_width).astype(jnp.bfloat16)
    d_joint = jnp.stack([d_query_low, d_key_low, d_value_low], axis=1).reshape(
        tokens, 3 * local_width
    )
    joint_grad = contract_rows(flat_input, d_joint).reshape(width, 3, local_width)
    input_grad = (d_first + lax.psum(contract_cols(d_joint, joint_flat), "tp")).reshape(
        rows, local_len, width
    )
    bias_grads = jnp.stack(
        [
            jnp.sum(d_query_low, axis=0, dtype=jnp.float32),
            jnp.sum(d_value_low, axis=0, dtype=jnp.float32),
        ]
    )
    small = lax.psum(
        (
            bias_grads,
            out_bias_grad,
            gain_one_grad,
            shift_one_grad,
            up_bias_grad,
            down_bias_grad,
            gain_two_grad,
            shift_two_grad,
        ),
        ("fsdp", "ctx"),
    )
    shares = (
        lax.psum_scatter(joint_grad, ("fsdp", "ctx"), scatter_dimension=0, tiled=True),
        lax.psum_scatter(out_weight_grad, ("fsdp", "ctx"), scatter_dimension=1, tiled=True),
        lax.psum_scatter(up_weight_grad, ("fsdp", "ctx"), scatter_dimension=0, tiled=True),
        lax.psum_scatter(down_weight_grad, ("fsdp", "ctx"), scatter_dimension=1, tiled=True),
    )
    spread = (
        lax.all_gather(shares[0], "ctx", axis=0, tiled=True),
        lax.all_gather(shares[1], "ctx", axis=1, tiled=True),
        lax.all_gather(shares[2], "ctx", axis=0, tiled=True),
        lax.all_gather(shares[3], "ctx", axis=1, tiled=True),
    )
    return (
        layer_output,
        input_grad,
        spread[0],
        small[0],
        spread[1],
        small[1],
        small[2],
        small[3],
        spread[2],
        small[4],
        spread[3],
        small[5],
        small[6],
        small[7],
    )


def solution(mesh):
    return jax.shard_map(
        local,
        mesh=mesh,
        in_specs=(
            P("fsdp", "ctx", None),
            P("fsdp", "ctx"),
            P("fsdp", None, "tp"),
            P(None, "tp"),
            P("tp", "fsdp"),
            P(),
            P(),
            P(),
            P("fsdp", "tp"),
            P("tp"),
            P("tp", "fsdp"),
            P(),
            P(),
            P(),
            P("fsdp", "ctx", None),
        ),
        out_specs=(
            P("fsdp", "ctx", None),
            P("fsdp", "ctx", None),
            P("fsdp", None, "tp"),
            P(None, "tp"),
            P("tp", "fsdp"),
            P(),
            P(),
            P(),
            P("fsdp", "tp"),
            P("tp"),
            P("tp", "fsdp"),
            P(),
            P(),
            P(),
        ),
        check_vma=False,
    )
```

profile of v0, /device:TPU:0, one launch (start us, length us, event | category | flops | bytes accessed | tf_op | source)
XLA Modules:
  0.0 3267.6 jit_solution(8020912910166900562)
XLA Ops:
  8.0 84.7 %all-gather.11.cloned.1.call-done = bf16[2048,3,512]{2,0,1:T(8,128)(2,1)} async-done(((bf16[1024,3,512]{2,0,1:T(8,128)(2,1)}), bf16[2048,3,512]{2,0,1:T(8,128)(2,1)}) %all-gather.11.cloned.1.call-update) | async-done | bytes 6291472 | tf_op jit(solution)/shard_map/all_gather | solution.py:174
  124.0 13.4 all_gather.33
  143.4 53.2 %all-gather.15.cloned.1.call-done = bf16[2,2048,512]{2,1,0:T(8,128)(2,1)} async-done(((bf16[2,512,512]{2,1,0:T(8,128)(2,1)}), bf16[2,2048,512]{2,1,0:T(8,128)(2,1)}) %all-gather.15.cloned.1.call-update) | async-done | bytes 4194320 | tf_op jit(solution)/shard_map/all_gather | solution.py:190
  202.8 75.2 %all-gather.13.cloned.1.call-done = bf16[2,2048,512]{1,2,0:T(8,128)(2,1)} async-done(((bf16[2,512,512]{1,2,0:T(8,128)(2,1)}), bf16[2,2048,512]{1,2,0:T(8,128)(2,1)}) %all-gather.13.cloned.1.call-update) | async-done | bytes 4194320 | tf_op jit(solution)/shard_map/all_gather | solution.py:191
  278.1 146.0 %while.26 = (s32[]{:T(128)}, bf16[2,512,512]{2,1,0:T(8,128)(2,1)}, f32[2,4,512]{2,1,0:T(4,128)S(1)}, s32[2,512]{1,0:T(2,128)S(1)}, s32[2,2048]{1,0:T(2,128)S(1)}...) while((s32[]{:T(128)}, bf16[2,512,512]{2,1,0:T(8,128)(2,1)}, ...), condition=%wide.region_26.27_spmd, body=%wide.region_0.26_spmd.sunk | while | flops 2205153280 | bytes 185235968 | solution.py:198
  433.3 149.3 %all-reduce.6.cloned.1.call-done = f32[1024,2048]{1,0:T(8,128)} async-done(((f32[1024,2048]{1,0:T(8,128)}), f32[1024,2048]{1,0:T(8,128)}) %all-reduce.6.cloned.1.call-update) | async-done | bytes 8388624 | tf_op jit(solution)/shard_map/psum | solution.py:202
  593.3 94.9 %all-gather.19.cloned.1.call-done = bf16[2048,2048]{1,0:T(8,128)(2,1)} async-done(((bf16[1024,2048]{1,0:T(8,128)(2,1)}), bf16[2048,2048]{1,0:T(8,128)(2,1)}) %all-gather.19.cloned.1.call-update) | async-done | bytes 8388624 | tf_op jit(solution)/shard_map/all_gather | solution.py:176
  688.2 15.8 fusion.132
  704.0 89.8 %all-gather.21.cloned.1.call-done = bf16[2048,2048]{1,0:T(8,128)(2,1)} async-done(((bf16[2048,1024]{1,0:T(8,128)(2,1)}), bf16[2048,2048]{1,0:T(8,128)(2,1)}) %all-gather.21.cloned.1.call-update) | async-done | bytes 8388624 | tf_op jit(solution)/shard_map/all_gather | solution.py:177
  793.7 17.3 fusion.129
  811.8 152.3 %all-reduce.8.cloned.1.call-done = f32[1024,2048]{1,0:T(8,128)} async-done(((f32[1024,2048]{1,0:T(8,128)}), f32[1024,2048]{1,0:T(8,128)}) %all-reduce.8.cloned.1.call-update) | async-done | bytes 8388624 | tf_op jit(solution)/shard_map/psum | solution.py:218
  987.3 20.8 convert_reduce_fusion.2
  1010.0 13.5 fusion.144
  1023.7 153.1 %all-reduce.10.cloned.1.call-done = f32[1024,2048]{1,0:T(8,128)} async-done(((f32[1024,2048]{1,0:T(8,128)}), f32[1024,2048]{1,0:T(8,128)}) %all-reduce.10.cloned.1.call-update) | async-done | bytes 8388624 | tf_op jit(solution)/shard_map/psum | solution.py:232
  1203.7 256.4 %while.27 = (s32[]{:T(128)}, bf16[2,512,512]{1,2,0:T(8,128)(2,1)}, f32[2,2048,512]{1,2,0:T(8,128)}, f32[2,2048,512]{1,2,0:T(8,128)}, s32[2,512]{1,0:T(2,128)S(1)...) while((s32[]{:T(128)}, bf16[2,512,512]{1,2,0:T(8,128)(2,1)}, ...), condition=%wide.region_68.69_spmd, body=%wide.region_38.68_spmd.sunk | while | flops 5484318720 | bytes 302578912 | solution.py:238
  1248.0 31.5 multiply_convert_fusion.5
  1376.0 31.5 multiply_convert_fusion.5
  1468.1 16.4 fusion.130
  1485.2 17.3 fusion.128
  1505.2 98.9 %reduce-scatter.7.cloned.1.call-done = f32[2,512,512]{1,2,0:T(8,128)} async-done(((f32[2,2048,512]{1,2,0:T(8,128)}), f32[2,512,512]{1,2,0:T(8,128)}) %reduce-scatter.7.cloned.1.call-update) | async-done | bytes 2097168 | tf_op jit(solution)/shard_map/reduce_scatter | solution.py:251
  1607.1 144.5 %reduce-scatter.9.cloned.1.call-done = f32[2,512,512]{1,2,0:T(8,128)} async-done(((f32[2,2048,512]{1,2,0:T(8,128)}), f32[2,512,512]{1,2,0:T(8,128)}) %reduce-scatter.9.cloned.1.call-update) | async-done | bytes 2097168 | tf_op jit(solution)/shard_map/reduce_scatter | solution.py:252
  1772.1 12.7 copy.76
  1784.9 59.9 %reduce-scatter.13.cloned.1.call-done = f32[512,256]{1,0:T(8,128)} async-done(((f32[512,2048]{1,0:T(8,128)}), f32[512,256]{1,0:T(8,128)}) %reduce-scatter.13.cloned.1.call-update) | async-done | bytes 524304 | tf_op jit(solution)/shard_map/reduce_scatter | solution.py:285
  1855.9 274.9 %reduce-scatter.15.cloned.1.call-done = f32[256,2048]{1,0:T(8,128)} async-done(((f32[2048,2048]{1,0:T(8,128)}), f32[256,2048]{1,0:T(8,128)}) %reduce-scatter.15.cloned.1.call-update) | async-done | bytes 2097168 | tf_op jit(solution)/shard_map/reduce_scatter | solution.py:286
  2130.8 284.8 %reduce-scatter.17.cloned.1.call-done = f32[2048,256]{1,0:T(8,128)} async-done(((f32[2048,2048]{1,0:T(8,128)}), f32[2048,256]{1,0:T(8,128)}) %reduce-scatter.17.cloned.1.call-update) | async-done | bytes 2097168 | tf_op jit(solution)/shard_map/reduce_scatter | solution.py:287
  2415.7 210.6 %reduce-scatter.11.cloned.1.call-done = f32[256,3,512]{2,0,1:T(8,128)} async-done(((f32[2048,3,512]{2,0,1:T(8,128)}), f32[256,3,512]{2,0,1:T(8,128)}) %reduce-scatter.11.cloned.1.call-update) | async-done | bytes 1572880 | tf_op jit(solution)/shard_map/reduce_scatter | solution.py:284
  2629.3 43.5 %all-gather.25.cloned.1.call-done = f32[512,1024]{1,0:T(8,128)} async-done(((f32[512,256]{1,0:T(8,128)}), f32[512,1024]{1,0:T(8,128)}) %all-gather.25.cloned.1.call-update) | async-done | bytes 2097168 | tf_op jit(solution)/shard_map/all_gather | solution.py:291
  2672.9 36.4 %all-reduce = (f32[2,512]{1,0:T(2,128)}, f32[2048]{0:T(1024)}, f32[2048]{0:T(1024)}, f32[2048]{0:T(1024)}, f32[2048]{0:T(1024)}, /*index=5*/f32[2048]{0:T(1024)}, f32[2048]{0:T(1024)}, f32[2048]{0:T(1024)}) all-reduce(f32[2,512]{1,0:T(2,128)S(1)} %pad_maximum_fusion.5, ...), channel_id=1, replica_groups=mesh['fsdp'=2,'ctx'=4,'tp'=4] {'fsdp','ctx'}, use_global_device_ids=true, to_apply=%region_75.76 | all-reduce | flops 15360 | bytes 122880 | tf_op jit(solution)/shard_map/psum | solution.py:270
  2709.3 118.2 %all-reduce.12.cloned.1.call-done = f32[1024,2048]{1,0:T(8,128)} async-done(((f32[1024,2048]{1,0:T(8,128)}), f32[1024,2048]{1,0:T(8,128)}) %all-reduce.12.cloned.1.call-update) | async-done | bytes 8388624 | tf_op jit(solution)/shard_map/psum | solution.py:261
  2838.0 140.8 %all-gather.27.cloned.1.call-done = f32[1024,2048]{1,0:T(8,128)} async-done(((f32[256,2048]{1,0:T(8,128)}), f32[1024,2048]{1,0:T(8,128)}) %all-gather.27.cloned.1.call-update) | async-done | bytes 8388624 | tf_op jit(solution)/shard_map/all_gather | solution.py:292
  2978.8 149.5 %all-gather.29.cloned.1.call-done = f32[2048,1024]{1,0:T(8,128)} async-done(((f32[2048,256]{1,0:T(8,128)}), f32[2048,1024]{1,0:T(8,128)}) %all-gather.29.cloned.1.call-update) | async-done | bytes 8388624 | tf_op jit(solution)/shard_map/all_gather | solution.py:293
  3128.4 115.1 %all-gather.23.cloned.1.call-done = f32[1024,3,512]{2,0,1:T(8,128)} async-done(((f32[256,3,512]{2,0,1:T(8,128)}), f32[1024,3,512]{2,0,1:T(8,128)}) %all-gather.23.cloned.1.call-update) | async-done | bytes 6291472 | tf_op jit(solution)/shard_map/all_gather | solution.py:290
  (449 shorter events, 684.6 us)
Async XLA Ops:
  7.2 85.5 %all-gather.11.cloned.1.call-start = ((), (), s32[]{:S(2)}) async-start(), calls=%async_computation.6 | async-start | bytes 9437184 | tf_op jit(solution)/shard_map/all_gather | solution.py:174
  7.9 188.7 %all-gather.15.cloned.1.call-start = ((), (), s32[]{:S(2)}) async-start(), calls=%async_computation.8 | async-start | bytes 5242880 | tf_op jit(solution)/shard_map/all_gather | solution.py:190
  115.5 162.5 %all-gather.13.cloned.1.call-start = ((), (), s32[]{:S(2)}) async-start(), calls=%async_computation.7 | async-start | bytes 5242880 | tf_op jit(solution)/shard_map/all_gather | solution.py:191
  123.4 300.7 %all-gather.17.cloned.1.call-start = ((), (), s32[]{:S(2)}) async-start(), calls=%async_computation.9 | async-start | bytes 3145728 | tf_op jit(solution)/shard_map/all_gather | solution.py:175
  124.0 458.6 %all-reduce.6.cloned.1.call-start = ((), (), s32[]{:S(2)}) async-start(), calls=%async_computation.10 | async-start | bytes 16777216 | tf_op jit(solution)/shard_map/psum | solution.py:202
  431.8 256.3 %all-gather.19.cloned.1.call-start = ((), (), s32[]{:S(2)}) async-start(), calls=%async_computation.11 | async-start | bytes 12582912 | tf_op jit(solution)/shard_map/all_gather | solution.py:176
  432.4 361.3 %all-gather.21.cloned.1.call-start = ((), (), s32[]{:S(2)}) async-start(), calls=%async_computation.12 | async-start | bytes 12582912 | tf_op jit(solution)/shard_map/all_gather | solution.py:177
  433.2 531.0 %all-reduce.8.cloned.1.call-start = ((), (), s32[]{:S(2)}) async-start(), calls=%async_computation.13 | async-start | bytes 16777216 | tf_op jit(solution)/shard_map/psum | solution.py:218
  433.2 755.0 %copy-start.38 = (f32[2048]{0:T(1024)}, f32[2048]{0:T(1024)S(1)}, u32[]{:S(2)}) copy-start(f32[2048]{0:T(1024)S(1)} %convert_element_type.182) | copy-start | bytes 24580
  433.3 554.0 %copy-start.56 = (f32[2048]{0:T(1024)}, f32[2048]{0:T(1024)S(1)}, u32[]{:S(2)}) copy-start(f32[2048]{0:T(1024)S(1)} %convert_element_type.185) | copy-start | bytes 24580
  588.4 599.8 %copy-start.42 = (f32[1024]{0:T(1024)}, f32[1024]{0:T(1024)S(1)}, u32[]{:S(2)}) copy-start(f32[1024]{0:T(1024)S(1)} %broadcast_multiply_fusion.1) | copy-start | bytes 12292
  593.3 594.9 %copy-start.44 = (f32[1024]{0:T(1024)}, f32[1024]{0:T(1024)S(1)}, u32[]{:S(2)}) copy-start(f32[1024]{0:T(1024)S(1)} %fusion.126) | copy-start | bytes 12292
  811.1 365.7 %all-reduce.10.cloned.1.call-start = ((), (), s32[]{:S(2)}) async-start(), calls=%async_computation.14 | async-start | bytes 16777216 | tf_op jit(solution)/shard_map/psum | solution.py:232
  1023.6 580.5 %reduce-scatter.7.cloned.1.call-start = ((), (), s32[]{:S(2)}) async-start(), calls=%async_computation.15 | async-start | bytes 10485760 | tf_op jit(solution)/shard_map/reduce_scatter | solution.py:251
  1460.2 291.5 %reduce-scatter.9.cloned.1.call-start = ((), (), s32[]{:S(2)}) async-start(), calls=%async_computation.16 | async-start | bytes 10485760 | tf_op jit(solution)/shard_map/reduce_scatter | solution.py:252
  1461.0 383.8 %reduce-scatter.13.cloned.1.call-start = ((), (), s32[]{:S(2)}) async-start(), calls=%async_computation.20 | async-start | bytes 4718592 | tf_op jit(solution)/shard_map/reduce_scatter | solution.py:285
  1468.0 662.7 %reduce-scatter.15.cloned.1.call-start = ((), (), s32[]{:S(2)}) async-start(), calls=%async_computation.22 | async-start | bytes 18874368 | tf_op jit(solution)/shard_map/reduce_scatter | solution.py:286
  1484.5 931.1 %reduce-scatter.17.cloned.1.call-start = ((), (), s32[]{:S(2)}) async-start(), calls=%async_computation.24 | async-start | bytes 18874368 | tf_op jit(solution)/shard_map/reduce_scatter | solution.py:287
  1502.5 1123.7 %reduce-scatter.11.cloned.1.call-start = ((), (), s32[]{:S(2)}) async-start(), calls=%async_computation.18 | async-start | bytes 14155776 | tf_op jit(solution)/shard_map/reduce_scatter | solution.py:284
  1784.8 888.0 %all-gather.25.cloned.1.call-start = ((), (), s32[]{:S(2)}) async-start(), calls=%async_computation.21 | async-start | bytes 2621440 | tf_op jit(solution)/shard_map/all_gather | solution.py:291
  1844.8 982.7 %all-reduce.12.cloned.1.call-start = ((), (), s32[]{:S(2)}) async-start(), calls=%async_computation.17 | async-start | bytes 16777216 | tf_op jit(solution)/shard_map/psum | solution.py:261
  1855.7 773.4 %copy-start.28 = (bf16[2,512,512]{1,2,0:T(8,128)(2,1)S(1)}, bf16[2,512,512]{1,2,0:T(8,128)(2,1)}, u32[]{:S(2)}) copy-start(bf16[2,512,512]{1,2,0:T(8,128)(2,1)} %get-tuple-element.398) | copy-start | bytes 3145732
  1855.7 817.1 %copy-start.48 = (f32[2048]{0:T(1024)S(1)}, f32[2048]{0:T(1024)}, u32[]{:S(2)}) copy-start(f32[2048]{0:T(1024)} %get-tuple-element.489) | copy-start | bytes 24580
  1855.7 817.1 %copy-start.49 = (f32[2048]{0:T(1024)S(1)}, f32[2048]{0:T(1024)}, u32[]{:S(2)}) copy-start(f32[2048]{0:T(1024)} %get-tuple-element.540) | copy-start | bytes 24580
  1855.7 817.2 %copy-start.50 = (f32[2048]{0:T(1024)S(1)}, f32[2048]{0:T(1024)}, u32[]{:S(2)}) copy-start(f32[2048]{0:T(1024)} %get-tuple-element.544) | copy-start | bytes 24580
  1855.8 817.2 %copy-start.53 = (f32[2048]{0:T(1024)S(1)}, f32[2048]{0:T(1024)}, u32[]{:S(2)}) copy-start(f32[2048]{0:T(1024)} %get-tuple-element.487) | copy-start | bytes 24580
  1855.8 817.2 %copy-start.54 = (f32[2048]{0:T(1024)S(1)}, f32[2048]{0:T(1024)}, u32[]{:S(2)}) copy-start(f32[2048]{0:T(1024)} %get-tuple-element.491) | copy-start | bytes 24580
  1855.8 817.2 %copy-start.55 = (f32[2048]{0:T(1024)S(1)}, f32[2048]{0:T(1024)}, u32[]{:S(2)}) copy-start(f32[2048]{0:T(1024)} %get-tuple-element.542) | copy-start | bytes 24580
  1855.8 971.7 %copy-start.47 = (f32[1024]{0:T(1024)S(1)}, f32[1024]{0:T(1024)}, u32[]{:S(2)}) copy-start(f32[1024]{0:T(1024)} %copy-done.46) | copy-start | bytes 12292
  1855.8 1123.0 %all-gather.27.cloned.1.call-start = ((), (), s32[]{:S(2)}) async-start(), calls=%async_computation.23 | async-start | bytes 10485760 | tf_op jit(solution)/shard_map/all_gather | solution.py:292
  2130.8 997.6 %all-gather.29.cloned.1.call-start = ((), (), s32[]{:S(2)}) async-start(), calls=%async_computation.25 | async-start | bytes 10485760 | tf_op jit(solution)/shard_map/all_gather | solution.py:293
  2415.6 827.8 %all-gather.23.cloned.1.call-start = ((), (), s32[]{:S(2)}) async-start(), calls=%async_computation.19 | async-start | bytes 7864320 | tf_op jit(solution)/shard_map/all_gather | solution.py:290
  (80 other events, 1550.9 us)
Sparse Core Ops, SparseCore 0:
  9.6 83.0 all-gather.10
  115.6 80.9 all-gather.14
  198.8 79.2 all-gather.12
  279.5 31.6 all-gather.16
  431.9 150.5 all-reduce.5
  584.0 104.1 all-gather.18
  689.7 103.9 all-gather.20
  811.2 152.8 all-reduce.7
  1023.7 153.0 all-reduce.9
  1460.3 143.7 reduce-scatter.6
  1606.5 145.1 reduce-scatter.8
  1755.8 89.0 reduce-scatter.12
  1849.1 281.6 reduce-scatter.14
  2134.4 281.1 reduce-scatter.16
  2419.5 206.7 reduce-scatter.10
  2627.8 45.0 all-gather.24
  2675.9 151.5 all-reduce.11
  2829.0 149.7 all-gather.26
  2980.5 147.8 all-gather.28
  3129.9 113.5 all-gather.22
where the time goes:
time: 3270 us
  waiting for transfers between devices  2500 us (76%)
  matrix products  315 us (10%)
  other arithmetic  229 us (7%)
  local copies, waits for them, and re-layouts  148 us (5%)
  blocking collectives  49.7 us (2%)
    reduce_scatter x1, waiting for transfers between devices, local(): lax.psum_scatter(down_weight_grad, ('fsdp', 'ctx'), scatter_dimension=1,...  285 us
    reduce_scatter x1, waiting for transfers between devices, local(): lax.psum_scatter(up_weight_grad, ('fsdp', 'ctx'), scatter_dimension=0, ti...  275 us
    reduce_scatter x1, waiting for transfers between devices, local(): lax.psum_scatter(joint_grad, ('fsdp', 'ctx'), scatter_dimension=0, tiled=...  211 us
    psum x1, waiting for transfers between devices, local(): lax.psum(contract_cols(d_pre_low, upward_weight), 'tp')  153 us
    psum x1, waiting for transfers between devices, local(): lax.psum(jnp.dot(act_low, downward_weight, preferred_element_type=jnp.flo...  152 us
    all_gather x1, waiting for transfers between devices, local(): lax.all_gather(shares[3], 'ctx', axis=1, tiled=True)  150 us
    psum x1, waiting for transfers between devices, local(): lax.psum(jnp.dot(attended, output_weight, preferred_element_type=jnp.floa...  149 us
    reduce_scatter x1, waiting for transfers between devices, local(): lax.psum_scatter(d_value_rows, 'ctx', scatter_dimension=1, tiled=True)  145 us
  transfers between devices with their start and end apart: 20, of which 19 were waited for; matrix products, arithmetic and copies ran while one was open for 9% of the time, Pallas kernels for 0%

commit v1 on v0

v1 whole, which is shorter than its diff:
```python
import functools
import math

import jax
import jax.numpy as jnp
from jax import lax
from jax.experimental import pallas as pl
from jax.experimental.pallas import tpu as pltpu
from jax.sharding import PartitionSpec as P

HEAD = 128
EPSILON = 1e-12
NEGATIVE = -1e30
LOG2E = 1.4426950408889634
VMEM_LIMIT = 56 * 2**20

BF16 = jnp.bfloat16
F32 = jnp.float32


def dot(left, right, left_dim, right_dim):
    return lax.dot_general(
        left, right, (((left_dim,), (right_dim,)), ((), ())), preferred_element_type=F32
    )


def core_swap(value):
    size = lax.axis_size("tp")
    return lax.ppermute(value, "tp", [(i, i ^ 1) for i in range(size)])


def chip_swap(value):
    size = lax.axis_size("tp")
    return lax.ppermute(value, "tp", [(i, i ^ 2) for i in range(size)])


def shift(value, axis, by):
    size = lax.axis_size(axis)
    return lax.ppermute(value, axis, [(i, (i + by) % size) for i in range(size)])


def after(value, *others):
    return lax.optimization_barrier((value, *others))[0]


def line_sum(value):
    first = lax.ppermute(value, "ctx", [(0, 1), (3, 2)])
    pair = (value.astype(F32) + first.astype(F32)).astype(BF16)
    second = lax.ppermute(pair, "ctx", [(1, 2), (2, 1)])
    total = (pair.astype(F32) + second.astype(F32)).astype(BF16)
    third = lax.ppermute(total, "ctx", [(1, 0), (2, 3)])
    place = lax.axis_index("ctx")
    return jnp.where((place == 0) | (place == 3), third, total)


def rotate(value, axis, by, count):
    size = value.shape[axis]
    block = size // count
    if count == 1:
        return value
    twice = jnp.concatenate([value, value], axis=axis)
    if count == 2:
        swapped = lax.slice_in_dim(twice, block, block + size, axis=axis)
        return jnp.where(by == 0, value, swapped)
    return lax.dynamic_slice_in_dim(twice, by * block, size, axis=axis)


def project_kernel(blocks, x_ref, *refs):
    weights, bias_ref, outs = refs[:blocks], refs[blocks], refs[blocks + 1 :]
    total = bias_ref[...].astype(F32)
    depth = x_ref.shape[1] // blocks
    acc = None
    for index, weight in enumerate(weights):
        part = dot(x_ref[:, index * depth : (index + 1) * depth], weight[...], 1, 0)
        acc = part if acc is None else acc + part
    low = (acc + total).astype(BF16)
    for slot, out in enumerate(outs):
        out[...] = low[:, slot * HEAD : (slot + 1) * HEAD]


def project(x, weights, bias):
    tokens, width = x.shape
    columns = weights[0].shape[1]
    heads = columns // HEAD
    tile = 512
    return pl.pallas_call(
        functools.partial(project_kernel, len(weights)),
        grid=(tokens // tile,),
        in_specs=[pl.BlockSpec((tile, width), lambda i: (i, 0))]
        + [pl.BlockSpec(w.shape, lambda i: (0, 0)) for w in weights]
        + [pl.BlockSpec((1, columns), lambda i: (0, 0))],
        out_specs=[pl.BlockSpec((tile, HEAD), lambda i: (i, 0))] * heads,
        out_shape=[jax.ShapeDtypeStruct((tokens, HEAD), BF16)] * heads,
        compiler_params=pltpu.CompilerParams(vmem_limit_bytes=VMEM_LIMIT),
        cost_estimate=pl.CostEstimate(
            flops=2 * tokens * width * columns,
            bytes_accessed=2 * (tokens * width + width * columns + tokens * columns),
            transcendentals=0,
        ),
        name="project",
    )(x, *weights, bias)


def grad_kernel(pairs, has_add, *refs):
    out = refs[-1]
    acc = None
    for index in range(pairs):
        part = dot(refs[2 * index][...], refs[2 * index + 1][...], 0, 0)
        acc = part if acc is None else acc + part
    if has_add:
        acc = acc + refs[2 * pairs][...].astype(F32)
    out[...] = acc.astype(out.dtype)


def weight_grad(lefts, rights, left_cols, right_cols, add=None):
    row_from, rows = left_cols
    col_from, cols = right_cols
    row_tile, col_tile = min(1024, rows), min(512, cols)
    depth = sum(v.shape[0] for v in lefts)
    specs, values = [], []
    row_base, col_base = row_from // row_tile, col_from // col_tile
    for left, right in zip(lefts, rights):
        specs.append(pl.BlockSpec((left.shape[0], row_tile), lambda i, j: (0, i + row_base)))
        specs.append(pl.BlockSpec((right.shape[0], col_tile), lambda i, j: (0, j + col_base)))
        values += [left, right]
    if add is not None:
        specs.append(pl.BlockSpec((row_tile, col_tile), lambda i, j: (i, j)))
        values.append(add)
    return pl.pallas_call(
        functools.partial(grad_kernel, len(lefts), add is not None),
        grid=(rows // row_tile, cols // col_tile),
        in_specs=specs,
        out_specs=pl.BlockSpec((row_tile, col_tile), lambda i, j: (i, j)),
        out_shape=jax.ShapeDtypeStruct((rows, cols), BF16),
        compiler_params=pltpu.CompilerParams(vmem_limit_bytes=VMEM_LIMIT),
        cost_estimate=pl.CostEstimate(
            flops=2 * rows * cols * depth,
            bytes_accessed=2 * (depth * rows + depth * cols + 2 * rows * cols),
            transcendentals=0,
        ),
        name="weight_grad",
    )(*values)


def gather_blocks(scratch, sources):
    size = sources[0].shape[0]
    for index, source in enumerate(sources):
        scratch[index * size : (index + 1) * size, :] = source[...]


def attend_kernel(parts, block, live, *refs):
    q_in, k_in, v_in = refs[:parts], refs[parts : 2 * parts], refs[2 * parts : 3 * parts]
    seg_row, seg_col = refs[3 * parts : 3 * parts + 2]
    outs = refs[3 * parts + 2 : 4 * parts + 2]
    mixed_ref, total_ref = refs[4 * parts + 2 : 4 * parts + 4]
    qs, ks, vs, scores, top, total, mixed = refs[4 * parts + 4 :]
    at = pl.program_id(0)
    count = qs.shape[0] // block

    @pl.when(at == 0)
    def _():
        gather_blocks(qs, q_in)
        gather_blocks(ks, k_in)
        gather_blocks(vs, v_in)

    here = pl.multiple_of(at * block, block)
    query = qs[pl.ds(here, block), :]
    seg_query = seg_row[:, pl.ds(here, block)]
    top[...] = jnp.full_like(top, NEGATIVE)
    total[...] = jnp.zeros_like(total)
    mixed[...] = jnp.zeros_like(mixed)

    def score(step, masked):
        rows = pl.ds(pl.multiple_of(step * block, block), block)
        raw = dot(ks[rows, :], query, 1, 1) * (LOG2E / math.sqrt(HEAD))
        if masked:
            raw = jnp.where(seg_col[rows, 0:1] == seg_query, raw, NEGATIVE)
        scores[rows, :] = raw
        top[...] = jnp.maximum(top[...], jnp.max(raw, axis=0, keepdims=True))

    def first(step, carry):
        pl.when(live[at, step] == 1)(functools.partial(score, step, True))
        pl.when(live[at, step] == 2)(functools.partial(score, step, False))
        return carry

    def second(step, carry):
        @pl.when(live[at, step] > 0)
        def _():
            rows = pl.ds(pl.multiple_of(step * block, block), block)
            weight = jnp.exp2(scores[rows, :] - top[...])
            total[...] += jnp.sum(weight, axis=0, keepdims=True)
            mixed[...] += dot(vs[rows, :], weight.astype(BF16), 0, 0)

        return carry

    lax.fori_loop(0, count, first, 0)
    lax.fori_loop(0, count, second, 0)
    result = mixed[...] / total[...]
    mixed_ref[:, pl.ds(here, block)] = result
    total_ref[:, pl.ds(here, block)] = top[...] + jnp.log2(total[...])
    low = result.T.astype(BF16)
    per = count // parts
    for slot, out in enumerate(outs):

        @pl.when(at // per == slot)
        def _(out=out):
            out[pl.ds(pl.multiple_of((at % per) * block, block), block), :] = low


def attend(row, queries, keys, values, seg_row, seg_col, live):
    parts = len(queries)
    length = seg_row.shape[2]
    size = length // parts
    block = length // live.shape[1]
    part_spec = pl.BlockSpec((size, HEAD), lambda i, s: (row, 0))
    whole = lambda i, s: (0, 0)
    flops = 2 * 2 * length * length * HEAD * 5 // 8
    return pl.pallas_call(
        functools.partial(attend_kernel, parts, block),
        grid_spec=pltpu.PrefetchScalarGridSpec(
            num_scalar_prefetch=1,
            grid=(length // block,),
            in_specs=[part_spec] * (3 * parts)
            + [
                pl.BlockSpec((None, 1, length), lambda i, s: (row, 0, 0)),
                pl.BlockSpec((None, length, HEAD), lambda i, s: (row, 0, 0)),
            ],
            out_specs=[pl.BlockSpec((size, HEAD), whole)] * parts
            + [pl.BlockSpec((HEAD, length), whole), pl.BlockSpec((1, length), whole)],
            scratch_shapes=[pltpu.VMEM((length, HEAD), BF16)] * 3
            + [
                pltpu.VMEM((length, block), F32),
                pltpu.VMEM((1, block), F32),
                pltpu.VMEM((1, block), F32),
                pltpu.VMEM((HEAD, block), F32),
            ],
        ),
        out_shape=[jax.ShapeDtypeStruct((size, HEAD), BF16)] * parts
        + [
            jax.ShapeDtypeStruct((HEAD, length), F32),
            jax.ShapeDtypeStruct((1, length), F32),
        ],
        compiler_params=pltpu.CompilerParams(vmem_limit_bytes=VMEM_LIMIT),
        cost_estimate=pl.CostEstimate(
            flops=flops, bytes_accessed=8 * length * HEAD, transcendentals=length * length // 2
        ),
        name="attend",
    )(live[row], *queries, *keys, *values, seg_row, seg_col)


def attend_back_kernel(parts, block, live, *refs):
    q_in, k_in, v_in = refs[:parts], refs[parts : 2 * parts], refs[2 * parts : 3 * parts]
    g_in = refs[3 * parts : 4 * parts]
    seg_row, seg_col, mixed_ref, total_ref = refs[4 * parts : 4 * parts + 4]
    outs = refs[4 * parts + 4 : 5 * parts + 4]
    qs, ks, vs, gs, d_keys, d_values, d_query = refs[5 * parts + 4 :]
    at = pl.program_id(0)
    count = qs.shape[0] // block
    scale = 1.0 / math.sqrt(HEAD)

    @pl.when(at == 0)
    def _():
        gather_blocks(qs, q_in)
        gather_blocks(ks, k_in)
        gather_blocks(vs, v_in)
        gather_blocks(gs, g_in)
        d_keys[...] = jnp.zeros_like(d_keys)
        d_values[...] = jnp.zeros_like(d_values)

    here = pl.multiple_of(at * block, block)
    query = qs[pl.ds(here, block), :]
    grad = gs[pl.ds(here, block), :]
    seg_query = seg_row[:, pl.ds(here, block)]
    log_total = total_ref[:, pl.ds(here, block)]
    weighted = jnp.sum(
        mixed_ref[:, pl.ds(here, block)] * grad.astype(F32).T, axis=0, keepdims=True
    )
    d_query[...] = jnp.zeros_like(d_query)

    def back(step, masked):
        rows = pl.ds(pl.multiple_of(step * block, block), block)
        key, value = ks[rows, :], vs[rows, :]
        raw = dot(key, query, 1, 1) * (LOG2E / math.sqrt(HEAD))
        if masked:
            raw = jnp.where(seg_col[rows, 0:1] == seg_query, raw, NEGATIVE)
        probs = jnp.exp2(raw - log_total)
        d_scores = (probs * (dot(value, grad, 1, 1) - weighted)).astype(BF16)
        d_values[rows, :] += dot(probs.astype(BF16), grad, 1, 0)
        d_keys[rows, :] += dot(d_scores, query, 1, 0)
        d_query[...] += dot(d_scores, key, 0, 0)

    def step_of(step, carry):
        pl.when(live[at, step] == 1)(functools.partial(back, step, True))
        pl.when(live[at, step] == 2)(functools.partial(back, step, False))
        return carry

    lax.fori_loop(0, count, step_of, 0)
    low = (d_query[...] * scale).astype(BF16)
    per = count // parts
    size = per * block
    for slot, out in enumerate(outs):

        @pl.when(at // per == slot)
        def _(out=out):
            out[0, pl.ds(pl.multiple_of((at % per) * block, block), block), :] = low

    @pl.when(at == count - 1)
    def _():
        for slot, out in enumerate(outs):
            rows = slice(slot * size, (slot + 1) * size)
            out[1] = (d_keys[rows, :] * scale).astype(BF16)
            out[2] = d_values[rows, :].astype(BF16)


def attend_back(row, queries, keys, values, grads, seg_row, seg_col, live, mixed, totals):
    parts = len(queries)
    length = seg_row.shape[2]
    size = length // parts
    block = length // live.shape[1]
    part_spec = pl.BlockSpec((size, HEAD), lambda i, s: (row, 0))
    own_spec = pl.BlockSpec((size, HEAD), lambda i, s: (0, 0))
    whole = lambda i, s: (0, 0)
    return pl.pallas_call(
        functools.partial(attend_back_kernel, parts, block),
        grid_spec=pltpu.PrefetchScalarGridSpec(
            num_scalar_prefetch=1,
            grid=(length // block,),
            in_specs=[part_spec] * (3 * parts)
            + [own_spec] * parts
            + [
                pl.BlockSpec((None, 1, length), lambda i, s: (row, 0, 0)),
                pl.BlockSpec((None, length, HEAD), lambda i, s: (row, 0, 0)),
                pl.BlockSpec((HEAD, length), whole),
                pl.BlockSpec((1, length), whole),
            ],
            out_specs=[pl.BlockSpec((3, size, HEAD), lambda i, s: (0, 0, 0))] * parts,
            scratch_shapes=[pltpu.VMEM((length, HEAD), BF16)] * 4
            + [pltpu.VMEM((length, HEAD), F32)] * 2
            + [pltpu.VMEM((block, HEAD), F32)],
        ),
        out_shape=[jax.ShapeDtypeStruct((3, size, HEAD), BF16)] * parts,
        compiler_params=pltpu.CompilerParams(vmem_limit_bytes=VMEM_LIMIT),
        cost_estimate=pl.CostEstimate(
            flops=2 * 5 * length * length * HEAD * 5 // 8,
            bytes_accessed=16 * length * HEAD,
            transcendentals=length * length // 2,
        ),
        name="attend_back",
    )(live[row], *queries, *keys, *values, *grads, seg_row, seg_col, mixed, totals)


def normalize(hidden):
    center = hidden - jnp.mean(hidden, axis=-1, keepdims=True)
    inverse = lax.rsqrt(jnp.mean(center * center, axis=-1, keepdims=True) + EPSILON)
    return center * inverse, inverse


def normalize_back(grad, normal, inverse):
    return inverse * (
        grad
        - jnp.mean(grad, axis=-1, keepdims=True)
        - normal * jnp.mean(grad * normal, axis=-1, keepdims=True)
    )


def gelu_pair(pre):
    inner = 0.7978845608028654 * (pre + 0.044715 * pre * pre * pre)
    wave = jnp.tanh(inner)
    value = 0.5 * pre * (1.0 + wave)
    slope = 0.5 * (1.0 + wave) + 0.5 * pre * (1.0 - wave * wave) * 0.7978845608028654 * (
        1.0 + 3.0 * 0.044715 * pre * pre
    )
    return value, slope


def head_sum(part):
    half = part.shape[0] // 2
    near = core_swap(part[half:].astype(BF16))
    mine = (part[:half] + near.astype(F32)).astype(BF16)
    far = chip_swap(mine)
    return mine.astype(F32) + far.astype(F32)


def both_halves(value):
    return jnp.concatenate([value, core_swap(value)], axis=0)


def local(
    layer_input,
    segment_ids,
    qkv_weight,
    qv_bias,
    out_weight,
    out_bias,
    norm1_gain,
    norm1_bias,
    up_weight,
    up_bias,
    down_weight,
    down_bias,
    norm2_gain,
    norm2_bias,
    out_grad,
):
    rows, local_len, width = layer_input.shape
    fsdp, ctx = lax.axis_size("fsdp"), lax.axis_size("ctx")
    y, place = lax.axis_index("fsdp"), lax.axis_index("ctx")
    core = lax.axis_index("tp") % 2
    columns = qkv_weight.shape[2]
    heads = columns // HEAD
    half = local_len // 2
    share = width // fsdp
    assert heads == ctx == 4 and lax.axis_size("tp") == 4

    def features(value):
        return rotate(value, value.ndim - 1, y, fsdp)

    def features_back(value):
        return rotate(value, value.ndim - 1, (fsdp - y) % fsdp, fsdp)

    def spread(block):
        return [block] + [shift(block, "fsdp", -by) for by in range(1, fsdp)]

    own = [rotate(qkv_weight[:, j], 1, place, heads) for j in range(3)]
    query_blocks = spread(own[0])
    key_blocks = spread(after(own[1], *query_blocks[1:]))
    value_blocks = spread(after(own[2], *key_blocks[1:]))
    out_blocks = spread(after(rotate(out_weight, 0, place, heads), *value_blocks[1:]))
    up_blocks = spread(after(up_weight, *out_blocks[1:]))
    down_blocks = spread(after(down_weight, *up_blocks[1:]))

    x_all_rows = features(rotate(layer_input, 1, core, 2))
    x = x_all_rows.reshape(rows * local_len, width)
    biases = rotate(qv_bias, 1, place, heads)
    vectors = features(
        jnp.stack([out_bias, norm1_gain, norm1_bias, down_bias, norm2_gain, norm2_bias])
    ).astype(F32)
    out_shift, gain_one, shift_one, down_shift, gain_two, shift_two = (
        vectors[i : i + 1] for i in range(6)
    )
    upper = up_bias.astype(F32)[None]

    seg_own = rotate(segment_ids, 1, core, 2)
    seg = jnp.concatenate([seg_own] + [shift(seg_own, "ctx", by) for by in range(1, ctx)], axis=1)
    length = ctx * local_len
    seg_row = seg[:, None, :]
    seg_col = jnp.broadcast_to(seg[:, :, None], (rows, length, HEAD))
    blocks = seg.reshape(rows, length // half, half)
    low_id, high_id = blocks[:, :, 0], blocks[:, :, half - 1]
    meets = (low_id[:, :, None] <= high_id[:, None, :]) & (low_id[:, None, :] <= high_id[:, :, None])
    one = low_id == high_id
    same = one[:, :, None] & one[:, None, :] & meets
    live = meets.astype(jnp.int32) + same.astype(jnp.int32)

    zero_bias = jnp.zeros_like(biases[:1])

    def exchange(pieces):
        return [pieces[0]] + [shift(pieces[by], "ctx", by) for by in range(1, ctx)]

    def exchange_back(pieces):
        return [pieces[0]] + [shift(pieces[by], "ctx", -by) for by in range(1, ctx)]

    queries = exchange(project(x, query_blocks, biases[:1]))
    keys = exchange(project(x, key_blocks, zero_bias))
    values = exchange(project(x, value_blocks, biases[1:]))

    x_half = x_all_rows[:, :half].reshape(rows * half, width)
    x_ring = [after(x_half, *values[1:])]
    for _ in range(1, ctx):
        x_ring.append(shift(x_ring[-1], "ctx", 1))
    x_other = [core_swap(piece) for piece in x_ring[1:]]

    out_cat = jnp.concatenate(out_blocks, axis=1)
    up_cat = jnp.concatenate(up_blocks, axis=0)
    down_cat = jnp.concatenate(down_blocks, axis=1)

    attended, kept = [], []
    for r in range(rows):
        *pieces, mixed, totals = attend(r, queries, keys, values, seg_row, seg_col, live)
        kept.append((mixed, totals))
        attended.append(jnp.concatenate(exchange_back(pieces), axis=1))

    norm_one, normal_one, inverse_one, norm_low = [], [], [], []
    for r in range(rows):
        total = head_sum(dot(attended[r], out_cat, 1, 0))
        hidden = x_all_rows[r, :half].astype(F32) + total + out_shift
        normal, inverse = normalize(hidden)
        result = normal * gain_one + shift_one
        norm_one.append(result)
        normal_one.append(normal)
        inverse_one.append(inverse)
        norm_low.append(both_halves(result.astype(BF16)))

    act_low, slopes = [], []
    for r in range(rows):
        value, slope = gelu_pair(dot(norm_low[r], up_cat, 1, 0) + upper)
        act_low.append(value.astype(BF16))
        slopes.append(slope)

    grad_half = features(
        lax.dynamic_slice_in_dim(out_grad, core * half, half, axis=1)
    )
    layer_low, d_second, d_mlp_low, sums = [], [], [], []
    for r in range(rows):
        total = head_sum(dot(act_low[r], down_cat, 1, 0))
        normal, inverse = normalize(norm_one[r] + total + down_shift)
        layer_low.append(both_halves((normal * gain_two + shift_two).astype(BF16)))
        grad = grad_half[r].astype(F32)
        d_hidden = normalize_back(grad * gain_two, normal, inverse)
        low = d_hidden.astype(BF16)
        d_second.append(d_hidden)
        d_mlp_low.append(both_halves(low))
        sums.append(
            (jnp.sum(low.astype(F32), axis=0), jnp.sum(grad * normal, axis=0), jnp.sum(grad, axis=0))
        )

    d_pre_low = []
    for r in range(rows):
        d_act = dot(d_mlp_low[r], down_cat, 1, 1)
        d_pre_low.append((d_act * slopes[r]).astype(BF16))

    def reduced(lefts, rights, left_range, right_range, split_left, row_pieces, gate):
        def ranges(by, piece):
            if split_left:
                size = left_range // fsdp // row_pieces
                return ((by * row_pieces + piece) * size, size), (0, right_range)
            size = left_range // row_pieces
            return (piece * size, size), (by * (right_range // fsdp), right_range // fsdp)

        results = []
        for piece in range(row_pieces):
            arrived = None
            for by in range(1, fsdp):
                sent = weight_grad(lefts, rights, *ranges(by, piece))
                got = shift(after(sent, *gate), "fsdp", by)
                gate = [got]
                arrived = got if arrived is None else (arrived.astype(F32) + got.astype(F32))
            results.append(weight_grad(lefts, rights, *ranges(0, piece), add=arrived))
        return results, gate

    hidden_units = up_weight.shape[1]
    down_pieces, gate = reduced(act_low, d_mlp_low, hidden_units, width, False, 2, [])
    up_pieces, gate = reduced(norm_low, d_pre_low, width, hidden_units, True, 2, gate)

    d_first, d_attn_low = [], []
    for r in range(rows):
        d_norm = d_second[r] + head_sum(dot(d_pre_low[r], up_cat, 1, 1))
        d_hidden = normalize_back(d_norm * gain_one, normal_one[r], inverse_one[r])
        low = d_hidden.astype(BF16)
        d_first.append(d_hidden)
        d_attn_low.append(both_halves(low))
        sums[r] = sums[r] + (
            jnp.sum(low.astype(F32), axis=0),
            jnp.sum(d_norm * normal_one[r], axis=0),
            jnp.sum(d_norm, axis=0),
        )

    out_pieces, gate = reduced(attended, d_attn_low, columns, width, False, 1, gate)

    d_heads, d_joint = [], []
    for r in range(rows):
        d_att = dot(d_attn_low[r], out_cat, 1, 1).astype(BF16)
        grads = exchange([d_att[:, s * HEAD : (s + 1) * HEAD] for s in range(heads)])
        mixed, totals = kept[r]
        pieces = attend_back(
            r, queries, keys, values, grads, seg_row, seg_col, live, mixed, totals
        )
        d_heads.append(pieces)
        d_joint.append(exchange_back(pieces))

    flat_heads = [
        jnp.concatenate([d_heads[r][s][j] for j in range(3)], axis=1)
        for s in range(ctx)
        for r in range(rows)
    ]
    lefts = []
    for s in range(ctx):
        for r in range(rows):
            near = x_ring[s][r * half : (r + 1) * half]
            far = x_half_other(x_all_rows, x_other, s, r, half)
            lefts.append(jnp.concatenate([near, far], axis=0))
    joint_pieces, gate = reduced(lefts, flat_heads, width, 3 * HEAD, True, 1, gate)
    ring = [joint_pieces[0]]
    for _ in range(1, ctx):
        ring.append(shift(ring[-1], "ctx", 1))
    in_order = rotate(jnp.stack(ring[::-1]), 0, (ctx - 1 - place) % ctx, ctx)
    joint_grad = (
        in_order.reshape(ctx, share, 3, HEAD).transpose(1, 2, 0, 3).reshape(share, 3, columns)
    ).astype(F32)

    joint_cat = [
        jnp.concatenate([query_blocks[b], key_blocks[b], value_blocks[b]], axis=1)
        for b in range(fsdp)
    ]
    joint_cat = jnp.concatenate(joint_cat, axis=0)
    input_low = []
    bias_sums = 0.0
    for r in range(rows):
        d_row = jnp.concatenate(
            [d_joint[r][s][j] for j in range(3) for s in range(heads)], axis=1
        )
        bias_sums = bias_sums + jnp.sum(d_row.astype(F32), axis=0)
        total = head_sum(dot(d_row, joint_cat, 1, 1))
        input_low.append(both_halves((d_first[r] + total).astype(BF16)))

    layer_output = features_back(rotate(jnp.stack(layer_low), 1, core, 2))
    input_grad = features_back(rotate(jnp.stack(input_low), 1, core, 2)).astype(F32)

    wide = jnp.stack([sum(sums[r][i] for r in range(rows)) for i in range(6)])
    wide = features_back(wide)
    wide = wide + core_swap(wide)
    bias_rows = jnp.concatenate([bias_sums[None, :columns], bias_sums[None, 2 * columns :]], axis=0)
    bias_rows = rotate(bias_rows, 1, (heads - place) % heads, heads)
    up_sum = sum(jnp.sum(d_pre_low[r].astype(F32), axis=0) for r in range(rows))
    small = jnp.concatenate([wide.reshape(-1), up_sum, bias_rows.reshape(-1)])
    if fsdp == 2:
        small = small + shift(small, "fsdp", 1)
    else:
        small = lax.psum(small, "fsdp")
    small = small + lax.ppermute(small, "ctx", [(0, 1), (1, 0), (2, 3), (3, 2)])
    small = small + lax.ppermute(small, "ctx", [(0, 2), (2, 0), (1, 3), (3, 1)])
    wide = small[: 6 * width].reshape(6, width)
    up_bias_grad = small[6 * width : 6 * width + hidden_units]
    qv_bias_grad = small[6 * width + hidden_units :].reshape(2, columns)

    out_sum = rotate(out_pieces[0], 0, (heads - place) % heads, heads)
    down_sums = [line_sum(p) for p in down_pieces]
    up_sums = [line_sum(p) for p in up_pieces]
    out_total = line_sum(out_sum)
    return (
        layer_output,
        input_grad,
        joint_grad,
        qv_bias_grad,
        out_total.astype(F32),
        wide[3],
        wide[4],
        wide[5],
        jnp.concatenate(up_sums, axis=0).astype(F32),
        up_bias_grad,
        jnp.concatenate(down_sums, axis=0).astype(F32),
        wide[0],
        wide[1],
        wide[2],
    )


def x_half_other(x_all_rows, x_other, s, r, half):
    if s == 0:
        return x_all_rows[r, half:]
    return x_other[s - 1][r * half : (r + 1) * half]


def solution(mesh):
    return jax.shard_map(
        local,
        mesh=mesh,
        in_specs=(
            P("fsdp", "ctx", None),
            P("fsdp", "ctx"),
            P("fsdp", None, "tp"),
            P(None, "tp"),
            P("tp", "fsdp"),
            P(),
            P(),
            P(),
            P("fsdp", "tp"),
            P("tp"),
            P("tp", "fsdp"),
            P(),
            P(),
            P(),
            P("fsdp", "ctx", None),
        ),
        out_specs=(
            P("fsdp", "ctx", None),
            P("fsdp", "ctx", None),
            P("fsdp", None, "tp"),
            P(None, "tp"),
            P("tp", "fsdp"),
            P(),
            P(),
            P(),
            P("fsdp", "tp"),
            P("tp"),
            P("tp", "fsdp"),
            P(),
            P(),
            P(),
        ),
        check_vma=False,
    )
```

time: 3270 us -> 1220 us (0.37)
  waiting for transfers between devices: 2500 us -> 462 us
  matrix products: 315 us -> 82.3 us
  Pallas kernels: 0 us -> 205 us
  starting transfers between devices: 0.8 us -> 202 us
  local copies, waits for them, and re-layouts: 148 us -> 79 us
  blocking collectives: 49.7 us -> 0 us
  other arithmetic: 229 us -> 181 us
    reduce_scatter x6 -> x0, waiting for transfers between devices: 1070 us -> none  [the longest x1 285 us: local(): lax.psum_scatter(down_weight_grad, ('fsdp', 'ctx'), scatter_dimension=1,...]
    all_gather x10 -> x0, waiting for transfers between devices: 847 us -> none  [the longest x1 150 us: local(): lax.all_gather(shares[3], 'ctx', axis=1, tiled=True)]
    psum x4 -> x0, waiting for transfers between devices: 573 us -> none  [the longest x1 153 us: local(): lax.psum(contract_cols(d_pre_low, upward_weight), 'tp')]
    ppermute x0 -> x96, waiting for transfers between devices: none -> 462 us  [the longest x49 308 us: shift(): lax.ppermute(value, axis, [(i, (i + by) % size) for i in range(size)])]
    dot_general x68 -> x14, matrix products: 315 us -> 82.3 us  [dot(): lax.dot_general(left, right, (((left_dim,), (right_dim,)), ((), ())), pre...]
    pallas_call x0 -> x19, Pallas kernels: none -> 205 us  [the longest x12 76.2 us: weight_grad(): pl.pallas_call(functools.partial(grad_kernel, len(lefts), add is not None...]
    ppermute x0 -> x96, starting transfers between devices: none -> 202 us  [the longest x49 149 us: shift(): lax.ppermute(value, axis, [(i, (i + by) % size) for i in range(size)])]
    sub x2 -> x0, other arithmetic: 63 us -> none  [attend_back_row(): d_scores = (probs * (d_probs - weighted)).astype(jnp.bfloat16)]
  transfers between devices with their start and end apart: 20 -> 96, of which waited for: 19 -> 33; matrix products, arithmetic and copies ran while one was open for 9% -> 27% of each run, Pallas kernels for 0% -> 17%
where the time goes in v1:
time: 1220 us; the launch traced here: 1210 us
  waiting for transfers between devices  462 us (38%)
  Pallas kernels  205 us (17%)
  starting transfers between devices  202 us (17%)
  other arithmetic  181 us (15%)
  matrix products  82.3 us (7%)
  local copies, waits for them, and re-layouts  79 us (6%)
    ppermute x49, waiting for transfers between devices, shift(): lax.ppermute(value, axis, [(i, (i + by) % size) for i in range(size)])  308 us
    ppermute x49, starting transfers between devices, shift(): lax.ppermute(value, axis, [(i, (i + by) % size) for i in range(size)])  149 us
    ppermute x8, waiting for transfers between devices, chip_swap(): return lax.ppermute(value, 'tp', [(i, i ^ 2) for i in range(size)])  91.4 us
    dot_general x14, matrix products, dot(): lax.dot_general(left, right, (((left_dim,), (right_dim,)), ((), ())), pre...  82.3 us
    pallas_call x12, Pallas kernels, weight_grad(): pl.pallas_call(functools.partial(grad_kernel, len(lefts), add is not None...  76.2 us
    pallas_call x2, Pallas kernels, attend_back(): pl.pallas_call(functools.partial(attend_back_kernel, parts, block), grid_...  60.9 us
    pallas_call x2, Pallas kernels, attend(): pl.pallas_call(functools.partial(attend_kernel, parts, block), grid_spec=...  50.8 us
    ppermute x5, waiting for transfers between devices, line_sum(): third = lax.ppermute(total, 'ctx', [(1, 0), (2, 3)])  42.3 us
  transfers between devices with their start and end apart: 96, of which 33 were waited for; matrix products, arithmetic and copies ran while one was open for 27% of the time, Pallas kernels for 17%

profile of v1, /device:TPU:0, one launch (start us, length us, event | category | flops | bytes accessed | tf_op | source)
XLA Modules:
  0.0 1213.4 jit_solution(4254319101856976921)
XLA Ops:
  44.2 14.6 %collective-permute-done.7.refs_1_ = bf16[1024,512]{1,0:T(8,128)(2,1)} collective-permute-done((bf16[1024,512]{1,0:T(8,128)(2,1)}, bf16[1024,512]{1,0:T(8,128)(2,1)}, u32[]{:S(2)}, u32[]{:S(2)}) %collective-permute-start.7) | collective-permute-done | bytes 1048608 | tf_op jit(solution)/shard_map/ppermute | solution.py:39
  91.7 10.3 collective-permute-start.12
  107.7 9.1 collective-permute-done.9.refs_6_
  117.5 11.9 collective-permute-done.13.refs_10_
  133.1 27.7 %attend.2 = (bf16[512,128]{1,0:T(8,128)(2,1)}, bf16[512,128]{1,0:T(8,128)(2,1)}, bf16[512,128]{1,0:T(8,128)(2,1)}, bf16[512,128]{1,0:T(8,128)(2,1)}, f32[128,2048]{1,0:T(8,128)}, /*index=5*/f32[1,2048]{1,0:T(1,128)}) custom-call(s32[8,8]{1,0:T(8,128)} %get-tuple-element.235.live, bf16[1024,128]{1,0:T(8,128)(2,1)} %get-tuple-element.57.refs_0_, ...), custom_call_target="tpu_custom_call" | custom-call | flops 1342177280 | bytes 2097152 | tf_op jit(solution)/shard_map/attend/pallas_call | solution.py:218
  168.6 23.1 %attend.3 = (bf16[512,128]{1,0:T(8,128)(2,1)}, bf16[512,128]{1,0:T(8,128)(2,1)}, bf16[512,128]{1,0:T(8,128)(2,1)}, bf16[512,128]{1,0:T(8,128)(2,1)}, f32[128,2048]{1,0:T(8,128)}, /*index=5*/f32[1,2048]{1,0:T(1,128)}) custom-call(s32[8,8]{1,0:T(8,128)} %get-tuple-element.236.live, bf16[1024,128]{1,0:T(8,128)(2,1)} %get-tuple-element.57.refs_0_, ...), custom_call_target="tpu_custom_call" | custom-call | flops 1342177280 | bytes 2097152 | tf_op jit(solution)/shard_map/attend/pallas_call | solution.py:218
  216.2 26.9 %maximum_maximum_fusion = bf16[2048,1536]{1,0:T(8,128)(2,1)} fusion(bf16[1024,512]{1,0:T(8,128)(2,1)S(1)} %copy-done.42, bf16[1024,512]{1,0:T(8,128)(2,1)} %collective-permute-done.7.refs_1_, bf16[1024,512]{1,0:T(8,128)(2,1)} %collective-permute-done.3.refs_1_, bf16[1024,512]{1,0:T(8,128)(2,1)S(1)} %copy-done.25, bf16[1024,512]{1,0:T(8,128)(2,1)} %fusion.57.refs_0_, ...), kind=kLoop, calls=%fused_computation | loop fusion | flops 37748736 | bytes 12582912 | tf_op jit(solution)/shard_map/concatenate | solution.py:595
  250.4 9.6 collective-permute-done.62
  276.9 63.8 %collective-permute-done.22 = bf16[1024,2048]{1,0:T(8,128)(2,1)S(1)} collective-permute-done((bf16[1024,2048]{1,0:T(8,128)(2,1)S(1)}, bf16[1024,2048]{1,0:T(8,128)(2,1)S(1)}, u32[]{:S(2)}, u32[]{:S(2)}) %collective-permute-start.22) | collective-permute-done | bytes 4194336 | tf_op jit(solution)/shard_map/ppermute | solution.py:39
  358.7 12.0 multiply_convert_fusion.1
  370.7 61.6 %collective-permute-done.23 = bf16[2048,1024]{1,0:T(8,128)(2,1)S(1)} collective-permute-done((bf16[2048,1024]{1,0:T(8,128)(2,1)S(1)}, bf16[2048,1024]{1,0:T(8,128)(2,1)S(1)}, u32[]{:S(2)}, u32[]{:S(2)}) %collective-permute-start.23) | collective-permute-done | bytes 4194336 | tf_op jit(solution)/shard_map/ppermute | solution.py:39
  455.8 20.0 %collective-permute-done.25 = bf16[256,2048]{1,0:T(8,128)(2,1)S(1)} collective-permute-done((bf16[256,2048]{1,0:T(8,128)(2,1)S(1)}, bf16[256,2048]{1,0:T(8,128)(2,1)S(1)}, u32[]{:S(2)}, u32[]{:S(2)}) %collective-permute-start.25) | collective-permute-done | bytes 1048608 | tf_op jit(solution)/shard_map/ppermute | solution.py:34
  475.7 22.1 %collective-permute-done.34 = bf16[256,2048]{1,0:T(8,128)(2,1)S(1)} collective-permute-done((bf16[256,2048]{1,0:T(8,128)(2,1)S(1)}, bf16[256,2048]{1,0:T(8,128)(2,1)S(1)}, u32[]{:S(2)}, u32[]{:S(2)}) %collective-permute-start.34) | collective-permute-done | bytes 1048608 | tf_op jit(solution)/shard_map/ppermute | solution.py:34
  511.2 11.7 convert_reduce_fusion.1
  544.3 11.6 convert_reduce_fusion
  555.9 8.0 fusion.119
  597.8 17.0 %collective-permute-done.51 = bf16[256,2048]{1,0:T(8,128)(2,1)S(1)} collective-permute-done((bf16[256,2048]{1,0:T(8,128)(2,1)S(1)}, bf16[256,2048]{1,0:T(8,128)(2,1)S(1)}, u32[]{:S(2)}, u32[]{:S(2)}) %collective-permute-start.51) | collective-permute-done | bytes 1048608 | tf_op jit(solution)/shard_map/ppermute | solution.py:34
  659.7 20.7 %collective-permute-done.40.refs_13_ = bf16[512,128]{1,0:T(8,128)(2,1)S(1)} collective-permute-done((bf16[512,128]{1,0:T(8,128)(2,1)S(1)}, bf16[512,128]{1,0:T(8,128)(2,1)S(1)}, u32[]{:S(2)}, u32[]{:S(2)}) %collective-permute-start.40) | collective-permute-done | bytes 131104 | tf_op jit(solution)/shard_map/ppermute | solution.py:39
  689.6 33.5 %attend_back.2 = (bf16[3,512,128]{2,1,0:T(8,128)(2,1)}, bf16[3,512,128]{2,1,0:T(8,128)(2,1)}, bf16[3,512,128]{2,1,0:T(8,128)(2,1)}, bf16[3,512,128]{2,1,0:T(8,128)(2,1)}) custom-call(s32[8,8]{1,0:T(8,128)} %get-tuple-element.235.live, bf16[1024,128]{1,0:T(8,128)(2,1)} %get-tuple-element.57.refs_0_, bf16[1024,128]{1,0:T(8,128)(2,1)} %copy-done.44, ...), custom_call_target="tpu_custom_call" | custom-call | flops 3355443200 | bytes 4194304 | tf_op jit(solution)/shard_map/attend_back/pallas_call | solution.py:323
  725.9 27.4 %attend_back.3 = (bf16[3,512,128]{2,1,0:T(8,128)(2,1)}, bf16[3,512,128]{2,1,0:T(8,128)(2,1)}, bf16[3,512,128]{2,1,0:T(8,128)(2,1)}, bf16[3,512,128]{2,1,0:T(8,128)(2,1)}) custom-call(s32[8,8]{1,0:T(8,128)} %get-tuple-element.236.live, bf16[1024,128]{1,0:T(8,128)(2,1)} %get-tuple-element.57.refs_0_, bf16[1024,128]{1,0:T(8,128)(2,1)} %copy-done.44, ...), custom_call_target="tpu_custom_call" | custom-call | flops 3355443200 | bytes 4194304 | tf_op jit(solution)/shard_map/attend_back/pallas_call | solution.py:323
  770.2 33.2 %collective-permute-done.57 = bf16[3,512,128]{2,1,0:T(8,128)(2,1)S(1)} collective-permute-done((bf16[3,512,128]{2,1,0:T(8,128)(2,1)}, bf16[3,512,128]{2,1,0:T(8,128)(2,1)S(1)}, u32[]{:S(2)}, u32[]{:S(2)}) %collective-permute-start.57) | collective-permute-done | bytes 393248 | tf_op jit(solution)/shard_map/ppermute | solution.py:39
  803.9 17.4 %collective-permute-done.44 = bf16[3,512,128]{2,1,0:T(8,128)(2,1)S(1)} collective-permute-done((bf16[3,512,128]{2,1,0:T(8,128)(2,1)S(1)}, bf16[3,512,128]{2,1,0:T(8,128)(2,1)S(1)}, u32[]{:S(2)}, u32[]{:S(2)}) %collective-permute-start.44) | collective-permute-done | bytes 393248 | tf_op jit(solution)/shard_map/ppermute | solution.py:39
  864.3 9.7 weight_grad.12
  875.3 11.8 collective-permute-done.60
  890.0 17.7 %collective-permute-done.47 = bf16[256,2048]{1,0:T(8,128)(2,1)} collective-permute-done((bf16[256,2048]{1,0:T(8,128)(2,1)S(1)}, bf16[256,2048]{1,0:T(8,128)(2,1)}, u32[]{:S(2)}, u32[]{:S(2)}) %collective-permute-start.47) | collective-permute-done | bytes 1048608 | tf_op jit(solution)/shard_map/ppermute | solution.py:34
  937.0 20.9 %collective-permute-done.71.refs_4_ = bf16[512,2048]{1,0:T(8,128)(2,1)} collective-permute-done((bf16[512,2048]{1,0:T(8,128)(2,1)}, bf16[512,2048]{1,0:T(8,128)(2,1)}, u32[]{:S(2)}, u32[]{:S(2)}) %collective-permute-start.71) | collective-permute-done | bytes 2097184 | tf_op jit(solution)/shard_map/ppermute | solution.py:39
  998.5 15.5 %collective-permute-done.87 = bf16[512,2048]{1,0:T(8,128)(2,1)} collective-permute-done((bf16[512,2048]{1,0:T(8,128)(2,1)}, bf16[512,2048]{1,0:T(8,128)(2,1)}, u32[]{:S(2)}, u32[]{:S(2)}) %collective-permute-start.87) | collective-permute-done | bytes 2097184 | tf_op jit(solution)/shard_map/ppermute | solution.py:47
  1018.5 10.0 weight_grad.18
  1045.3 8.6 collective-permute-done.74
  1053.9 30.8 %collective-permute-start.75 = (bf16[1024,384]{1,0:T(8,128)(2,1)S(1)}, bf16[1024,384]{1,0:T(8,128)(2,1)S(1)}, u32[]{:S(2)}, u32[]{:S(2)}) collective-permute-start(bf16[1024,384]{1,0:T(8,128)(2,1)S(1)} %collective-permute-done.74), channel_id=1, source_target_pairs={{0,4},{4,8},{8,12},{12,0},{1,5},{5,9},{9,13},{13,1},{2,6},{6,10},{... | collective-permute-start | bytes 2359304 | tf_op jit(solution)/shard_map/ppermute | solution.py:39
  1098.4 23.8 %collective-permute-start.76 = (bf16[1024,384]{1,0:T(8,128)(2,1)S(1)}, bf16[1024,384]{1,0:T(8,128)(2,1)S(1)}, u32[]{:S(2)}, u32[]{:S(2)}) collective-permute-start(bf16[1024,384]{1,0:T(8,128)(2,1)S(1)} %collective-permute-done.75), channel_id=1, source_target_pairs={{0,4},{4,8},{8,12},{12,0},{1,5},{5,9},{9,13},{13,1},{2,6},{6,10},{... | collective-permute-start | bytes 2359304 | tf_op jit(solution)/shard_map/ppermute | solution.py:39
  1171.4 37.1 %collective-permute-done.89 = bf16[512,2048]{1,0:T(8,128)(2,1)S(1)} collective-permute-done((bf16[512,2048]{1,0:T(8,128)(2,1)}, bf16[512,2048]{1,0:T(8,128)(2,1)S(1)}, u32[]{:S(2)}, u32[]{:S(2)}) %collective-permute-start.89) | collective-permute-done | bytes 2097184 | tf_op jit(solution)/shard_map/ppermute | solution.py:51
  (585 shorter events, 531.3 us)
Async XLA Ops:
  116.8 83.7 %collective-permute-start.18 = (bf16[512,1024]{1,0:T(8,128)(2,1)S(1)}, bf16[512,1024]{1,0:T(8,128)(2,1)}, u32[]{:S(2)}, u32[]{:S(2)}) collective-permute-start(bf16[512,1024]{1,0:T(8,128)(2,1)S(1)} %copy-done.26), channel_id=1, source_target_pairs={{0,16},{16,0},{1,17},{17,1},{2,18},{18,2},{3,19},{19,3},{4,20},{20... | collective-permute-start | bytes 3145736 | tf_op jit(solution)/shard_map/ppermute | solution.py:39
  211.4 48.5 %collective-permute-start.62 = (bf16[512,2048]{1,0:T(8,128)(2,1)S(1)}, bf16[512,2048]{1,0:T(8,128)(2,1)}, u32[]{:S(2)}, u32[]{:S(2)}) collective-permute-start(bf16[512,2048]{1,0:T(8,128)(2,1)S(1)} %bitcast.290), channel_id=1, source_target_pairs={{0,4},{4,8},{8,12},{12,0},{1,5},{5,9},{9,13},{13,1},{2,6},{6,10},{... | collective-permute-start | bytes 6291464 | tf_op jit(solution)/shard_map/ppermute | solution.py:39
  213.7 46.2 %collective-permute-start.20 = (bf16[256,2048]{1,0:T(8,128)(2,1)S(1)}, bf16[256,2048]{1,0:T(8,128)(2,1)S(1)}, u32[]{:S(2)}, u32[]{:S(2)}) collective-permute-start(bf16[256,2048]{1,0:T(8,128)(2,1)S(1)} %fusion.49), channel_id=1, source_target_pairs={{0,2},{1,3},{2,0},{3,1},{4,6},{5,7},{6,4},{7,5},{8,10},{9,11},{10,... | collective-permute-start | bytes 3145736 | tf_op jit(solution)/shard_map/ppermute | solution.py:34
  215.6 45.9 %collective-permute-start.31 = (bf16[256,2048]{1,0:T(8,128)(2,1)S(1)}, bf16[256,2048]{1,0:T(8,128)(2,1)S(1)}, u32[]{:S(2)}, u32[]{:S(2)}) collective-permute-start(bf16[256,2048]{1,0:T(8,128)(2,1)S(1)} %fusion.47), channel_id=1, source_target_pairs={{0,2},{1,3},{2,0},{3,1},{4,6},{5,7},{6,4},{7,5},{8,10},{9,11},{10,... | collective-permute-start | bytes 3145736 | tf_op jit(solution)/shard_map/ppermute | solution.py:34
  245.3 95.5 %collective-permute-start.22 = (bf16[1024,2048]{1,0:T(8,128)(2,1)S(1)}, bf16[1024,2048]{1,0:T(8,128)(2,1)S(1)}, u32[]{:S(2)}, u32[]{:S(2)}) collective-permute-start(bf16[1024,2048]{1,0:T(8,128)(2,1)S(1)} %copy-done.27), channel_id=1, source_target_pairs={{0,16},{16,0},{1,17},{17,1},{2,18},{18,2},{3,19},{19,3},{4,20},{20... | collective-permute-start | bytes 12582920 | tf_op jit(solution)/shard_map/ppermute | solution.py:39
  268.6 76.4 %collective-permute-start.64 = (bf16[512,2048]{1,0:T(8,128)(2,1)}, bf16[512,2048]{1,0:T(8,128)(2,1)}, u32[]{:S(2)}, u32[]{:S(2)}) collective-permute-start(bf16[512,2048]{1,0:T(8,128)(2,1)} %collective-permute-done.62), channel_id=1, source_target_pairs={{0,4},{4,8},{8,12},{12,0},{1,5},{5,9},{9,13},{13,1},{2,6},{6,10},{... | collective-permute-start | bytes 6291464 | tf_op jit(solution)/shard_map/ppermute | solution.py:39
  340.7 91.5 %collective-permute-start.23 = (bf16[2048,1024]{1,0:T(8,128)(2,1)S(1)}, bf16[2048,1024]{1,0:T(8,128)(2,1)S(1)}, u32[]{:S(2)}, u32[]{:S(2)}) collective-permute-start(bf16[2048,1024]{1,0:T(8,128)(2,1)S(1)} %copy-done.28), channel_id=1, source_target_pairs={{0,16},{16,0},{1,17},{17,1},{2,18},{18,2},{3,19},{19,3},{4,20},{20... | collective-permute-start | bytes 12582920 | tf_op jit(solution)/shard_map/ppermute | solution.py:39
  344.9 109.0 %collective-permute-start.65 = (bf16[512,2048]{1,0:T(8,128)(2,1)}, bf16[512,2048]{1,0:T(8,128)(2,1)}, u32[]{:S(2)}, u32[]{:S(2)}) collective-permute-start(bf16[512,2048]{1,0:T(8,128)(2,1)} %collective-permute-done.64), channel_id=1, source_target_pairs={{0,1},{1,0},{2,3},{3,2},{4,5},{5,4},{6,7},{7,6},{8,9},{9,8},{10,11... | collective-permute-start | bytes 6291464 | tf_op jit(solution)/shard_map/ppermute | solution.py:29
  344.9 104.4 %collective-permute-start.66 = (bf16[512,2048]{1,0:T(8,128)(2,1)}, bf16[512,2048]{1,0:T(8,128)(2,1)}, u32[]{:S(2)}, u32[]{:S(2)}) collective-permute-start(bf16[512,2048]{1,0:T(8,128)(2,1)} %collective-permute-done.64), channel_id=1, source_target_pairs={{0,4},{4,8},{8,12},{12,0},{1,5},{5,9},{9,13},{13,1},{2,6},{6,10},{... | collective-permute-start | bytes 6291464 | tf_op jit(solution)/shard_map/ppermute | solution.py:39
  449.3 57.7 %collective-permute-start.67 = (bf16[512,2048]{1,0:T(8,128)(2,1)}, bf16[512,2048]{1,0:T(8,128)(2,1)S(1)}, u32[]{:S(2)}, u32[]{:S(2)}) collective-permute-start(bf16[512,2048]{1,0:T(8,128)(2,1)} %collective-permute-done.66), channel_id=1, source_target_pairs={{0,1},{1,0},{2,3},{3,2},{4,5},{5,4},{6,7},{7,6},{8,9},{9,8},{10,11... | collective-permute-start | bytes 6291464 | tf_op jit(solution)/shard_map/ppermute | solution.py:29
  451.6 46.2 %collective-permute-start.34 = (bf16[256,2048]{1,0:T(8,128)(2,1)S(1)}, bf16[256,2048]{1,0:T(8,128)(2,1)S(1)}, u32[]{:S(2)}, u32[]{:S(2)}) collective-permute-start(bf16[256,2048]{1,0:T(8,128)(2,1)S(1)} %fusion.46), channel_id=1, source_target_pairs={{0,2},{1,3},{2,0},{3,1},{4,6},{5,7},{6,4},{7,5},{8,10},{9,11},{10,... | collective-permute-start | bytes 3145736 | tf_op jit(solution)/shard_map/ppermute | solution.py:34
  542.8 47.9 %collective-permute-start.68 = (bf16[1024,1024]{1,0:T(8,128)(2,1)}, bf16[1024,1024]{1,0:T(8,128)(2,1)}, u32[]{:S(2)}, u32[]{:S(2)}) collective-permute-start(bf16[1024,1024]{1,0:T(8,128)(2,1)} %weight_grad.17), channel_id=1, source_target_pairs={{0,16},{16,0},{1,17},{17,1},{2,18},{18,2},{3,19},{19,3},{4,20},{20... | collective-permute-start | bytes 6291464 | tf_op jit(solution)/shard_map/ppermute | solution.py:39
  590.8 251.8 %collective-permute-start.69 = (bf16[1024,1024]{1,0:T(8,128)(2,1)}, bf16[1024,1024]{1,0:T(8,128)(2,1)}, u32[]{:S(2)}, u32[]{:S(2)}) collective-permute-start(bf16[1024,1024]{1,0:T(8,128)(2,1)} %weight_grad.16), channel_id=1, source_target_pairs={{0,16},{16,0},{1,17},{17,1},{2,18},{18,2},{3,19},{19,3},{4,20},{20... | collective-permute-start | bytes 6291464 | tf_op jit(solution)/shard_map/ppermute | solution.py:39
  627.7 221.3 %collective-permute-start.90 = (bf16[1024,1024]{1,0:T(8,128)(2,1)}, bf16[1024,1024]{1,0:T(8,128)(2,1)}, u32[]{:S(2)}, u32[]{:S(2)}) collective-permute-start(bf16[1024,1024]{1,0:T(8,128)(2,1)} %weight_grad.22), channel_id=1, source_target_pairs={{0,4},{12,8},{1,5},{13,9},{2,6},{14,10},{3,7},{15,11},{16,20},{28,... | collective-permute-start | bytes 6291464 | tf_op jit(solution)/shard_map/ppermute | solution.py:47
  680.5 44.6 %collective-permute-start.53 = (bf16[512,128]{1,0:T(8,128)(2,1)S(1)}, bf16[512,128]{1,0:T(8,128)(2,1)S(1)}, u32[]{:S(2)}, u32[]{:S(2)}) collective-permute-start(bf16[512,128]{1,0:T(8,128)(2,1)S(1)} %get-tuple-element.183), channel_id=1, source_target_pairs={{0,4},{4,8},{8,12},{12,0},{1,5},{5,9},{9,13},{13,1},{2,6},{6,10},{... | collective-permute-start | bytes 393224 | tf_op jit(solution)/shard_map/ppermute | solution.py:39
  757.1 46.4 %collective-permute-start.57 = (bf16[3,512,128]{2,1,0:T(8,128)(2,1)}, bf16[3,512,128]{2,1,0:T(8,128)(2,1)S(1)}, u32[]{:S(2)}, u32[]{:S(2)}) collective-permute-start(bf16[3,512,128]{2,1,0:T(8,128)(2,1)} %get-tuple-element.92), channel_id=1, source_target_pairs={{0,8},{4,12},{8,0},{12,4},{1,9},{5,13},{9,1},{13,5},{2,10},{6,14},... | collective-permute-start | bytes 1179656 | tf_op jit(solution)/shard_map/ppermute | solution.py:39
  757.2 46.3 %collective-permute-start.58 = (bf16[3,512,128]{2,1,0:T(8,128)(2,1)S(1)}, bf16[3,512,128]{2,1,0:T(8,128)(2,1)S(1)}, u32[]{:S(2)}, u32[]{:S(2)}) collective-permute-start(bf16[3,512,128]{2,1,0:T(8,128)(2,1)S(1)} %copy-done.63), channel_id=1, source_target_pairs={{0,4},{4,8},{8,12},{12,0},{1,5},{5,9},{9,13},{13,1},{2,6},{6,10},{... | collective-permute-start | bytes 1179656 | tf_op jit(solution)/shard_map/ppermute | solution.py:39
  842.6 67.0 %collective-permute-start.70 = (bf16[512,2048]{1,0:T(8,128)(2,1)}, bf16[512,2048]{1,0:T(8,128)(2,1)}, u32[]{:S(2)}, u32[]{:S(2)}) collective-permute-start(bf16[512,2048]{1,0:T(8,128)(2,1)} %weight_grad.15), channel_id=1, source_target_pairs={{0,16},{16,0},{1,17},{17,1},{2,18},{18,2},{3,19},{19,3},{4,20},{20... | collective-permute-start | bytes 6291464 | tf_op jit(solution)/shard_map/ppermute | solution.py:39
  849.0 68.9 %collective-permute-start.93 = (bf16[1024,1024]{1,0:T(8,128)(2,1)}, bf16[1024,1024]{1,0:T(8,128)(2,1)}, u32[]{:S(2)}, u32[]{:S(2)}) collective-permute-start(bf16[1024,1024]{1,0:T(8,128)(2,1)} %weight_grad.23), channel_id=1, source_target_pairs={{0,4},{12,8},{1,5},{13,9},{2,6},{14,10},{3,7},{15,11},{16,20},{28,... | collective-permute-start | bytes 6291464 | tf_op jit(solution)/shard_map/ppermute | solution.py:47
  857.3 67.1 %collective-permute-start.91 = (bf16[1024,1024]{1,0:T(8,128)(2,1)S(1)}, bf16[1024,1024]{1,0:T(8,128)(2,1)}, u32[]{:S(2)}, u32[]{:S(2)}) collective-permute-start(bf16[1024,1024]{1,0:T(8,128)(2,1)S(1)} %add_convert_fusion.3), channel_id=1, source_target_pairs={{4,8},{8,4},{5,9},{9,5},{6,10},{10,6},{7,11},{11,7},{20,24},{24,20... | collective-permute-start | bytes 6291464 | tf_op jit(solution)/shard_map/ppermute | solution.py:49
  909.5 48.4 %collective-permute-start.71 = (bf16[512,2048]{1,0:T(8,128)(2,1)}, bf16[512,2048]{1,0:T(8,128)(2,1)}, u32[]{:S(2)}, u32[]{:S(2)}) collective-permute-start(bf16[512,2048]{1,0:T(8,128)(2,1)} %weight_grad.14), channel_id=1, source_target_pairs={{0,16},{16,0},{1,17},{17,1},{2,18},{18,2},{3,19},{19,3},{4,20},{20... | collective-permute-start | bytes 6291464 | tf_op jit(solution)/shard_map/ppermute | solution.py:39
  917.9 55.4 %collective-permute-start.84 = (bf16[512,2048]{1,0:T(8,128)(2,1)}, bf16[512,2048]{1,0:T(8,128)(2,1)}, u32[]{:S(2)}, u32[]{:S(2)}) collective-permute-start(bf16[512,2048]{1,0:T(8,128)(2,1)} %weight_grad.20), channel_id=1, source_target_pairs={{0,4},{12,8},{1,5},{13,9},{2,6},{14,10},{3,7},{15,11},{16,20},{28,... | collective-permute-start | bytes 6291464 | tf_op jit(solution)/shard_map/ppermute | solution.py:47
  924.4 53.6 %collective-permute-start.94 = (bf16[1024,1024]{1,0:T(8,128)(2,1)}, bf16[1024,1024]{1,0:T(8,128)(2,1)}, u32[]{:S(2)}, u32[]{:S(2)}) collective-permute-start(bf16[1024,1024]{1,0:T(8,128)(2,1)} %add_convert_fusion.1), channel_id=1, source_target_pairs={{4,8},{8,4},{5,9},{9,5},{6,10},{10,6},{7,11},{11,7},{20,24},{24,20... | collective-permute-start | bytes 6291464 | tf_op jit(solution)/shard_map/ppermute | solution.py:49
  930.3 61.6 %collective-permute-start.92 = (bf16[1024,1024]{1,0:T(8,128)(2,1)}, bf16[1024,1024]{1,0:T(8,128)(2,1)S(1)}, u32[]{:S(2)}, u32[]{:S(2)}) collective-permute-start(bf16[1024,1024]{1,0:T(8,128)(2,1)} %add_convert_fusion.2), channel_id=1, source_target_pairs={{4,0},{8,12},{5,1},{9,13},{6,2},{10,14},{7,3},{11,15},{20,16},{24,... | collective-permute-start | bytes 6291464 | tf_op jit(solution)/shard_map/ppermute | solution.py:51
  966.2 47.8 %collective-permute-start.87 = (bf16[512,2048]{1,0:T(8,128)(2,1)}, bf16[512,2048]{1,0:T(8,128)(2,1)}, u32[]{:S(2)}, u32[]{:S(2)}) collective-permute-start(bf16[512,2048]{1,0:T(8,128)(2,1)} %weight_grad.21), channel_id=1, source_target_pairs={{0,4},{12,8},{1,5},{13,9},{2,6},{14,10},{3,7},{15,11},{16,20},{28,... | collective-permute-start | bytes 6291464 | tf_op jit(solution)/shard_map/ppermute | solution.py:47
  975.8 64.2 %collective-permute-start.85 = (bf16[512,2048]{1,0:T(8,128)(2,1)S(1)}, bf16[512,2048]{1,0:T(8,128)(2,1)}, u32[]{:S(2)}, u32[]{:S(2)}) collective-permute-start(bf16[512,2048]{1,0:T(8,128)(2,1)S(1)} %add_convert_fusion.7), channel_id=1, source_target_pairs={{4,8},{8,4},{5,9},{9,5},{6,10},{10,6},{7,11},{11,7},{20,24},{24,20... | collective-permute-start | bytes 6291464 | tf_op jit(solution)/shard_map/ppermute | solution.py:49
  981.2 103.5 %collective-permute-start.95 = (bf16[1024,1024]{1,0:T(8,128)(2,1)S(1)}, bf16[1024,1024]{1,0:T(8,128)(2,1)}, u32[]{:S(2)}, u32[]{:S(2)}) collective-permute-start(bf16[1024,1024]{1,0:T(8,128)(2,1)S(1)} %add_convert_fusion), channel_id=1, source_target_pairs={{4,0},{8,12},{5,1},{9,13},{6,2},{10,14},{7,3},{11,15},{20,16},{24,... | collective-permute-start | bytes 6291464 | tf_op jit(solution)/shard_map/ppermute | solution.py:51
  991.8 44.7 %collective-permute-start.81 = (bf16[512,1024]{1,0:T(8,128)(2,1)}, bf16[512,1024]{1,0:T(8,128)(2,1)}, u32[]{:S(2)}, u32[]{:S(2)}) collective-permute-start(bf16[512,1024]{1,0:T(8,128)(2,1)} %fusion.54), channel_id=1, source_target_pairs={{0,4},{12,8},{1,5},{13,9},{2,6},{14,10},{3,7},{15,11},{16,20},{28,... | collective-permute-start | bytes 3145736 | tf_op jit(solution)/shard_map/ppermute | solution.py:47
  1016.4 108.5 %collective-permute-start.88 = (bf16[512,2048]{1,0:T(8,128)(2,1)S(1)}, bf16[512,2048]{1,0:T(8,128)(2,1)}, u32[]{:S(2)}, u32[]{:S(2)}) collective-permute-start(bf16[512,2048]{1,0:T(8,128)(2,1)S(1)} %add_convert_fusion.5), channel_id=1, source_target_pairs={{4,8},{8,4},{5,9},{9,5},{6,10},{10,6},{7,11},{11,7},{20,24},{24,20... | collective-permute-start | bytes 6291464 | tf_op jit(solution)/shard_map/ppermute | solution.py:49
  1039.0 83.2 %collective-permute-start.82 = (bf16[512,1024]{1,0:T(8,128)(2,1)S(1)}, bf16[512,1024]{1,0:T(8,128)(2,1)S(1)}, u32[]{:S(2)}, u32[]{:S(2)}) collective-permute-start(bf16[512,1024]{1,0:T(8,128)(2,1)S(1)} %add_convert_fusion.9), channel_id=1, source_target_pairs={{4,8},{8,4},{5,9},{9,5},{6,10},{10,6},{7,11},{11,7},{20,24},{24,20... | collective-permute-start | bytes 3145736 | tf_op jit(solution)/shard_map/ppermute | solution.py:49
  1043.9 125.7 %collective-permute-start.86 = (bf16[512,2048]{1,0:T(8,128)(2,1)}, bf16[512,2048]{1,0:T(8,128)(2,1)}, u32[]{:S(2)}, u32[]{:S(2)}) collective-permute-start(bf16[512,2048]{1,0:T(8,128)(2,1)} %add_convert_fusion.6), channel_id=1, source_target_pairs={{4,0},{8,12},{5,1},{9,13},{6,2},{10,14},{7,3},{11,15},{20,16},{24,... | collective-permute-start | bytes 6291464 | tf_op jit(solution)/shard_map/ppermute | solution.py:51
  1128.7 79.7 %collective-permute-start.89 = (bf16[512,2048]{1,0:T(8,128)(2,1)}, bf16[512,2048]{1,0:T(8,128)(2,1)S(1)}, u32[]{:S(2)}, u32[]{:S(2)}) collective-permute-start(bf16[512,2048]{1,0:T(8,128)(2,1)} %add_convert_fusion.4), channel_id=1, source_target_pairs={{4,0},{8,12},{5,1},{9,13},{6,2},{10,14},{7,3},{11,15},{20,16},{24,... | collective-permute-start | bytes 6291464 | tf_op jit(solution)/shard_map/ppermute | solution.py:51
  (150 other events, 2621.5 us)

commit v2 on v1

v2 whole, which is shorter than its diff:
```python
import functools
import math

import jax
import jax.numpy as jnp
from jax import lax
from jax.experimental import pallas as pl
from jax.experimental.pallas import tpu as pltpu
from jax.sharding import PartitionSpec as P

HEAD = 128
EPSILON = 1e-12
NEGATIVE = -1e30
LOG2E = 1.4426950408889634
SCALE = 1.0 / math.sqrt(HEAD)
VMEM_LIMIT = 56 * 2**20

BF16 = jnp.bfloat16
F32 = jnp.float32


def dot(left, right, left_dim, right_dim):
    return lax.dot_general(
        left, right, (((left_dim,), (right_dim,)), ((), ())), preferred_element_type=F32
    )


def params():
    return pltpu.CompilerParams(vmem_limit_bytes=VMEM_LIMIT)


def cost(flops, moved, special=0):
    return pl.CostEstimate(flops=flops // 256, bytes_accessed=moved // 256, transcendentals=0)


def like(shape, dtype):
    return jax.ShapeDtypeStruct(shape, dtype)


def core_swap(value):
    size = lax.axis_size("tp")
    return lax.ppermute(value, "tp", [(i, i ^ 1) for i in range(size)])


def chip_swap(value):
    size = lax.axis_size("tp")
    return lax.ppermute(value, "tp", [(i, i ^ 2) for i in range(size)])


def shift(value, axis, by):
    size = lax.axis_size(axis)
    return lax.ppermute(value, axis, [(i, (i + by) % size) for i in range(size)])


def rotate(value, axis, by, count):
    size = value.shape[axis]
    block = size // count
    if count == 1:
        return value
    twice = jnp.concatenate([value, value], axis=axis)
    if count == 2:
        swapped = lax.slice_in_dim(twice, block, block + size, axis=axis)
        return jnp.where(by == 0, value, swapped)
    return lax.dynamic_slice_in_dim(twice, by * block, size, axis=axis)


def after(value, *others):
    return lax.optimization_barrier((value, *others))[0]


class Order:
    def __init__(self):
        self.last = ()

    def ready(self, value):
        return after(value, *self.last) if self.last else value

    def done(self, value):
        self.last = (value,)
        return value

    def pin(self, value):
        self.last += (value,)


class Weight:
    def __init__(self, parts, axis, blocks, rows=None):
        self.parts, self.axis, self.blocks = parts, axis, blocks
        self.turned = not isinstance(parts[0], tuple)
        self.shape = list((parts[0] if self.turned else parts[0][0]).shape[-2:])
        if self.turned:
            self.shape[axis] //= blocks
        if rows is not None:
            self.shape[0] = rows

    def arrays(self):
        if self.turned:
            return [self.parts[0]] * self.blocks
        return [array for array, _, _ in self.parts]

    def specs(self, split_axis, tile):
        shape = list(self.shape)
        steps = shape[split_axis] // tile
        shape[split_axis] = tile

        def spec(block):
            lead, row = (None, 0) if self.turned else self.parts[block][1:]

            def find(*args):
                at = [0, 0]
                if self.turned:
                    at[self.axis] = lax.rem(args[1][0] + block, self.blocks)
                else:
                    at[0] = row
                at[split_axis] = at[split_axis] * steps + args[0]
                return tuple(at) if lead is None else (lead, *at)

            return pl.BlockSpec(tuple(shape) if lead is None else (None, *shape), find)

        return [spec(b) for b in range(self.blocks)]


def grid_call(kernel, name, place, grid, in_specs, out_specs, out_shape, scratch, estimate, values):
    return pl.pallas_call(
        kernel,
        grid_spec=pltpu.PrefetchScalarGridSpec(
            num_scalar_prefetch=1,
            grid=grid,
            in_specs=in_specs,
            out_specs=out_specs,
            scratch_shapes=scratch,
        ),
        out_shape=out_shape,
        compiler_params=params(),
        cost_estimate=estimate,
        name=name,
    )(place, *values)


def fixed(shape):
    return pl.BlockSpec(shape, lambda i, p: (0,) * len(shape))


def project_kernel(blocks, x_ref, *refs):
    weights, bias_ref, out = refs[:blocks], *refs[blocks:]
    depth = x_ref.shape[1] // blocks
    acc = None
    for index, weight in enumerate(weights):
        part = dot(x_ref[:, index * depth : (index + 1) * depth], weight[...], 1, 0)
        acc = part if acc is None else acc + part
    low = (acc + bias_ref[...].astype(F32)).astype(BF16)
    for slot in range(out.shape[0]):
        out[slot] = low[:, slot * HEAD : (slot + 1) * HEAD]


def project(x, weight, bias):
    tokens, width = x.shape
    columns = weight.shape[1]
    heads = columns // HEAD
    tile = 256

    def whole(block):
        _, lead, row = weight.parts[block]
        return pl.BlockSpec((None, *weight.shape), lambda i: (lead, row, 0))

    return pl.pallas_call(
        functools.partial(project_kernel, weight.blocks),
        grid=(tokens // tile,),
        in_specs=[pl.BlockSpec((tile, width), lambda i: (i, 0))]
        + [whole(b) for b in range(weight.blocks)]
        + [pl.BlockSpec((1, columns), lambda i: (0, 0))],
        out_specs=pl.BlockSpec((heads, tile, HEAD), lambda i: (0, i, 0)),
        out_shape=like((heads, tokens, HEAD), BF16),
        compiler_params=params(),
        cost_estimate=cost(2 * tokens * width * columns, 2 * (tokens * width + width * columns)),
        name="project",
    )(x, *weight.arrays(), bias)


def up_kernel(blocks, place_ref, near, far, *refs):
    weights, bias_ref, act_ref, slope_ref = refs[:blocks], *refs[blocks:]
    half = near.shape[0]
    depth = near.shape[1] // blocks
    for index, source in enumerate((near, far)):
        pre = bias_ref[...].astype(F32)
        for block, weight in enumerate(weights):
            pre = pre + dot(source[:, block * depth : (block + 1) * depth], weight[...], 1, 0)
        square = pre * pre
        wave = jnp.tanh(pre * (0.7978845608028654 + 0.7978845608028654 * 0.044715 * square))
        half_up = 0.5 + 0.5 * wave
        slope = half_up + (0.5 * pre) * (1.0 - wave * wave) * (
            0.7978845608028654 + 3.0 * 0.7978845608028654 * 0.044715 * square
        )
        rows = slice(index * half, (index + 1) * half)
        act_ref[rows, :] = (pre * half_up).astype(BF16)
        slope_ref[rows, :] = slope.astype(slope_ref.dtype)


def up_project(place, near, far, weight, bias):
    half, width = near.shape
    columns = weight.shape[1]
    tile = 512
    out_spec = pl.BlockSpec((2 * half, tile), lambda i, p: (0, i))
    return grid_call(
        functools.partial(up_kernel, weight.blocks),
        "up_project",
        place,
        (columns // tile,),
        [fixed((half, width))] * 2
        + weight.specs(1, tile)
        + [pl.BlockSpec((1, tile), lambda i, p: (0, i))],
        [out_spec] * 2,
        [like((2 * half, columns), BF16)] * 2,
        [],
        cost(4 * half * width * columns, 2 * width * (2 * half + columns) + 8 * half * columns),
        [near, far, *weight.arrays(), bias],
    )


def act_back_kernel(blocks, place_ref, near, far, *refs):
    weights, slope_ref, out_ref, sum_ref = refs[:blocks], *refs[blocks:]
    half = near.shape[0]
    depth = near.shape[1] // blocks
    total = None
    for index, source in enumerate((near, far)):
        grad = None
        for block, weight in enumerate(weights):
            part = dot(source[:, block * depth : (block + 1) * depth], weight[...], 1, 1)
            grad = part if grad is None else grad + part
        rows = slice(index * half, (index + 1) * half)
        low = (grad * slope_ref[rows, :].astype(F32)).astype(BF16)
        out_ref[rows, :] = low
        part = jnp.sum(low.astype(F32), axis=0, keepdims=True)
        total = part if total is None else total + part
    sum_ref[...] = total


def act_back(place, near, far, weight, slope):
    half, width = near.shape
    columns = weight.shape[0]
    tile = 512
    out_spec = pl.BlockSpec((2 * half, tile), lambda i, p: (0, i))
    return grid_call(
        functools.partial(act_back_kernel, weight.blocks),
        "act_back",
        place,
        (columns // tile,),
        [fixed((half, width))] * 2 + weight.specs(0, tile) + [out_spec],
        [out_spec, pl.BlockSpec((1, tile), lambda i, p: (0, i))],
        [like((2 * half, columns), BF16), like((1, columns), F32)],
        [],
        cost(4 * half * width * columns, 2 * width * (2 * half + columns) + 8 * half * columns),
        [near, far, *weight.arrays(), slope],
    )


def head_back_kernel(blocks, place_ref, near, far, *refs):
    weights, out = refs[:blocks], refs[blocks]
    half = near.shape[0]
    depth = near.shape[1] // blocks
    for index, source in enumerate((near, far)):
        grad = None
        for block, weight in enumerate(weights):
            part = dot(source[:, block * depth : (block + 1) * depth], weight[...], 1, 1)
            grad = part if grad is None else grad + part
        low = grad.astype(BF16)
        for slot in range(out.shape[0]):
            out[slot, index * half : (index + 1) * half, :] = low[:, slot * HEAD : (slot + 1) * HEAD]


def head_back(place, near, far, weight):
    half, width = near.shape
    columns = weight.shape[0]
    heads = columns // HEAD
    return grid_call(
        functools.partial(head_back_kernel, weight.blocks),
        "head_back",
        place,
        (1,),
        [fixed((half, width))] * 2 + weight.specs(0, columns),
        fixed((heads, 2 * half, HEAD)),
        like((heads, 2 * half, HEAD), BF16),
        [],
        cost(4 * half * width * columns, 2 * width * (2 * half + columns)),
        [near, far, *weight.arrays()],
    )


def terms_kernel(transposed, blocks, parts, place_ref, left_ref, *refs):
    weights = refs[: blocks * parts]
    sent, kept, *rest = refs[blocks * parts :]
    at = pl.program_id(0)
    left = left_ref
    if rest:
        left = rest[0]

        @pl.when(at == 0)
        def _():
            if len(left_ref.shape) == 3:
                for head in range(left_ref.shape[0]):
                    left[:, head * HEAD : (head + 1) * HEAD] = left_ref[head]
            else:
                heads, kinds = left_ref.shape[:2]
                for head in range(heads):
                    for kind in range(kinds):
                        column = (kind * heads + head) * HEAD
                        left[:, column : column + HEAD] = left_ref[head, kind]
                rest[1][...] = jnp.sum(left[...].astype(F32), axis=0, keepdims=True)

    half = sent.shape[0]
    depth = left.shape[1] // parts
    share = sent.shape[1] // blocks
    for block in range(blocks):
        acc = None
        for part in range(parts):
            weight = weights[part * blocks + block]
            here = dot(
                left[:, part * depth : (part + 1) * depth], weight[...], 1, 1 if transposed else 0
            )
            acc = here if acc is None else acc + here
        tile = acc.shape[1]
        columns = pl.ds(pl.multiple_of(block * share + at * tile, tile), tile)
        kept[:, columns] = acc[:half]
        sent[:, columns] = acc[half:].astype(BF16)


def terms(place, left, weights, transposed, tile):
    tokens = left.shape[-2]
    blocks, parts = weights[0].blocks, len(weights)
    out_axis = 0 if transposed else 1
    share = weights[0].shape[out_axis]
    tile = min(tile, share)
    depth = math.prod(left.shape) // tokens
    half = tokens // 2
    outs = [like((half, blocks * share), BF16), like((half, blocks * share), F32)]
    if left.ndim > 2:
        outs.append(like((tokens, depth), BF16))
    if left.ndim > 3:
        outs.append(like((1, depth), F32))
    return grid_call(
        functools.partial(terms_kernel, transposed, blocks, parts),
        "terms",
        place,
        (share // tile,),
        [fixed(left.shape)] + [spec for w in weights for spec in w.specs(out_axis, tile)],
        [fixed(v.shape) for v in outs],
        outs,
        [],
        cost(
            2 * tokens * depth * blocks * share,
            2 * depth * (tokens + blocks * share) + 6 * half * blocks * share,
        ),
        [left] + [v for w in weights for v in w.arrays()],
    )


def grad_kernel(pairs, place_ref, *refs):
    out = refs[-1]
    acc = None
    for index in range(pairs):
        part = dot(refs[2 * index][...], refs[2 * index + 1][...], 0, 0)
        acc = part if acc is None else acc + part
    out[...] = acc.astype(out.dtype)


def weight_grad(pairs, rows, columns, place, blocks, split_left):
    row_from, row_count = rows
    col_from, col_count = columns
    row_tile = min(1024, row_count // blocks if split_left else row_count)
    col_tile = min(512, col_count if split_left else col_count // blocks)
    row_base, col_base = row_from // row_tile, col_from // col_tile
    specs, values, depth = [], [], 0
    row_per, col_per = row_count // blocks // row_tile, col_count // blocks // col_tile

    def turned(at, per, place_ref):
        return lax.rem(at // per + blocks - place_ref[0], blocks) * per + lax.rem(at, per)

    def left_map(first):
        if split_left:
            return lambda i, j, p: (first, turned(i, row_per, p))
        return lambda i, j, p: (first, i + row_base)

    def right_map(first):
        if split_left:
            return lambda i, j, p: (first, j + col_base)
        return lambda i, j, p: (first, turned(j, col_per, p))

    for (left, left_at), (right, right_at), height in pairs:
        specs.append(pl.BlockSpec((height, row_tile), left_map(left_at)))
        specs.append(pl.BlockSpec((height, col_tile), right_map(right_at)))
        values += [left, right]
        depth += height
    return pl.pallas_call(
        functools.partial(grad_kernel, len(pairs)),
        grid_spec=pltpu.PrefetchScalarGridSpec(
            num_scalar_prefetch=1,
            grid=(row_count // row_tile, col_count // col_tile),
            in_specs=specs,
            out_specs=pl.BlockSpec((row_tile, col_tile), lambda i, j, p: (i, j)),
        ),
        out_shape=like((row_count, col_count), BF16),
        compiler_params=params(),
        cost_estimate=cost(
            2 * row_count * col_count * depth,
            2 * (depth * row_count + depth * col_count + row_count * col_count),
        ),
        name="weight_grad",
    )(place, *values)


def joint_grad_kernel(rows, count, has_add, place_ref, *refs):
    heads, near, far = refs[:rows], refs[rows : rows + count], refs[rows + count : rows + 2 * count]
    out, scratch = refs[-2:]
    _, kinds, size, _ = heads[0].shape
    half = size // 2
    depth = rows * half

    @pl.when(pl.program_id(0) == 0)
    def _():
        for step in range(count):
            source = lax.rem(place_ref[0] + count - step, count)
            for row, head in enumerate(heads):
                for part in range(2):
                    start = ((step * 2 + part) * rows + row) * half
                    for kind in range(kinds):
                        scratch[start : start + half, kind * HEAD : (kind + 1) * HEAD] = head[
                            source, kind, part * half : (part + 1) * half, :
                        ]

    acc = None
    for index in range(2 * count):
        left = (near, far)[index % 2][index // 2]
        part = dot(left[...], scratch[index * depth : (index + 1) * depth, :], 0, 0)
        acc = part if acc is None else acc + part
    if has_add:
        acc = acc + refs[rows + 2 * count][...].astype(F32)
    out[...] = acc.astype(BF16)


def joint_grad_terms(place, near, far, heads, left_cols, add=None):
    row_from, rows = left_cols
    tile = min(256, rows)
    base = row_from // tile
    places, kinds, size, _ = heads[0].shape
    depth = near[0].shape[0]
    specs = [pl.BlockSpec(h.shape, lambda i, p: (0, 0, 0, 0)) for h in heads]
    specs += [pl.BlockSpec((depth, tile), lambda i, p: (0, i + base))] * (2 * places)
    values = [*heads, *near, *far]
    if add is not None:
        specs.append(pl.BlockSpec((tile, kinds * HEAD), lambda i, p: (i, 0)))
        values.append(add)
    return pl.pallas_call(
        functools.partial(joint_grad_kernel, len(heads), places, add is not None),
        grid_spec=pltpu.PrefetchScalarGridSpec(
            num_scalar_prefetch=1,
            grid=(rows // tile,),
            in_specs=specs,
            out_specs=pl.BlockSpec((tile, kinds * HEAD), lambda i, p: (i, 0)),
            scratch_shapes=[pltpu.VMEM((2 * places * depth, kinds * HEAD), BF16)],
        ),
        out_shape=like((rows, kinds * HEAD), BF16),
        compiler_params=params(),
        cost_estimate=cost(
            4 * places * depth * rows * kinds * HEAD, 4 * places * depth * (rows + kinds * HEAD)
        ),
        name="joint_grad",
    )(place, *values)


def gather_blocks(scratch, source, transposed=False):
    count, size, _ = source.shape
    for index in range(count):
        rows = slice(index * size, (index + 1) * size)
        if transposed:
            scratch[:, rows] = source[index].T
        else:
            scratch[rows, :] = source[index]


def put_rows(out, at, query_block, value, lead=()):
    size = out.shape[-2]
    per = query_block // size
    for slot in range(per):
        out[(at * per + slot, *lead)] = value[slot * size : (slot + 1) * size]


def attend_kernel(query_block, key_block, live, *refs):
    q_in, k_in, v_in, seg_row, seg_col, out, mixed_ref, total_ref = refs[:8]
    qs, ks, vs, scores, top, total, mixed = refs[8:]
    at = pl.program_id(0)
    count = qs.shape[0] // key_block

    @pl.when(at == 0)
    def _():
        gather_blocks(qs, q_in)
        gather_blocks(ks, k_in)
        gather_blocks(vs, v_in)

    here = pl.ds(pl.multiple_of(at * query_block, query_block), query_block)
    query = qs[here, :]
    seg_query = seg_row[:, here]
    top[...] = jnp.full_like(top, NEGATIVE)
    total[...] = jnp.zeros_like(total)
    mixed[...] = jnp.zeros_like(mixed)

    def score(step, masked):
        rows = pl.ds(pl.multiple_of(step * key_block, key_block), key_block)
        raw = dot(ks[rows, :], query, 1, 1) * (LOG2E * SCALE)
        if masked:
            raw = jnp.where(seg_col[rows, 0:1] == seg_query, raw, NEGATIVE)
        scores[rows, :] = raw
        top[...] = jnp.maximum(top[...], jnp.max(raw, axis=0, keepdims=True))

    def first(step, carry):
        pl.when(live[at, step] == 1)(functools.partial(score, step, True))
        pl.when(live[at, step] == 2)(functools.partial(score, step, False))
        return carry

    def second(step, carry):
        @pl.when(live[at, step] > 0)
        def _():
            rows = pl.ds(pl.multiple_of(step * key_block, key_block), key_block)
            weight = jnp.exp2(scores[rows, :] - top[...])
            total[...] += jnp.sum(weight, axis=0, keepdims=True)
            mixed[...] += dot(vs[rows, :], weight.astype(BF16), 0, 0)

        return carry

    lax.fori_loop(0, count, first, 0)
    lax.fori_loop(0, count, second, 0)
    result = mixed[...] / total[...]
    mixed_ref[:, here] = result
    total_ref[:, here] = top[...] + jnp.log2(total[...])
    put_rows(out, at, query_block, result.T.astype(BF16))


def attend(row, queries, keys, values, seg_row, seg_col, live):
    parts = queries.shape[0]
    length = seg_row.shape[2]
    size = length // parts
    query_block, key_block = length // live.shape[1], length // live.shape[2]
    part_spec = pl.BlockSpec((parts, size, HEAD), lambda i, s: (0, row, 0))
    whole = lambda i, s: (0, 0)
    return pl.pallas_call(
        functools.partial(attend_kernel, query_block, key_block),
        grid_spec=pltpu.PrefetchScalarGridSpec(
            num_scalar_prefetch=1,
            grid=(length // query_block,),
            in_specs=[
                part_spec,
                part_spec,
                part_spec,
                pl.BlockSpec((None, 1, length), lambda i, s: (row, 0, 0)),
                pl.BlockSpec((None, length, HEAD), lambda i, s: (row, 0, 0)),
            ],
            out_specs=[
                pl.BlockSpec((parts, size, HEAD), lambda i, s: (0, 0, 0)),
                pl.BlockSpec((HEAD, length), whole),
                pl.BlockSpec((1, length), whole),
            ],
            scratch_shapes=[pltpu.VMEM((length, HEAD), BF16)] * 3
            + [
                pltpu.VMEM((length, query_block), F32),
                pltpu.VMEM((1, query_block), F32),
                pltpu.VMEM((1, query_block), F32),
                pltpu.VMEM((HEAD, query_block), F32),
            ],
        ),
        out_shape=[
            like((parts, size, HEAD), BF16),
            like((HEAD, length), F32),
            like((1, length), F32),
        ],
        compiler_params=params(),
        cost_estimate=cost(4 * length * length * HEAD, 8 * length * HEAD, length * length // 2),
        name="attend",
    )(live[row], queries, keys, values, seg_row, seg_col)


def attend_back_kernel(query_block, key_block, live, *refs):
    q_in, k_in, v_in, g_in, seg_row, seg_col, mixed_ref, total_ref, out = refs[:9]
    qs, ks, vs, gs, kt, d_keys, d_values, d_query = refs[9:]
    at = pl.program_id(0)
    count = qs.shape[0] // key_block

    @pl.when(at == 0)
    def _():
        gather_blocks(qs, q_in)
        gather_blocks(ks, k_in)
        gather_blocks(vs, v_in)
        gather_blocks(gs, g_in)
        gather_blocks(kt, k_in, True)
        d_keys[...] = jnp.zeros_like(d_keys)
        d_values[...] = jnp.zeros_like(d_values)

    here = pl.ds(pl.multiple_of(at * query_block, query_block), query_block)
    query = qs[here, :]
    grad = gs[here, :]
    seg_query = seg_row[:, here]
    log_total = total_ref[:, here]
    weighted = jnp.sum(mixed_ref[:, here] * grad.astype(F32).T, axis=0, keepdims=True)
    d_query[...] = jnp.zeros_like(d_query)

    def back(step, masked):
        rows = pl.ds(pl.multiple_of(step * key_block, key_block), key_block)
        key, value = ks[rows, :], vs[rows, :]
        raw = dot(key, query, 1, 1) * (LOG2E * SCALE)
        if masked:
            raw = jnp.where(seg_col[rows, 0:1] == seg_query, raw, NEGATIVE)
        probs = jnp.exp2(raw - log_total)
        d_scores = (probs * (dot(value, grad, 1, 1) - weighted)).astype(BF16)
        d_values[rows, :] += dot(probs.astype(BF16), grad, 1, 0)
        d_keys[rows, :] += dot(d_scores, query, 1, 0)
        d_query[...] += dot(kt[:, rows], d_scores, 1, 0)

    def step_of(step, carry):
        pl.when(live[at, step] == 1)(functools.partial(back, step, True))
        pl.when(live[at, step] == 2)(functools.partial(back, step, False))
        return carry

    lax.fori_loop(0, count, step_of, 0)
    put_rows(out, at, query_block, (d_query[...] * SCALE).T.astype(BF16), (0,))

    @pl.when(at == pl.num_programs(0) - 1)
    def _():
        size = out.shape[2]
        for slot in range(out.shape[0]):
            rows = slice(slot * size, (slot + 1) * size)
            out[slot, 1] = (d_keys[rows, :] * SCALE).astype(BF16)
            out[slot, 2] = d_values[rows, :].astype(BF16)


def attend_back(row, queries, keys, values, grads, seg_row, seg_col, live, mixed, totals):
    parts = queries.shape[0]
    length = seg_row.shape[2]
    size = length // parts
    query_block, key_block = length // live.shape[1], length // live.shape[2]
    part_spec = pl.BlockSpec((parts, size, HEAD), lambda i, s: (0, row, 0))
    whole = lambda i, s: (0, 0)
    return pl.pallas_call(
        functools.partial(attend_back_kernel, query_block, key_block),
        grid_spec=pltpu.PrefetchScalarGridSpec(
            num_scalar_prefetch=1,
            grid=(length // query_block,),
            in_specs=[
                part_spec,
                part_spec,
                part_spec,
                pl.BlockSpec((parts, size, HEAD), lambda i, s: (0, 0, 0)),
                pl.BlockSpec((None, 1, length), lambda i, s: (row, 0, 0)),
                pl.BlockSpec((None, length, HEAD), lambda i, s: (row, 0, 0)),
                pl.BlockSpec((HEAD, length), whole),
                pl.BlockSpec((1, length), whole),
            ],
            out_specs=pl.BlockSpec((parts, 3, size, HEAD), lambda i, s: (0, 0, 0, 0)),
            scratch_shapes=[pltpu.VMEM((length, HEAD), BF16)] * 4
            + [pltpu.VMEM((HEAD, length), BF16)]
            + [pltpu.VMEM((length, HEAD), F32)] * 2
            + [pltpu.VMEM((HEAD, query_block), F32)],
        ),
        out_shape=like((parts, 3, size, HEAD), BF16),
        compiler_params=params(),
        cost_estimate=cost(10 * length * length * HEAD, 16 * length * HEAD, length * length // 2),
        name="attend_back",
    )(live[row], queries, keys, values, grads, seg_row, seg_col, mixed, totals)


def normalize(hidden):
    center = hidden - jnp.mean(hidden, axis=-1, keepdims=True)
    inverse = lax.rsqrt(jnp.mean(center * center, axis=-1, keepdims=True) + EPSILON)
    return center * inverse, inverse


def normalize_back(grad, normal, inverse):
    return inverse * (
        grad
        - jnp.mean(grad, axis=-1, keepdims=True)
        - normal * jnp.mean(grad * normal, axis=-1, keepdims=True)
    )


def add_up(ref, values):
    @pl.when(pl.program_id(0) == 0)
    def _():
        ref[...] = jnp.zeros_like(ref)

    ref[...] += jnp.concatenate([jnp.sum(v, axis=0, keepdims=True) for v in values], axis=0)


def norm_one_kernel(near, far, x, vectors, normal_ref, inverse_ref, low_ref):
    hidden = x[...].astype(F32) + (near[...].astype(F32) + far[...].astype(F32)) + vectors[0:1, :]
    normal, inverse = normalize(hidden)
    normal_ref[...] = normal
    inverse_ref[...] = jnp.broadcast_to(inverse, inverse_ref.shape)
    low_ref[...] = (normal * vectors[1:2, :] + vectors[2:3, :]).astype(BF16)


def norm_two_kernel(near, far, normal_one, grad_ref, vectors, out_ref, second_ref, low_ref, sum_ref):
    hidden = (
        normal_one[...] * vectors[1:2, :]
        + vectors[2:3, :]
        + (near[...].astype(F32) + far[...].astype(F32))
        + vectors[3:4, :]
    )
    normal, inverse = normalize(hidden)
    out_ref[...] = (normal * vectors[4:5, :] + vectors[5:6, :]).astype(BF16)
    grad = grad_ref[...].astype(F32)
    d_hidden = normalize_back(grad * vectors[4:5, :], normal, inverse)
    low = d_hidden.astype(BF16)
    second_ref[...] = d_hidden
    low_ref[...] = low
    add_up(sum_ref, (low.astype(F32), grad * normal, grad))


def norm_back_kernel(near, far, second, normal_ref, inverse_ref, vectors, first_ref, low_ref, sum_ref):
    d_norm = second[...] + (near[...].astype(F32) + far[...].astype(F32))
    normal = normal_ref[...]
    d_hidden = normalize_back(d_norm * vectors[1:2, :], normal, inverse_ref[:, 0:1])
    low = d_hidden.astype(BF16)
    first_ref[...] = d_hidden
    low_ref[...] = low
    add_up(sum_ref, (low.astype(F32), d_norm * normal, d_norm))


def by_tokens(kernel, name, inputs, vectors, outs, sums=0):
    tokens, width = inputs[0][0].shape
    tile = tokens // 4
    specs = [
        pl.BlockSpec((tile, v.shape[1]), lambda i, a=at: (a * 4 + i, 0)) for v, at in inputs
    ]
    out_specs = [pl.BlockSpec((tile, columns), lambda i: (i, 0)) for columns, _ in outs]
    out_shape = [like((tokens, columns), dtype) for columns, dtype in outs]
    if sums:
        out_specs.append(pl.BlockSpec((sums, width), lambda i: (0, 0)))
        out_shape.append(like((sums, width), F32))
    return pl.pallas_call(
        kernel,
        grid=(4,),
        in_specs=specs + [pl.BlockSpec(vectors.shape, lambda i: (0, 0))],
        out_specs=out_specs,
        out_shape=out_shape,
        compiler_params=params(),
        cost_estimate=cost(20 * tokens * width, 16 * tokens * width),
        name=name,
    )(*[v for v, _ in inputs], vectors)


def local(
    layer_input,
    segment_ids,
    qkv_weight,
    qv_bias,
    out_weight,
    out_bias,
    norm1_gain,
    norm1_bias,
    up_weight,
    up_bias,
    down_weight,
    down_bias,
    norm2_gain,
    norm2_bias,
    out_grad,
):
    rows, local_len, width = layer_input.shape
    fsdp, ctx = lax.axis_size("fsdp"), lax.axis_size("ctx")
    y, place = lax.axis_index("fsdp"), lax.axis_index("ctx")
    core = lax.axis_index("tp") % 2
    columns = qkv_weight.shape[2]
    hidden_units = up_weight.shape[1]
    heads = columns // HEAD
    half = local_len // 2
    share = width // fsdp
    each = range(rows)
    assert heads == ctx == 4 and lax.axis_size("tp") == 4
    order = Order()

    def features(value):
        return rotate(value, value.ndim - 1, y, fsdp)

    def features_back(value):
        return rotate(value, value.ndim - 1, (fsdp - y) % fsdp, fsdp)

    def spread(block):
        return [block] + [shift(block, "fsdp", -by) for by in range(1, fsdp)]

    def swap_ctx(value):
        return lax.all_to_all(value, "ctx", 0, 0, tiled=True)

    def from_all(value):
        return swap_ctx(jnp.broadcast_to(value[None], (ctx, *value.shape)))

    def both(value):
        return value, core_swap(value)

    seg_own = rotate(segment_ids, 1, core, 2)
    seg = from_all(seg_own).transpose(1, 0, 2).reshape(rows, ctx * local_len)

    x_rows = features(rotate(layer_input, 1, core, 2))
    x = x_rows.reshape(rows * local_len, width)

    vectors = features(
        jnp.stack([out_bias, norm1_gain, norm1_bias, down_bias, norm2_gain, norm2_bias])
    ).astype(F32)
    grad_half = features(
        lax.dynamic_slice_in_dim(out_grad, core * half, half, axis=1)
    ).reshape(rows * half, width)

    zero_bias = jnp.zeros_like(qv_bias[:1])
    biases = qv_bias[:1], zero_bias, qv_bias[1:]
    pair = spread(jnp.stack([qkv_weight[:, 0], qkv_weight[:, 1]]))
    cuts = share // columns
    pieces = [out_weight[:, i * columns : (i + 1) * columns] for i in range(cuts)]
    rest = jnp.concatenate([qkv_weight[:, 2], *pieces], axis=0)
    rest, seg, *pair[1:] = lax.optimization_barrier((rest, seg, *pair[1:]))
    rest = [v[None] for v in spread(after(rest, x))]
    joint_matrices = [
        Weight([(v, 0, 0) for v in pair], 0, fsdp),
        Weight([(v, 1, 0) for v in pair], 0, fsdp),
        Weight([(v, 0, 0) for v in rest], 0, fsdp, share),
    ]
    if cuts:
        out_parts = [(v, 0, cuts + i) for v in rest for i in range(cuts)]
        out_full = Weight(out_parts, 1, fsdp * cuts, columns)
    else:
        out_full = Weight([(v, None, 0) for v in spread(after(out_weight, rest[1]))], 1, fsdp)
    query_pieces = project(x, joint_matrices[0], biases[0])
    queries = swap_ctx(query_pieces)
    key_pieces = project(after(x, query_pieces), joint_matrices[1], biases[1])
    keys = swap_ctx(after(key_pieces, queries))
    gate = [*rest[1:], keys]

    def whole(block, axis):
        full = lax.all_gather(after(block, *gate), "fsdp", axis=axis, tiled=True)
        return Weight([full], axis, fsdp)

    up_full = whole(up_weight, 0)
    down_full = whole(down_weight, 1)
    pieces = order.done(project(after(x, key_pieces), joint_matrices[2], biases[2]))
    values = swap_ctx(after(pieces, keys))
    fsdp_place = y.astype(jnp.int32)[None]

    length = ctx * local_len
    seg_row = seg[:, None, :]
    seg_col = jnp.broadcast_to(seg[:, :, None], (rows, length, HEAD))

    def span(size):
        blocks = seg.reshape(rows, length // size, size)
        return jnp.min(blocks, axis=2), jnp.max(blocks, axis=2)

    (query_low, query_high), (key_low, key_high) = span(2 * local_len), span(local_len)
    meets = (query_low[:, :, None] <= key_high[:, None, :]) & (
        key_low[:, None, :] <= query_high[:, :, None]
    )
    same = (query_low == query_high)[:, :, None] & (key_low == key_high)[:, None, :] & meets
    live = meets.astype(jnp.int32) + same.astype(jnp.int32)

    attended, kept = [], []
    for r in each:
        pieces, mixed, totals = attend(
            r, order.ready(queries), keys, values, seg_row, seg_col, live
        )
        order.done(totals)
        kept.append((mixed, totals))
        attended.append(swap_ctx(pieces))

    def begin(left, weights, transposed, tile):
        sent, mine, *rest = terms(fsdp_place, order.ready(left), weights, transposed, tile)
        order.done(sent)
        return core_swap(sent), mine, *rest

    def middle(near, mine):
        total = order.done((order.ready(mine) + near.astype(F32)).astype(BF16))
        return total, chip_swap(total)

    parts = [begin(attended[r], [out_full], False, 512) for r in each]
    attended_last = attended[-1]
    attended = [parts[r][2] for r in each]
    totals = [middle(*parts[r][:2]) for r in each]

    x_near = [after(x_rows[:, :half].reshape(rows * half, width), attended_last)]
    x_near.append(shift(x_near[0], "ctx", 1))

    normal_one, inverse_one, norm_low = [], [], []
    for r in each:
        near, far = totals[r]
        normal, inverse, low = by_tokens(
            norm_one_kernel,
            "norm_one",
            [(order.ready(near), 0), (far, 0), (x, 2 * r)],
            vectors,
            [(width, F32), (HEAD, F32), (width, BF16)],
        )
        order.done(low)
        normal_one.append(normal)
        inverse_one.append(inverse)
        norm_low.append(both(low))

    act_low, slopes = [], []
    for r in each:
        near, far = norm_low[r]
        if r == 0:
            x_near.append(shift(order.ready(x_near[1]), "ctx", 1))
        act, slope = up_project(fsdp_place, order.ready(near), far, up_full, up_bias[None])
        order.done(act)
        act_low.append(act)
        slopes.append(slope)

    order.pin(x_near[2])
    x_near.append(shift(x_near[2], "ctx", 1))
    parts = [begin(act_low[r], [down_full], False, 512) for r in each]
    totals = [middle(*parts[r]) for r in each]

    layer_low, second, mlp_low, sums_two = [], [], [], []
    pre_low, up_sums, up_parts = [], [], []

    def norm_two(r):
        near, far = totals[r]
        out, d_second, low, sums = by_tokens(
            norm_two_kernel,
            "norm_two",
            [(order.ready(near), 0), (far, 0), (normal_one[r], 0), (grad_half, r)],
            vectors,
            [(width, BF16), (width, F32), (width, BF16)],
            3,
        )
        order.done(low)
        layer_low.append(out)
        second.append(d_second)
        mlp_low.append(both(low))
        sums_two.append(sums)

    def act_step(r):
        near, far = mlp_low[r]
        low, sums = act_back(fsdp_place, order.ready(near), far, down_full, slopes[r])
        order.done(low)
        pre_low.append(low)
        up_sums.append(sums)

    def up_step(r):
        up_parts.append(begin(pre_low[r], [up_full], True, 512))

    halves = range(2)
    gradients = {}

    def pairs_of(left, right):
        made = []
        for r in each:
            for h in halves:
                a = (left[r][h], 0) if isinstance(left[r], tuple) else (left[r], h)
                b = (right[r][h], 0) if isinstance(right[r], tuple) else (right[r], h)
                made.append((a, b, half))
        return made

    def give(name, pairs, shape, split_left, piece, pieces):
        (left, *others) = pairs
        left = ((order.ready(left[0][0]), left[0][1]), *left[1:])
        if split_left:
            part = shape[1] // pieces
            ranges = (0, shape[0]), (piece * part, part)
        else:
            part = shape[0] // pieces
            ranges = (piece * part, part), (0, shape[1])
        mine = order.done(
            weight_grad([left, *others], *ranges, fsdp_place, fsdp, split_left)
        )
        gradients[name, piece] = lax.psum_scatter(
            mine, "fsdp", scatter_dimension=0 if split_left else 1, tiled=True
        )

    def line_one(value):
        return value, lax.ppermute(value, "ctx", [(0, 1), (3, 2)])

    def line_two(value, other):
        pair = order.done((order.ready(value).astype(F32) + other.astype(F32)).astype(BF16))
        return pair, lax.ppermute(pair, "ctx", [(1, 2), (2, 1)])

    def line_three(pair, other):
        total = order.done((order.ready(pair).astype(F32) + other.astype(F32)).astype(BF16))
        return total, lax.ppermute(total, "ctx", [(1, 0), (2, 3)])

    outer = (place == 0) | (place == ctx - 1)

    def line_end(total, other):
        return jnp.where(outer, other, total)

    first, attn_low, sums_one, head_grads = [], [], [], []

    def norm_back(r):
        near, far = up_totals[r]
        d_first, low, sums = by_tokens(
            norm_back_kernel,
            "norm_back",
            [(order.ready(near), 0), (far, 0), (second[r], 0), (normal_one[r], 0), (inverse_one[r], 0)],
            vectors,
            [(width, F32), (width, BF16)],
            3,
        )
        order.done(low)
        first.append(d_first)
        attn_low.append(both(low))
        sums_one.append(sums)

    def head_step(r):
        near, far = attn_low[r]
        pieces = order.done(head_back(fsdp_place, order.ready(near), far, out_full))
        head_grads.append(swap_ctx(pieces))

    joint_back, joint_rows = [], []

    def attend_step(r):
        mixed, row_totals = kept[r]
        grads = order.ready(head_grads[r])
        pieces = attend_back(
            r, queries, keys, values, grads, seg_row, seg_col, live, mixed, row_totals
        )
        joint_back.append(order.done(pieces))
        joint_rows.append(swap_ctx(pieces))

    lined = {}

    def line_start(name, piece):
        lined[name, piece] = line_one(order.ready(gradients[name, piece]))

    def line_step(step, name, piece):
        lined[name, piece] = step(*lined[name, piece])

    def small_start(value):
        value = value + shift(value, "fsdp", 1) if fsdp == 2 else lax.psum(value, "fsdp")
        value = order.done(value)
        return value, lax.ppermute(value, "ctx", [(0, 1), (1, 0), (2, 3), (3, 2)])

    def small_step(value, other):
        value = order.done(order.ready(value) + other)
        return value, lax.ppermute(value, "ctx", [(0, 2), (2, 0), (1, 3), (3, 1)])

    def small_end(value, other):
        return order.done(order.ready(value) + other)

    norm_two(0)
    act_step(0)
    up_step(0)
    order.pin(x_near[3])
    norm_two(1)
    up_totals = [middle(*up_parts[0])]
    down_args = (pairs_of(act_low, mlp_low), (hidden_units, width), False)
    give("down", *down_args, 0, 2)
    act_step(1)
    up_step(1)
    give("down", *down_args, 1, 2)
    up_totals.append(middle(*up_parts[1]))
    up_args = (pairs_of(norm_low, pre_low), (width, hidden_units), True)
    norm_back(0)
    give("up", *up_args, 0, 2)
    head_step(0)
    line_start("down", 0)
    norm_back(1)
    give("up", *up_args, 1, 2)
    head_step(1)
    out_args = (pairs_of(attended, attn_low), (columns, width), False)
    give("out", *out_args, 0, 1)
    wide = features_back(jnp.concatenate([sum(sums_two), sum(sums_one)], axis=0))
    wide = wide + core_swap(wide)
    line_step(line_two, "down", 0)
    line_start("down", 1)
    attend_step(0)
    wide_small = small_start(jnp.concatenate([wide.reshape(-1), sum(up_sums).reshape(-1)]))
    attend_step(1)

    x_far = [x_rows[:, half:].reshape(rows * half, width)] + [core_swap(v) for v in x_near[1:]]
    ctx_place = place.astype(jnp.int32)[None]
    arrived = None
    for by in range(1, fsdp):
        sent = joint_grad_terms(
            ctx_place, [order.ready(x_near[0])] + x_near[1:], x_far, joint_back, (by * share, share)
        )
        got = shift(order.done(sent), "fsdp", by)
        arrived = got if arrived is None else (arrived.astype(F32) + got.astype(F32))

    line_step(line_three, "down", 0)
    line_step(line_two, "down", 1)
    line_start("up", 0)
    wide_small = small_step(*wide_small)
    in_parts = [begin(joint_rows[0], joint_matrices, True, 512)]
    mine = joint_grad_terms(
        ctx_place, [order.ready(x_near[0])] + x_near[1:], x_far, joint_back, (0, share), add=arrived
    )
    order.done(mine)
    in_totals = [middle(*in_parts[0][:2])]
    line_step(line_three, "down", 1)
    line_step(line_two, "up", 0)
    line_start("up", 1)
    wide_small = small_end(*wide_small)
    in_parts.append(begin(joint_rows[1], joint_matrices, True, 512))
    joint_all = from_all(mine)
    in_totals.append(middle(*in_parts[1][:2]))
    bias_sums = sum(p[3] for p in in_parts)
    late_small = small_start(
        jnp.concatenate([bias_sums[0, :columns], bias_sums[0, 2 * columns :]])
    )
    line_step(line_three, "up", 0)
    line_step(line_two, "up", 1)
    line_start("out", 0)
    late_small = small_step(*late_small)
    line_step(line_three, "up", 1)
    line_step(line_two, "out", 0)
    late_small = small_end(*late_small)
    line_step(line_three, "out", 0)

    input_low = []
    for r in each:
        near, far = in_totals[r]
        input_low.append(both((first[r] + (near.astype(F32) + far.astype(F32))).astype(BF16)))

    def whole_rows(values):
        stacked = jnp.stack([jnp.concatenate(pair, axis=0) for pair in values])
        return features_back(rotate(stacked, 1, core, 2))

    layer_output = whole_rows([both(v) for v in layer_low])
    input_grad = whole_rows(input_low).astype(F32)

    joint_grad = (
        joint_all.reshape(ctx, share, 3, HEAD).transpose(1, 2, 0, 3).reshape(share, 3, columns)
    ).astype(F32)

    wide = wide_small[: 6 * width].reshape(6, width)
    up_bias_grad = wide_small[6 * width :]
    qv_bias_grad = late_small.reshape(2, columns)

    def final(name, pieces, axis=0):
        return jnp.concatenate(
            [line_end(*lined[name, p]) for p in range(pieces)], axis=axis
        ).astype(F32)

    return (
        layer_output,
        input_grad,
        joint_grad,
        qv_bias_grad,
        final("out", 1),
        wide[3],
        wide[4],
        wide[5],
        final("up", 2, 1),
        up_bias_grad,
        final("down", 2),
        wide[0],
        wide[1],
        wide[2],
    )


def solution(mesh):
    weights = P("fsdp", None, "tp"), P(None, "tp"), P("tp", "fsdp")
    tokens = P("fsdp", "ctx", None)
    up, down = P("fsdp", "tp"), P("tp", "fsdp")
    tail = (P(), P(), P(), up, P("tp"), down, P(), P(), P())
    return jax.shard_map(
        local,
        mesh=mesh,
        in_specs=(tokens, P("fsdp", "ctx"), *weights, *tail, tokens),
        out_specs=(tokens, tokens, *weights, *tail),
        check_vma=False,
    )
```

time: 1220 us -> 1030 us (0.84)
  matrix products: 82.3 us -> 0 us
  Pallas kernels: 205 us -> 286 us
  other arithmetic: 181 us -> 103 us
  starting transfers between devices: 202 us -> 124 us
  local copies, waits for them, and re-layouts: 79 us -> 40 us
  waiting for transfers between devices: 462 us -> 447 us
  between operations: 3.24 us -> 15.5 us
    ppermute x49 -> x8, waiting for transfers between devices: 308 us -> 74.4 us  [shift(): lax.ppermute(value, axis, [(i, (i + by) % size) for i in range(size)])]
    ppermute x49 -> x8, starting transfers between devices: 149 us -> 9.13 us  [shift(): lax.ppermute(value, axis, [(i, (i + by) % size) for i in range(size)])]
    all_to_all x0 -> x11, waiting for transfers between devices: none -> 95.1 us  [swap_ctx(): return lax.all_to_all(value, 'ctx', 0, 0, tiled=True)]
    ppermute x17 -> x19, waiting for transfers between devices: 62.6 us -> 157 us  [the longest x5 60 us: line_one(): return (value, lax.ppermute(value, 'ctx', [(0, 1), (3, 2)]))]
    dot_general x14 -> x0, matrix products: 82.3 us -> none  [dot(): lax.dot_general(left, right, (((left_dim,), (right_dim,)), ((), ())), pre...]
    pallas_call x19 -> x34, Pallas kernels: 205 us -> 286 us  [the longest x14 114 us: grid_call(): pl.pallas_call(kernel, grid_spec=pltpu.PrefetchScalarGridSpec(num_scalar_...]
    concatenate x27 -> x3, other arithmetic: 62.8 us -> 0.15 us  [the longest x1 0.14 us: local(): rest = jnp.concatenate([qkv_weight[:, 2], *pieces], axis=0)]
    all_to_all x0 -> x11, starting transfers between devices: none -> 46 us  [swap_ctx(): return lax.all_to_all(value, 'ctx', 0, 0, tiled=True)]
  transfers between devices with their start and end apart: 96 -> 75, of which waited for: 33 -> 32; matrix products, arithmetic and copies ran while one was open for 27% -> 12% of each run, Pallas kernels for 17% -> 26%
where the time goes in v2:
time: 1030 us; the launch traced here: 1020 us
  waiting for transfers between devices  447 us (43%)
  Pallas kernels  286 us (28%)
  starting transfers between devices  124 us (12%)
  other arithmetic  103 us (10%)
  local copies, waits for them, and re-layouts  40 us (4%)
  between operations  15.5 us (2%)
    pallas_call x14, Pallas kernels, grid_call(): pl.pallas_call(kernel, grid_spec=pltpu.PrefetchScalarGridSpec(num_scalar_...  114 us
    ppermute x8, waiting for transfers between devices, chip_swap(): return lax.ppermute(value, 'tp', [(i, i ^ 2) for i in range(size)])  98.9 us
    all_to_all x11, waiting for transfers between devices, swap_ctx(): return lax.all_to_all(value, 'ctx', 0, 0, tiled=True)  95.1 us
    ppermute x8, waiting for transfers between devices, shift(): lax.ppermute(value, axis, [(i, (i + by) % size) for i in range(size)])  74.4 us
    ppermute x5, waiting for transfers between devices, line_one(): return (value, lax.ppermute(value, 'ctx', [(0, 1), (3, 2)]))  60 us
    ppermute x5, waiting for transfers between devices, line_three(): return (total, lax.ppermute(total, 'ctx', [(1, 0), (2, 3)]))  59.9 us
    all_to_all x11, starting transfers between devices, swap_ctx(): return lax.all_to_all(value, 'ctx', 0, 0, tiled=True)  46 us
    pallas_call x5, Pallas kernels, weight_grad(): pl.pallas_call(functools.partial(grad_kernel, len(pairs)), grid_spec=pltp...  41.5 us
  transfers between devices with their start and end apart: 75, of which 32 were waited for; matrix products, arithmetic and copies ran while one was open for 12% of the time, Pallas kernels for 26%

profile of v2, /device:TPU:0, one launch (start us, length us, event | category | flops | bytes accessed | tf_op | source)
XLA Modules:
  0.0 1015.4 jit_solution(8807508507818477639)
XLA Ops:
  27.0 32.6 %collective-permute-done.refs_1_.refs_3_ = bf16[2,1024,512]{2,1,0:T(8,128)(2,1)} collective-permute-done((bf16[2,1024,512]{2,1,0:T(8,128)(2,1)}, bf16[2,1024,512]{2,1,0:T(8,128)(2,1)}, u32[]{:S(2)}, u32[]{:S(2)}) %collective-permute-start) | collective-permute-done | bytes 2097184 | tf_op jit(solution)/shard_map/ppermute | solution.py:52
  79.1 16.6 %all-to-all-done.1.refs_0_ = bf16[4,1024,128]{2,1,0:T(8,128)(2,1)S(1)} async-done(((bf16[4,1024,128]{2,1,0:T(8,128)(2,1)}), bf16[4,1024,128]{2,1,0:T(8,128)(2,1)S(1)}, u32[]{:S(2)}, u32[]{:S(2)}) %all-to-all-start.1) | async-done | bytes 1048608 | tf_op jit(solution)/shard_map/all_to_all | solution.py:788
  100.1 17.2 %collective-permute-done.1 = bf16[2048,512]{1,0:T(8,128)(2,1)} collective-permute-done((bf16[2048,512]{1,0:T(8,128)(2,1)S(1)}, bf16[2048,512]{1,0:T(8,128)(2,1)}, u32[]{:S(2)}, u32[]{:S(2)}) %collective-permute-start.1) | collective-permute-done | bytes 2097184 | tf_op jit(solution)/shard_map/ppermute | solution.py:52
  137.6 23.4 %all-to-all-done.3.refs_2_ = bf16[4,1024,128]{2,1,0:T(8,128)(2,1)S(1)} async-done(((bf16[4,1024,128]{2,1,0:T(8,128)(2,1)}), bf16[4,1024,128]{2,1,0:T(8,128)(2,1)S(1)}, u32[]{:S(2)}, u32[]{:S(2)}) %all-to-all-start.3) | async-done | bytes 1048608 | tf_op jit(solution)/shard_map/all_to_all | solution.py:788
  163.3 11.9 %attend.2 = (bf16[4,512,128]{2,1,0:T(8,128)(2,1)}, f32[128,2048]{1,0:T(8,128)}, f32[1,2048]{1,0:T(1,128)}) custom-call(s32[2,4]{1,0:T(2,128)} %get-tuple-element.312.live, bf16[4,1024,128]{2,1,0:T(8,128)(2,1)} %copy-done.2, bf16[4,1024,128]{2,1,0:T(8,128)(2,1)} %all-to-all-done.2.refs_1_, bf16[4,1024,128]{2,1,0:T(8,128)(2,1)} %copy-done.3, ...), custom_call_target="tpu_custom_call" | custom-call | flops 8388608 | bytes 8192 | tf_op jit(solution)/shard_map/attend/pallas_call | solution.py:544
  178.7 11.9 %attend.3 = (bf16[4,512,128]{2,1,0:T(8,128)(2,1)}, f32[128,2048]{1,0:T(8,128)}, f32[1,2048]{1,0:T(1,128)}) custom-call(s32[2,4]{1,0:T(2,128)} %get-tuple-element.313.live, bf16[4,1024,128]{2,1,0:T(8,128)(2,1)} %copy-done.2, bf16[4,1024,128]{2,1,0:T(8,128)(2,1)} %all-to-all-done.2.refs_1_, bf16[4,1024,128]{2,1,0:T(8,128)(2,1)} %copy-done.3, ...), custom_call_target="tpu_custom_call" | custom-call | flops 8388608 | bytes 8192 | tf_op jit(solution)/shard_map/attend/pallas_call | solution.py:544
  200.9 9.2 all-to-all-done.5.left_ref
  224.6 21.8 %collective-permute-done.4.far = bf16[256,2048]{1,0:T(8,128)(2,1)} collective-permute-done((bf16[256,2048]{1,0:T(8,128)(2,1)S(1)}, bf16[256,2048]{1,0:T(8,128)(2,1)}, u32[]{:S(2)}, u32[]{:S(2)}) %collective-permute-start.4) | collective-permute-done | bytes 1048608 | tf_op jit(solution)/shard_map/ppermute | solution.py:47
  251.4 17.0 %collective-permute-done.5.far = bf16[256,2048]{1,0:T(8,128)(2,1)} collective-permute-done((bf16[256,2048]{1,0:T(8,128)(2,1)}, bf16[256,2048]{1,0:T(8,128)(2,1)}, u32[]{:S(2)}, u32[]{:S(2)}) %collective-permute-start.5) | collective-permute-done | bytes 1048608 | tf_op jit(solution)/shard_map/ppermute | solution.py:47
  277.6 10.8 %up_project.2 = (bf16[512,2048]{1,0:T(8,128)(2,1)}, bf16[512,2048]{1,0:T(8,128)(2,1)}) custom-call(s32[1]{0:T(128)} %bitcast.place_ref, bf16[256,2048]{1,0:T(8,128)(2,1)} %get-tuple-element.217.near.refs_0_, bf16[256,2048]{1,0:T(8,128)(2,1)} %copy-done.6, bf16[2048,2048]{1,0:T(8,128)(2,1)} %all-gather.3.cloned.1.call-done.refs_0_.refs_1_, ...), custom_call_target="tpu_custom_call" | custom-call | flops 16777216 | bytes 57344 | tf_op jit(solution)/shard_map/up_project/pallas_call | solution.py:124
  289.4 10.8 %up_project.3 = (bf16[512,2048]{1,0:T(8,128)(2,1)}, bf16[512,2048]{1,0:T(8,128)(2,1)}) custom-call(s32[1]{0:T(128)} %bitcast.place_ref, bf16[256,2048]{1,0:T(8,128)(2,1)} %get-tuple-element.167.near.refs_4_, bf16[256,2048]{1,0:T(8,128)(2,1)} %copy-done.7, bf16[2048,2048]{1,0:T(8,128)(2,1)} %all-gather.3.cloned.1.call-done.refs_0_.refs_1_, ...), custom_call_target="tpu_custom_call" | custom-call | flops 16777216 | bytes 57344 | tf_op jit(solution)/shard_map/up_project/pallas_call | solution.py:124
  300.1 22.4 %collective-permute-done.9.refs_4_ = bf16[512,2048]{1,0:T(8,128)(2,1)} collective-permute-done((bf16[512,2048]{1,0:T(8,128)(2,1)}, bf16[512,2048]{1,0:T(8,128)(2,1)}, u32[]{:S(2)}, u32[]{:S(2)}) %collective-permute-start.9) | collective-permute-done | bytes 2097184 | tf_op jit(solution)/shard_map/ppermute | solution.py:52
  322.5 11.7 %all-gather.5.cloned.1.call-done.refs_0_.refs_1_ = bf16[2048,2048]{1,0:T(8,128)(2,1)} async-done(((bf16[2048,1024]{1,0:T(8,128)(2,1)}), bf16[2048,2048]{1,0:T(8,128)(2,1)}) %all-gather.5.cloned.1.call-update) | async-done | bytes 8388624 | tf_op jit(solution)/shard_map/all_gather | solution.py:834
  334.2 9.1 terms.10
  345.2 9.4 terms.11
  361.0 19.5 %collective-permute-done.12.far = bf16[256,2048]{1,0:T(8,128)(2,1)S(1)} collective-permute-done((bf16[256,2048]{1,0:T(8,128)(2,1)S(1)}, bf16[256,2048]{1,0:T(8,128)(2,1)S(1)}, u32[]{:S(2)}, u32[]{:S(2)}) %collective-permute-start.12) | collective-permute-done | bytes 1048608 | tf_op jit(solution)/shard_map/ppermute | solution.py:47
  391.7 9.6 act_back.2
  401.3 9.2 terms.12
  433.3 10.0 act_back.3
  443.3 9.2 terms.13
  467.7 20.2 %collective-permute-done.21.far = bf16[256,2048]{1,0:T(8,128)(2,1)S(1)} collective-permute-done((bf16[256,2048]{1,0:T(8,128)(2,1)S(1)}, bf16[256,2048]{1,0:T(8,128)(2,1)S(1)}, u32[]{:S(2)}, u32[]{:S(2)}) %collective-permute-start.21) | collective-permute-done | bytes 1048608 | tf_op jit(solution)/shard_map/ppermute | solution.py:47
  511.9 17.6 %collective-permute-done.23.far = bf16[256,2048]{1,0:T(8,128)(2,1)S(1)} collective-permute-done((bf16[256,2048]{1,0:T(8,128)(2,1)S(1)}, bf16[256,2048]{1,0:T(8,128)(2,1)S(1)}, u32[]{:S(2)}, u32[]{:S(2)}) %collective-permute-start.23) | collective-permute-done | bytes 1048608 | tf_op jit(solution)/shard_map/ppermute | solution.py:47
  566.1 35.2 %all-to-all-done.6.refs_3_ = bf16[4,512,128]{2,1,0:T(8,128)(2,1)} async-done(((bf16[4,512,128]{2,1,0:T(8,128)(2,1)}), bf16[4,512,128]{2,1,0:T(8,128)(2,1)}, u32[]{:S(2)}, u32[]{:S(2)}) %all-to-all-start.6) | async-done | bytes 524320 | tf_op jit(solution)/shard_map/all_to_all | solution.py:788
  622.2 17.3 %attend_back.2.refs_0_ = bf16[4,3,512,128]{3,2,1,0:T(8,128)(2,1)} custom-call(s32[2,4]{1,0:T(2,128)} %get-tuple-element.312.live, bf16[4,1024,128]{2,1,0:T(8,128)(2,1)} %copy-done.2, bf16[4,1024,128]{2,1,0:T(8,128)(2,1)} %all-to-all-done.2.refs_1_, bf16[4,1024,128]{2,1,0:T(8,128)(2,1)} %copy-done.3, bf16[4,512,128]{2,1,0:T(8,128)(2,1)} %all-to-all-done.6.refs_3_, ...), custom_call_target="tpu_custom_call" | custom-call | flops 20971520 | bytes 16384 | tf_op jit(solution)/shard_map/attend_back/pallas_call | solution.py:640
  649.8 17.3 %attend_back.3.refs_1_ = bf16[4,3,512,128]{3,2,1,0:T(8,128)(2,1)} custom-call(s32[2,4]{1,0:T(2,128)} %get-tuple-element.313.live, bf16[4,1024,128]{2,1,0:T(8,128)(2,1)} %copy-done.2, bf16[4,1024,128]{2,1,0:T(8,128)(2,1)} %all-to-all-done.2.refs_1_, bf16[4,1024,128]{2,1,0:T(8,128)(2,1)} %copy-done.3, bf16[4,512,128]{2,1,0:T(8,128)(2,1)} %copy-done.26, ...), custom_call_target="tpu_custom_call" | custom-call | flops 20971520 | bytes 16384 | tf_op jit(solution)/shard_map/attend_back/pallas_call | solution.py:640
  668.9 9.7 joint_grad.2
  703.5 9.2 terms.14
  721.2 9.9 joint_grad.3
  749.4 30.8 %collective-permute-done.40 = f32[14336]{0:T(1024)S(1)} collective-permute-done((f32[14336]{0:T(1024)S(1)}, f32[14336]{0:T(1024)S(1)}, u32[]{:S(2)}, u32[]{:S(2)}) %collective-permute-start.40) | collective-permute-done | bytes 57376 | tf_op jit(solution)/shard_map/ppermute | solution.py:1035
  819.8 58.9 %collective-permute-done.46 = bf16[1024,1024]{1,0:T(8,128)(2,1)S(1)} collective-permute-done((bf16[1024,1024]{1,0:T(8,128)(2,1)}, bf16[1024,1024]{1,0:T(8,128)(2,1)S(1)}, u32[]{:S(2)}, u32[]{:S(2)}) %collective-permute-start.46) | collective-permute-done | bytes 2097184 | tf_op jit(solution)/shard_map/ppermute | solution.py:972
  940.7 46.5 %collective-permute-done.54 = bf16[1024,1024]{1,0:T(8,128)(2,1)} collective-permute-done((bf16[1024,1024]{1,0:T(8,128)(2,1)S(1)}, bf16[1024,1024]{1,0:T(8,128)(2,1)}, u32[]{:S(2)}, u32[]{:S(2)}) %collective-permute-start.54) | collective-permute-done | bytes 2097184 | tf_op jit(solution)/shard_map/ppermute | solution.py:980
  993.5 13.4 %collective-permute-done.52 = bf16[512,1024]{1,0:T(8,128)(2,1)S(1)} collective-permute-done((bf16[512,1024]{1,0:T(8,128)(2,1)S(1)}, bf16[512,1024]{1,0:T(8,128)(2,1)S(1)}, u32[]{:S(2)}, u32[]{:S(2)}) %collective-permute-start.52) | collective-permute-done | bytes 1048608 | tf_op jit(solution)/shard_map/ppermute | solution.py:980
  (369 shorter events, 420.8 us)
Async XLA Ops:
  100.0 176.6 %all-gather.3.cloned.1.call-start = ((), (), s32[]{:S(2)}) async-start(), calls=%async_computation.16 | async-start | bytes 12582912 | tf_op jit(solution)/shard_map/all_gather | solution.py:834
  125.3 208.9 %all-gather.5.cloned.1.call-start = ((), (), s32[]{:S(2)}) async-start(), calls=%async_computation.17 | async-start | bytes 12582912 | tf_op jit(solution)/shard_map/all_gather | solution.py:834
  196.1 349.3 %reduce-scatter.6.cloned.1.call-start = ((), (), s32[]{:S(2)}) async-start(), calls=%async_computation.18 | async-start | bytes 6291456 | tf_op jit(solution)/shard_map/reduce_scatter | solution.py:967
  217.6 55.6 %collective-permute-start.8 = (bf16[512,2048]{1,0:T(8,128)(2,1)S(1)}, bf16[512,2048]{1,0:T(8,128)(2,1)}, u32[]{:S(2)}, u32[]{:S(2)}) collective-permute-start(bf16[512,2048]{1,0:T(8,128)(2,1)S(1)} %bitcast.58), channel_id=1, source_target_pairs={{0,4},{4,8},{8,12},{12,0},{1,5},{5,9},{9,13},{13,1},{2,6},{6,10},{... | collective-permute-start | bytes 6291464 | tf_op jit(solution)/shard_map/ppermute | solution.py:52
  359.0 51.7 %collective-permute-start.15 = (bf16[512,2048]{1,0:T(8,128)(2,1)}, bf16[512,2048]{1,0:T(8,128)(2,1)S(1)}, u32[]{:S(2)}, u32[]{:S(2)}) collective-permute-start(bf16[512,2048]{1,0:T(8,128)(2,1)} %collective-permute-done.9.refs_4_), channel_id=1, source_target_pairs={{0,4},{4,8},{8,12},{12,0},{1,5},{5,9},{9,13},{13,1},{2,6},{6,10},{... | collective-permute-start | bytes 6291464 | tf_op jit(solution)/shard_map/ppermute | solution.py:52
  433.3 179.9 %reduce-scatter.8.cloned.1.call-start = ((), (), s32[]{:S(2)}) async-start(), calls=%async_computation.19 | async-start | bytes 6291456 | tf_op jit(solution)/shard_map/reduce_scatter | solution.py:967
  461.3 229.8 %reduce-scatter.10.cloned.1.call-start = ((), (), s32[]{:S(2)}) async-start(), calls=%async_computation.20 | async-start | bytes 6291456 | tf_op jit(solution)/shard_map/reduce_scatter | solution.py:967
  503.7 282.3 %reduce-scatter.12.cloned.1.call-start = ((), (), s32[]{:S(2)}) async-start(), calls=%async_computation.21 | async-start | bytes 6291456 | tf_op jit(solution)/shard_map/reduce_scatter | solution.py:967
  545.4 60.6 %collective-permute-start.25 = (bf16[1024,1024]{1,0:T(8,128)(2,1)}, bf16[1024,1024]{1,0:T(8,128)(2,1)}, u32[]{:S(2)}, u32[]{:S(2)}) collective-permute-start(bf16[1024,1024]{1,0:T(8,128)(2,1)} %reduce-scatter.6.cloned.1.call-done), channel_id=1, source_target_pairs={{0,4},{12,8},{1,5},{13,9},{2,6},{14,10},{3,7},{15,11},{16,20},{28,... | collective-permute-start | bytes 6291464 | tf_op jit(solution)/shard_map/ppermute | solution.py:972
  550.2 62.4 %collective-permute-start.28 = (bf16[512,2048]{1,0:T(8,128)(2,1)}, bf16[512,2048]{1,0:T(8,128)(2,1)}, u32[]{:S(2)}, u32[]{:S(2)}) collective-permute-start(bf16[512,2048]{1,0:T(8,128)(2,1)} %collective-permute-done.8.refs_3_), channel_id=1, source_target_pairs={{0,1},{1,0},{2,3},{3,2},{4,5},{5,4},{6,7},{7,6},{8,9},{9,8},{10,11... | collective-permute-start | bytes 6291464 | tf_op jit(solution)/shard_map/ppermute | solution.py:42
  554.9 112.1 %collective-permute-start.29 = (bf16[512,2048]{1,0:T(8,128)(2,1)}, bf16[512,2048]{1,0:T(8,128)(2,1)}, u32[]{:S(2)}, u32[]{:S(2)}) collective-permute-start(bf16[512,2048]{1,0:T(8,128)(2,1)} %collective-permute-done.9.refs_4_), channel_id=1, source_target_pairs={{0,1},{1,0},{2,3},{3,2},{4,5},{5,4},{6,7},{7,6},{8,9},{9,8},{10,11... | collective-permute-start | bytes 6291464 | tf_op jit(solution)/shard_map/ppermute | solution.py:42
  555.0 113.9 %collective-permute-start.30 = (bf16[512,2048]{1,0:T(8,128)(2,1)S(1)}, bf16[512,2048]{1,0:T(8,128)(2,1)}, u32[]{:S(2)}, u32[]{:S(2)}) collective-permute-start(bf16[512,2048]{1,0:T(8,128)(2,1)S(1)} %collective-permute-done.15.refs_5_), channel_id=1, source_target_pairs={{0,1},{1,0},{2,3},{3,2},{4,5},{5,4},{6,7},{7,6},{8,9},{9,8},{10,11... | collective-permute-start | bytes 6291464 | tf_op jit(solution)/shard_map/ppermute | solution.py:42
  610.6 68.0 %collective-permute-start.31 = (bf16[1024,1024]{1,0:T(8,128)(2,1)}, bf16[1024,1024]{1,0:T(8,128)(2,1)}, u32[]{:S(2)}, u32[]{:S(2)}) collective-permute-start(bf16[1024,1024]{1,0:T(8,128)(2,1)} %add_convert_fusion.7), channel_id=1, source_target_pairs={{4,8},{8,4},{5,9},{9,5},{6,10},{10,6},{7,11},{11,7},{20,24},{24,20... | collective-permute-start | bytes 6291464 | tf_op jit(solution)/shard_map/ppermute | solution.py:976
  615.3 68.0 %collective-permute-start.32 = (bf16[1024,1024]{1,0:T(8,128)(2,1)}, bf16[1024,1024]{1,0:T(8,128)(2,1)}, u32[]{:S(2)}, u32[]{:S(2)}) collective-permute-start(bf16[1024,1024]{1,0:T(8,128)(2,1)} %reduce-scatter.8.cloned.1.call-done), channel_id=1, source_target_pairs={{0,4},{12,8},{1,5},{13,9},{2,6},{14,10},{3,7},{15,11},{16,20},{28,... | collective-permute-start | bytes 6291464 | tf_op jit(solution)/shard_map/ppermute | solution.py:972
  639.5 59.6 %all-to-all-start.7 = ((bf16[4,3,512,128]{3,2,1,0:T(8,128)(2,1)}), bf16[4,3,512,128]{3,2,1,0:T(8,128)(2,1)}, u32[]{:S(2)}, u32[]{:S(2)}) async-start(bf16[4,3,512,128]{3,2,1,0:T(8,128)(2,1)} %attend_back.2.refs_0_), calls=%async_computation.8 | async-start | bytes 3145728 | tf_op jit(solution)/shard_map/all_to_all | solution.py:788
  685.9 51.4 %collective-permute-start.38 = (bf16[1024,1024]{1,0:T(8,128)(2,1)S(1)}, bf16[1024,1024]{1,0:T(8,128)(2,1)}, u32[]{:S(2)}, u32[]{:S(2)}) collective-permute-start(bf16[1024,1024]{1,0:T(8,128)(2,1)S(1)} %add_convert_fusion.5), channel_id=1, source_target_pairs={{4,8},{8,4},{5,9},{9,5},{6,10},{10,6},{7,11},{11,7},{20,24},{24,20... | collective-permute-start | bytes 6291464 | tf_op jit(solution)/shard_map/ppermute | solution.py:976
  689.7 110.6 %collective-permute-start.55 = (bf16[1024,1024]{1,0:T(8,128)(2,1)}, bf16[1024,1024]{1,0:T(8,128)(2,1)}, u32[]{:S(2)}, u32[]{:S(2)}) collective-permute-start(bf16[1024,1024]{1,0:T(8,128)(2,1)} %add_convert_fusion.6), channel_id=1, source_target_pairs={{4,0},{8,12},{5,1},{9,13},{6,2},{10,14},{7,3},{11,15},{20,16},{24,... | collective-permute-start | bytes 6291464 | tf_op jit(solution)/shard_map/ppermute | solution.py:980
  691.1 52.4 %collective-permute-start.39 = (bf16[1024,1024]{1,0:T(8,128)(2,1)}, bf16[1024,1024]{1,0:T(8,128)(2,1)}, u32[]{:S(2)}, u32[]{:S(2)}) collective-permute-start(bf16[1024,1024]{1,0:T(8,128)(2,1)} %reduce-scatter.10.cloned.1.call-done), channel_id=1, source_target_pairs={{0,4},{12,8},{1,5},{13,9},{2,6},{14,10},{3,7},{15,11},{16,20},{28,... | collective-permute-start | bytes 6291464 | tf_op jit(solution)/shard_map/ppermute | solution.py:972
  699.1 81.1 %all-to-all-start.9 = ((bf16[4,3,512,128]{3,2,1,0:T(8,128)(2,1)}), bf16[4,3,512,128]{3,2,1,0:T(8,128)(2,1)}, u32[]{:S(2)}, u32[]{:S(2)}) async-start(bf16[4,3,512,128]{3,2,1,0:T(8,128)(2,1)} %attend_back.3.refs_1_), calls=%async_computation.11 | async-start | bytes 3145728 | tf_op jit(solution)/shard_map/all_to_all | solution.py:788
  703.5 184.1 %reduce-scatter.14.cloned.1.call-start = ((), (), s32[]{:S(2)}) async-start(), calls=%async_computation.22 | async-start | bytes 3145728 | tf_op jit(solution)/shard_map/reduce_scatter | solution.py:967
  718.3 61.8 %collective-permute-start.40 = (f32[14336]{0:T(1024)S(1)}, f32[14336]{0:T(1024)S(1)}, u32[]{:S(2)}, u32[]{:S(2)}) collective-permute-start(f32[14336]{0:T(1024)S(1)} %add.142), channel_id=1, source_target_pairs={{0,8},{8,0},{4,12},{12,4},{1,9},{9,1},{5,13},{13,5},{2,10},{10,2},... | collective-permute-start | bytes 172040 | tf_op jit(solution)/shard_map/ppermute | solution.py:1035
  735.6 68.1 %collective-permute-start.36 = (bf16[256,2048]{1,0:T(8,128)(2,1)}, bf16[256,2048]{1,0:T(8,128)(2,1)}, u32[]{:S(2)}, u32[]{:S(2)}) collective-permute-start(bf16[256,2048]{1,0:T(8,128)(2,1)} %add_convert_fusion.13), channel_id=1, source_target_pairs={{0,2},{1,3},{2,0},{3,1},{4,6},{5,7},{6,4},{7,5},{8,10},{9,11},{10,... | collective-permute-start | bytes 3145736 | tf_op jit(solution)/shard_map/ppermute | solution.py:47
  741.1 153.6 %collective-permute-start.56 = (bf16[1024,1024]{1,0:T(8,128)(2,1)}, bf16[1024,1024]{1,0:T(8,128)(2,1)}, u32[]{:S(2)}, u32[]{:S(2)}) collective-permute-start(bf16[1024,1024]{1,0:T(8,128)(2,1)} %add_convert_fusion.4), channel_id=1, source_target_pairs={{4,0},{8,12},{5,1},{9,13},{6,2},{10,14},{7,3},{11,15},{20,16},{24,... | collective-permute-start | bytes 6291464 | tf_op jit(solution)/shard_map/ppermute | solution.py:980
  747.3 66.5 %collective-permute-start.45 = (bf16[1024,1024]{1,0:T(8,128)(2,1)}, bf16[1024,1024]{1,0:T(8,128)(2,1)}, u32[]{:S(2)}, u32[]{:S(2)}) collective-permute-start(bf16[1024,1024]{1,0:T(8,128)(2,1)} %add_convert_fusion.3), channel_id=1, source_target_pairs={{4,8},{8,4},{5,9},{9,5},{6,10},{10,6},{7,11},{11,7},{20,24},{24,20... | collective-permute-start | bytes 6291464 | tf_op jit(solution)/shard_map/ppermute | solution.py:976
  782.2 119.2 %all-to-all-start.10 = ((bf16[4,1024,384]{1,2,0:T(8,128)(2,1)}), bf16[4,1024,384]{1,2,0:T(8,128)(2,1)S(1)}, u32[]{:S(2)}, u32[]{:S(2)}) async-start(bf16[4,1024,384]{1,2,0:T(8,128)(2,1)} %broadcast_in_dim.55), calls=%async_computation.13 | async-start | bytes 6291456 | tf_op jit(solution)/shard_map/all_to_all | solution.py:788
  786.0 92.8 %collective-permute-start.46 = (bf16[1024,1024]{1,0:T(8,128)(2,1)}, bf16[1024,1024]{1,0:T(8,128)(2,1)S(1)}, u32[]{:S(2)}, u32[]{:S(2)}) collective-permute-start(bf16[1024,1024]{1,0:T(8,128)(2,1)} %reduce-scatter.12.cloned.1.call-done), channel_id=1, source_target_pairs={{0,4},{12,8},{1,5},{13,9},{2,6},{14,10},{3,7},{15,11},{16,20},{28,... | collective-permute-start | bytes 6291464 | tf_op jit(solution)/shard_map/ppermute | solution.py:972
  810.7 76.9 %collective-permute-start.42 = (bf16[256,2048]{1,0:T(8,128)(2,1)}, bf16[256,2048]{1,0:T(8,128)(2,1)}, u32[]{:S(2)}, u32[]{:S(2)}) collective-permute-start(bf16[256,2048]{1,0:T(8,128)(2,1)} %add_convert_fusion.11), channel_id=1, source_target_pairs={{0,2},{1,3},{2,0},{3,1},{4,6},{5,7},{6,4},{7,5},{8,10},{9,11},{10,... | collective-permute-start | bytes 3145736 | tf_op jit(solution)/shard_map/ppermute | solution.py:47
  812.2 70.9 %collective-permute-start.47 = (f32[1024]{0:T(1024)S(1)}, f32[1024]{0:T(1024)S(1)}, u32[]{:S(2)}, u32[]{:S(2)}) collective-permute-start(f32[1024]{0:T(1024)S(1)} %fusion.16), channel_id=1, source_target_pairs={{0,4},{4,0},{8,12},{12,8},{1,5},{5,1},{9,13},{13,9},{2,6},{6,2},{1... | collective-permute-start | bytes 12296 | tf_op jit(solution)/shard_map/ppermute | solution.py:1031
  818.5 120.4 %collective-permute-start.53 = (bf16[1024,1024]{1,0:T(8,128)(2,1)}, bf16[1024,1024]{1,0:T(8,128)(2,1)}, u32[]{:S(2)}, u32[]{:S(2)}) collective-permute-start(bf16[1024,1024]{1,0:T(8,128)(2,1)} %add_convert_fusion.2), channel_id=1, source_target_pairs={{4,0},{8,12},{5,1},{9,13},{6,2},{10,14},{7,3},{11,15},{20,16},{24,... | collective-permute-start | bytes 6291464 | tf_op jit(solution)/shard_map/ppermute | solution.py:980
  883.1 52.3 %collective-permute-start.50 = (f32[1024]{0:T(1024)S(1)}, f32[1024]{0:T(1024)S(1)}, u32[]{:S(2)}, u32[]{:S(2)}) collective-permute-start(f32[1024]{0:T(1024)S(1)} %add.156), channel_id=1, source_target_pairs={{0,8},{8,0},{4,12},{12,4},{1,9},{9,1},{5,13},{13,5},{2,10},{10,2},... | collective-permute-start | bytes 12296 | tf_op jit(solution)/shard_map/ppermute | solution.py:1035
  917.1 70.1 %collective-permute-start.54 = (bf16[1024,1024]{1,0:T(8,128)(2,1)S(1)}, bf16[1024,1024]{1,0:T(8,128)(2,1)}, u32[]{:S(2)}, u32[]{:S(2)}) collective-permute-start(bf16[1024,1024]{1,0:T(8,128)(2,1)S(1)} %add_convert_fusion), channel_id=1, source_target_pairs={{4,0},{8,12},{5,1},{9,13},{6,2},{10,14},{7,3},{11,15},{20,16},{24,... | collective-permute-start | bytes 6291464 | tf_op jit(solution)/shard_map/ppermute | solution.py:980
  937.6 69.3 %collective-permute-start.52 = (bf16[512,1024]{1,0:T(8,128)(2,1)S(1)}, bf16[512,1024]{1,0:T(8,128)(2,1)S(1)}, u32[]{:S(2)}, u32[]{:S(2)}) collective-permute-start(bf16[512,1024]{1,0:T(8,128)(2,1)S(1)} %add_convert_fusion.8), channel_id=1, source_target_pairs={{4,0},{8,12},{5,1},{9,13},{6,2},{10,14},{7,3},{11,15},{20,16},{24,... | collective-permute-start | bytes 3145736 | tf_op jit(solution)/shard_map/ppermute | solution.py:980
  (103 other events, 1473.9 us)
Sparse Core Ops, SparseCore 0:
  125.4 103.1 all-gather.2
  230.2 103.9 all-gather.4
  433.4 54.2 reduce-scatter.5
  490.6 54.2 reduce-scatter.7
  547.6 54.3 reduce-scatter.9
  604.8 55.5 reduce-scatter.11
  718.4 33.1 reduce-scatter.13

commit v3 on v2

--- a/solution.py
+++ b/solution.py
@@ -84,19 +84,15 @@
 
 
 class Weight:
-    def __init__(self, parts, axis, blocks, rows=None):
-        self.parts, self.axis, self.blocks = parts, axis, blocks
-        self.turned = not isinstance(parts[0], tuple)
-        self.shape = list((parts[0] if self.turned else parts[0][0]).shape[-2:])
+    def __init__(self, parts, axis, blocks, lead=None):
+        self.parts, self.axis, self.blocks, self.lead = parts, axis, blocks, lead
+        self.turned = len(parts) < blocks
+        self.shape = list(parts[0].shape[-2:])
         if self.turned:
             self.shape[axis] //= blocks
-        if rows is not None:
-            self.shape[0] = rows
 
     def arrays(self):
-        if self.turned:
-            return [self.parts[0]] * self.blocks
-        return [array for array, _, _ in self.parts]
+        return [self.parts[b % len(self.parts)] for b in range(self.blocks)]
 
     def specs(self, split_axis, tile):
         shape = list(self.shape)
@@ -104,18 +100,14 @@
         shape[split_axis] = tile
 
         def spec(block):
-            lead, row = (None, 0) if self.turned else self.parts[block][1:]
-
-            def find(*args):
+            def find(i, place_ref):
                 at = [0, 0]
                 if self.turned:
-                    at[self.axis] = lax.rem(args[1][0] + block, self.blocks)
-                else:
-                    at[0] = row
-                at[split_axis] = at[split_axis] * steps + args[0]
-                return tuple(at) if lead is None else (lead, *at)
-
-            return pl.BlockSpec(tuple(shape) if lead is None else (None, *shape), find)
+                    at[self.axis] = lax.rem(place_ref[0] + block, self.blocks)
+                at[split_axis] = at[split_axis] * steps + i
+                return tuple(at) if self.lead is None else (self.lead, *at)
+
+            return pl.BlockSpec(tuple(shape) if self.lead is None else (None, *shape), find)
 
         return [spec(b) for b in range(self.blocks)]
 
@@ -141,40 +133,38 @@
     return pl.BlockSpec(shape, lambda i, p: (0,) * len(shape))
 
 
-def project_kernel(blocks, x_ref, *refs):
-    weights, bias_ref, out = refs[:blocks], *refs[blocks:]
-    depth = x_ref.shape[1] // blocks
-    acc = None
-    for index, weight in enumerate(weights):
-        part = dot(x_ref[:, index * depth : (index + 1) * depth], weight[...], 1, 0)
-        acc = part if acc is None else acc + part
-    low = (acc + bias_ref[...].astype(F32)).astype(BF16)
-    for slot in range(out.shape[0]):
-        out[slot] = low[:, slot * HEAD : (slot + 1) * HEAD]
-
-
-def project(x, weight, bias):
-    tokens, width = x.shape
-    columns = weight.shape[1]
-    heads = columns // HEAD
-    tile = 256
-
-    def whole(block):
-        _, lead, row = weight.parts[block]
-        return pl.BlockSpec((None, *weight.shape), lambda i: (lead, row, 0))
-
+def project_kernel(near, far, *refs):
+    *weights, bias_ref, out = refs
+    half = near.shape[0]
+    depth = near.shape[1] // len(weights)
+    for index, source in enumerate((near, far)):
+        acc = bias_ref[...].astype(F32)
+        for block, weight in enumerate(weights):
+            acc = acc + dot(source[:, block * depth : (block + 1) * depth], weight[...], 1, 0)
+        low = acc.astype(BF16)
+        for kind in range(out.shape[0]):
+            out[kind, index * half : (index + 1) * half, :] = low[:, kind * HEAD : (kind + 1) * HEAD]
+
+
+def project(near, far, rows, weights, bias):
+    tokens, width = near.shape
+    half = tokens // rows
+    columns = bias.shape[1]
+    kinds = columns // HEAD
+    token_spec = pl.BlockSpec((half, width), lambda i: (i, 0))
+    whole = lambda i: (0, 0)
     return pl.pallas_call(
-        functools.partial(project_kernel, weight.blocks),
-        grid=(tokens // tile,),
-        in_specs=[pl.BlockSpec((tile, width), lambda i: (i, 0))]
-        + [whole(b) for b in range(weight.blocks)]
-        + [pl.BlockSpec((1, columns), lambda i: (0, 0))],
-        out_specs=pl.BlockSpec((heads, tile, HEAD), lambda i: (0, i, 0)),
-        out_shape=like((heads, tokens, HEAD), BF16),
+        project_kernel,
+        grid=(rows,),
+        in_specs=[token_spec] * 2
+        + [pl.BlockSpec(w.shape, whole) for w in weights]
+        + [pl.BlockSpec((1, columns), whole)],
+        out_specs=pl.BlockSpec((kinds, 2 * half, HEAD), lambda i: (0, i, 0)),
+        out_shape=like((kinds, 2 * tokens, HEAD), BF16),
         compiler_params=params(),
-        cost_estimate=cost(2 * tokens * width * columns, 2 * (tokens * width + width * columns)),
+        cost_estimate=cost(4 * tokens * width * columns, 4 * (tokens * width + width * columns)),
         name="project",
-    )(x, *weight.arrays(), bias)
+    )(near, far, *weights, bias)
 
 
 def up_kernel(blocks, place_ref, near, far, *refs):
@@ -467,14 +457,22 @@
     )(place, *values)
 
 
-def gather_blocks(scratch, source, transposed=False):
+def gather_blocks(scratch, source):
     count, size, _ = source.shape
     for index in range(count):
-        rows = slice(index * size, (index + 1) * size)
-        if transposed:
-            scratch[:, rows] = source[index].T
-        else:
-            scratch[rows, :] = source[index]
+        scratch[index * size : (index + 1) * size, :] = source[index]
+
+
+def gather_kinds(place_ref, sources, scratches, turned=None):
+    count = len(sources)
+    for step, source in enumerate(sources):
+        size = source.shape[1]
+        start = lax.rem(place_ref[0] + count - step, count) * size
+        rows = pl.ds(pl.multiple_of(start, size), size)
+        for kind, scratch in enumerate(scratches):
+            scratch[rows, :] = source[kind]
+        if turned is not None:
+            turned[:, rows] = source[1].T
 
 
 def put_rows(out, at, query_block, value, lead=()):
@@ -484,17 +482,15 @@
         out[(at * per + slot, *lead)] = value[slot * size : (slot + 1) * size]
 
 
-def attend_kernel(query_block, key_block, live, *refs):
-    q_in, k_in, v_in, seg_row, seg_col, out, mixed_ref, total_ref = refs[:8]
-    qs, ks, vs, scores, top, total, mixed = refs[8:]
+def attend_kernel(parts, query_block, key_block, live, place_ref, *refs):
+    seg_row, seg_col, out, mixed_ref, total_ref = refs[parts : parts + 5]
+    qs, ks, vs, scores, top, total, mixed = refs[parts + 5 :]
     at = pl.program_id(0)
     count = qs.shape[0] // key_block
 
     @pl.when(at == 0)
     def _():
-        gather_blocks(qs, q_in)
-        gather_blocks(ks, k_in)
-        gather_blocks(vs, v_in)
+        gather_kinds(place_ref, refs[:parts], (qs, ks, vs))
 
     here = pl.ds(pl.multiple_of(at * query_block, query_block), query_block)
     query = qs[here, :]
@@ -534,27 +530,25 @@
     put_rows(out, at, query_block, result.T.astype(BF16))
 
 
-def attend(row, queries, keys, values, seg_row, seg_col, live):
-    parts = queries.shape[0]
+def attend(row, place, heads, seg_row, seg_col, live):
+    parts = len(heads)
     length = seg_row.shape[2]
     size = length // parts
     query_block, key_block = length // live.shape[1], length // live.shape[2]
-    part_spec = pl.BlockSpec((parts, size, HEAD), lambda i, s: (0, row, 0))
-    whole = lambda i, s: (0, 0)
+    part_spec = pl.BlockSpec((3, size, HEAD), lambda i, s, p: (0, row, 0))
+    whole = lambda i, s, p: (0, 0)
     return pl.pallas_call(
-        functools.partial(attend_kernel, query_block, key_block),
+        functools.partial(attend_kernel, parts, query_block, key_block),
         grid_spec=pltpu.PrefetchScalarGridSpec(
-            num_scalar_prefetch=1,
+            num_scalar_prefetch=2,
             grid=(length // query_block,),
-            in_specs=[
-                part_spec,
-                part_spec,
-                part_spec,
-                pl.BlockSpec((None, 1, length), lambda i, s: (row, 0, 0)),
-                pl.BlockSpec((None, length, HEAD), lambda i, s: (row, 0, 0)),
+            in_specs=[part_spec] * parts
+            + [
+                pl.BlockSpec((None, 1, length), lambda i, s, p: (row, 0, 0)),
+                pl.BlockSpec((None, length, HEAD), lambda i, s, p: (row, 0, 0)),
             ],
             out_specs=[
-                pl.BlockSpec((parts, size, HEAD), lambda i, s: (0, 0, 0)),
+                pl.BlockSpec((parts, size, HEAD), lambda i, s, p: (0, 0, 0)),
                 pl.BlockSpec((HEAD, length), whole),
                 pl.BlockSpec((1, length), whole),
             ],
@@ -574,22 +568,19 @@
         compiler_params=params(),
         cost_estimate=cost(4 * length * length * HEAD, 8 * length * HEAD, length * length // 2),
         name="attend",
-    )(live[row], queries, keys, values, seg_row, seg_col)
-
-
-def attend_back_kernel(query_block, key_block, live, *refs):
-    q_in, k_in, v_in, g_in, seg_row, seg_col, mixed_ref, total_ref, out = refs[:9]
-    qs, ks, vs, gs, kt, d_keys, d_values, d_query = refs[9:]
+    )(live[row], place, *heads, seg_row, seg_col)
+
+
+def attend_back_kernel(parts, query_block, key_block, live, place_ref, *refs):
+    g_in, seg_row, seg_col, mixed_ref, total_ref, out = refs[parts : parts + 6]
+    qs, ks, vs, gs, kt, d_keys, d_values, d_query = refs[parts + 6 :]
     at = pl.program_id(0)
     count = qs.shape[0] // key_block
 
     @pl.when(at == 0)
     def _():
-        gather_blocks(qs, q_in)
-        gather_blocks(ks, k_in)
-        gather_blocks(vs, v_in)
+        gather_kinds(place_ref, refs[:parts], (qs, ks, vs), kt)
         gather_blocks(gs, g_in)
-        gather_blocks(kt, k_in, True)
         d_keys[...] = jnp.zeros_like(d_keys)
         d_values[...] = jnp.zeros_like(d_values)
 
@@ -630,29 +621,27 @@
             out[slot, 2] = d_values[rows, :].astype(BF16)
 
 
-def attend_back(row, queries, keys, values, grads, seg_row, seg_col, live, mixed, totals):
-    parts = queries.shape[0]
+def attend_back(row, place, heads, grads, seg_row, seg_col, live, mixed, totals):
+    parts = len(heads)
     length = seg_row.shape[2]
     size = length // parts
     query_block, key_block = length // live.shape[1], length // live.shape[2]
-    part_spec = pl.BlockSpec((parts, size, HEAD), lambda i, s: (0, row, 0))
-    whole = lambda i, s: (0, 0)
+    part_spec = pl.BlockSpec((3, size, HEAD), lambda i, s, p: (0, row, 0))
+    whole = lambda i, s, p: (0, 0)
     return pl.pallas_call(
-        functools.partial(attend_back_kernel, query_block, key_block),
+        functools.partial(attend_back_kernel, parts, query_block, key_block),
         grid_spec=pltpu.PrefetchScalarGridSpec(
-            num_scalar_prefetch=1,
+            num_scalar_prefetch=2,
             grid=(length // query_block,),
-            in_specs=[
-                part_spec,
-                part_spec,
-                part_spec,
-                pl.BlockSpec((parts, size, HEAD), lambda i, s: (0, 0, 0)),
-                pl.BlockSpec((None, 1, length), lambda i, s: (row, 0, 0)),
-                pl.BlockSpec((None, length, HEAD), lambda i, s: (row, 0, 0)),
+            in_specs=[part_spec] * parts
+            + [
+                pl.BlockSpec((parts, size, HEAD), lambda i, s, p: (0, 0, 0)),
+                pl.BlockSpec((None, 1, length), lambda i, s, p: (row, 0, 0)),
+                pl.BlockSpec((None, length, HEAD), lambda i, s, p: (row, 0, 0)),
                 pl.BlockSpec((HEAD, length), whole),
                 pl.BlockSpec((1, length), whole),
             ],
-            out_specs=pl.BlockSpec((parts, 3, size, HEAD), lambda i, s: (0, 0, 0, 0)),
+            out_specs=pl.BlockSpec((parts, 3, size, HEAD), lambda i, s, p: (0, 0, 0, 0)),
             scratch_shapes=[pltpu.VMEM((length, HEAD), BF16)] * 4
             + [pltpu.VMEM((HEAD, length), BF16)]
             + [pltpu.VMEM((length, HEAD), F32)] * 2
@@ -662,7 +651,7 @@
         compiler_params=params(),
         cost_estimate=cost(10 * length * length * HEAD, 16 * length * HEAD, length * length // 2),
         name="attend_back",
-    )(live[row], queries, keys, values, grads, seg_row, seg_col, mixed, totals)
+    )(live[row], place, *heads, grads, seg_row, seg_col, mixed, totals)
 
 
 def normalize(hidden):
@@ -765,7 +754,7 @@
     rows, local_len, width = layer_input.shape
     fsdp, ctx = lax.axis_size("fsdp"), lax.axis_size("ctx")
     y, place = lax.axis_index("fsdp"), lax.axis_index("ctx")
-    core = lax.axis_index("tp") % 2
+    core, chip = lax.axis_index("tp") % 2, lax.axis_index("tp") // 2
     columns = qkv_weight.shape[2]
     hidden_units = up_weight.shape[1]
     heads = columns // HEAD
@@ -796,6 +785,8 @@
     seg_own = rotate(segment_ids, 1, core, 2)
     seg = from_all(seg_own).transpose(1, 0, 2).reshape(rows, ctx * local_len)
 
+    first_token = core * half + chip * (half // 2)
+    quarter = features(lax.dynamic_slice_in_dim(layer_input, first_token, half // 2, axis=1))
     x_rows = features(rotate(layer_input, 1, core, 2))
     x = x_rows.reshape(rows * local_len, width)
 
@@ -806,39 +797,51 @@
         lax.dynamic_slice_in_dim(out_grad, core * half, half, axis=1)
     ).reshape(rows * half, width)
 
-    zero_bias = jnp.zeros_like(qv_bias[:1])
-    biases = qv_bias[:1], zero_bias, qv_bias[1:]
-    pair = spread(jnp.stack([qkv_weight[:, 0], qkv_weight[:, 1]]))
-    cuts = share // columns
-    pieces = [out_weight[:, i * columns : (i + 1) * columns] for i in range(cuts)]
-    rest = jnp.concatenate([qkv_weight[:, 2], *pieces], axis=0)
-    rest, seg, *pair[1:] = lax.optimization_barrier((rest, seg, *pair[1:]))
-    rest = [v[None] for v in spread(after(rest, x))]
-    joint_matrices = [
-        Weight([(v, 0, 0) for v in pair], 0, fsdp),
-        Weight([(v, 1, 0) for v in pair], 0, fsdp),
-        Weight([(v, 0, 0) for v in rest], 0, fsdp, share),
-    ]
-    if cuts:
-        out_parts = [(v, 0, cuts + i) for v in rest for i in range(cuts)]
-        out_full = Weight(out_parts, 1, fsdp * cuts, columns)
-    else:
-        out_full = Weight([(v, None, 0) for v in spread(after(out_weight, rest[1]))], 1, fsdp)
-    query_pieces = project(x, joint_matrices[0], biases[0])
-    queries = swap_ctx(query_pieces)
-    key_pieces = project(after(x, query_pieces), joint_matrices[1], biases[1])
-    keys = swap_ctx(after(key_pieces, queries))
-    gate = [*rest[1:], keys]
+    fsdp_place = y.astype(jnp.int32)[None]
+    ctx_place = place.astype(jnp.int32)[None]
+
+    mine = lax.dynamic_slice_in_dim(qkv_weight, place * HEAD, HEAD, axis=2)
+    head_weight = spread(mine.reshape(share, 3 * HEAD))
+    bias_pair = lax.dynamic_slice_in_dim(qv_bias, place * HEAD, HEAD, axis=1)
+    head_bias = jnp.concatenate(
+        [bias_pair[:1], jnp.zeros_like(bias_pair[:1]), bias_pair[1:]], axis=1
+    )
+
+    def joined(quarter, other):
+        parts = jnp.stack([quarter, other], axis=1).reshape(rows, half, width)
+        return rotate(parts, 1, chip, 2).reshape(rows * half, width)
+
+    def flat(value):
+        return value.reshape(rows * half, width)
+
+    x_near, x_far = [flat(x_rows[:, :half])], [flat(x_rows[:, half:])]
+    quarter, seg = lax.optimization_barrier((quarter, seg))
+    first_quarter = shift(quarter, "ctx", 1)
+    heads_all = [project(x_near[0], x_far[0], rows, head_weight, head_bias)]
+    second_quarter = shift(first_quarter, "ctx", 1)
+    x_near.append(joined(first_quarter, chip_swap(first_quarter)))
+    x_far.append(core_swap(x_near[1]))
+    third_quarter = shift(after(second_quarter, x_near[1]), "ctx", 1)
+    heads_all.append(project(x_near[1], x_far[1], rows, head_weight, head_bias))
+    x_near.append(joined(second_quarter, chip_swap(second_quarter)))
+    x_far.append(core_swap(x_near[2]))
+    heads_all.append(project(x_near[2], x_far[2], rows, head_weight, head_bias))
+    third_other = chip_swap(after(third_quarter, heads_all[0], x_near[2]))
+    third_quarter = after(third_quarter, heads_all[1], heads_all[2])
+    x_near.append(joined(third_quarter, third_other))
+    x_far.append(core_swap(x_near[3]))
+    heads_all.append(order.done(project(x_near[3], x_far[3], rows, head_weight, head_bias)))
+
+    gate = [*head_weight[1:], first_quarter]
 
     def whole(block, axis):
-        full = lax.all_gather(after(block, *gate), "fsdp", axis=axis, tiled=True)
-        return Weight([full], axis, fsdp)
-
-    up_full = whole(up_weight, 0)
-    down_full = whole(down_weight, 1)
-    pieces = order.done(project(after(x, key_pieces), joint_matrices[2], biases[2]))
-    values = swap_ctx(after(pieces, keys))
-    fsdp_place = y.astype(jnp.int32)[None]
+        return lax.all_gather(after(block, *gate), "fsdp", axis=axis, tiled=True)
+
+    out_full = Weight([whole(out_weight, 1)], 1, fsdp)
+    up_full = Weight([whole(up_weight, 0)], 0, fsdp)
+    down_full = Weight([whole(down_weight, 1)], 1, fsdp)
+    joint_full = whole(jnp.stack([qkv_weight[:, j] for j in range(3)]), 1)
+    joint_matrices = [Weight([joint_full], 0, fsdp, j) for j in range(3)]
 
     length = ctx * local_len
     seg_row = seg[:, None, :]
@@ -858,14 +861,14 @@
     attended, kept = [], []
     for r in each:
         pieces, mixed, totals = attend(
-            r, order.ready(queries), keys, values, seg_row, seg_col, live
+            r, ctx_place, [order.ready(heads_all[0]), *heads_all[1:]], seg_row, seg_col, live
         )
         order.done(totals)
         kept.append((mixed, totals))
         attended.append(swap_ctx(pieces))
 
     def begin(left, weights, transposed, tile):
-        sent, mine, *rest = terms(fsdp_place, order.ready(left), weights, transposed, tile)
+        sent, mine, *rest = terms(order.ready(fsdp_place), left, weights, transposed, tile)
         order.done(sent)
         return core_swap(sent), mine, *rest
 
@@ -877,9 +880,6 @@
     attended_last = attended[-1]
     attended = [parts[r][2] for r in each]
     totals = [middle(*parts[r][:2]) for r in each]
-
-    x_near = [after(x_rows[:, :half].reshape(rows * half, width), attended_last)]
-    x_near.append(shift(x_near[0], "ctx", 1))
 
     normal_one, inverse_one, norm_low = [], [], []
     for r in each:
@@ -899,15 +899,11 @@
     act_low, slopes = [], []
     for r in each:
         near, far = norm_low[r]
-        if r == 0:
-            x_near.append(shift(order.ready(x_near[1]), "ctx", 1))
         act, slope = up_project(fsdp_place, order.ready(near), far, up_full, up_bias[None])
         order.done(act)
         act_low.append(act)
         slopes.append(slope)
 
-    order.pin(x_near[2])
-    x_near.append(shift(x_near[2], "ctx", 1))
     parts = [begin(act_low[r], [down_full], False, 512) for r in each]
     totals = [middle(*parts[r]) for r in each]
 
@@ -1010,9 +1006,9 @@
 
     def attend_step(r):
         mixed, row_totals = kept[r]
-        grads = order.ready(head_grads[r])
+        place_now = order.ready(ctx_place)
         pieces = attend_back(
-            r, queries, keys, values, grads, seg_row, seg_col, live, mixed, row_totals
+            r, place_now, heads_all, head_grads[r], seg_row, seg_col, live, mixed, row_totals
         )
         joint_back.append(order.done(pieces))
         joint_rows.append(swap_ctx(pieces))
@@ -1020,14 +1016,13 @@
     lined = {}
 
     def line_start(name, piece):
-        lined[name, piece] = line_one(order.ready(gradients[name, piece]))
+        lined[name, piece] = line_one(gradients[name, piece])
 
     def line_step(step, name, piece):
         lined[name, piece] = step(*lined[name, piece])
 
     def small_start(value):
         value = value + shift(value, "fsdp", 1) if fsdp == 2 else lax.psum(value, "fsdp")
-        value = order.done(value)
         return value, lax.ppermute(value, "ctx", [(0, 1), (1, 0), (2, 3), (3, 2)])
 
     def small_step(value, other):
@@ -1040,7 +1035,7 @@
     norm_two(0)
     act_step(0)
     up_step(0)
-    order.pin(x_near[3])
+    order.pin(joint_full)
     norm_two(1)
     up_totals = [middle(*up_parts[0])]
     down_args = (pairs_of(act_low, mlp_low), (hidden_units, width), False)
@@ -1052,23 +1047,28 @@
     up_args = (pairs_of(norm_low, pre_low), (width, hidden_units), True)
     norm_back(0)
     give("up", *up_args, 0, 2)
+    order.pin(gradients["down", 0])
     head_step(0)
     line_start("down", 0)
+    order.pin(head_grads[0])
+    line_step(line_two, "down", 0)
     norm_back(1)
+    order.pin(gradients["down", 1])
     give("up", *up_args, 1, 2)
+    line_start("down", 1)
     head_step(1)
     out_args = (pairs_of(attended, attn_low), (columns, width), False)
     give("out", *out_args, 0, 1)
     wide = features_back(jnp.concatenate([sum(sums_two), sum(sums_one)], axis=0))
     wide = wide + core_swap(wide)
-    line_step(line_two, "down", 0)
-    line_start("down", 1)
     attend_step(0)
     wide_small = small_start(jnp.concatenate([wide.reshape(-1), sum(up_sums).reshape(-1)]))
+    order.pin(gradients["up", 0])
+    line_step(line_three, "down", 0)
+    line_step(line_two, "down", 1)
+    line_start("up", 0)
     attend_step(1)
 
-    x_far = [x_rows[:, half:].reshape(rows * half, width)] + [core_swap(v) for v in x_near[1:]]
-    ctx_place = place.astype(jnp.int32)[None]
     arrived = None
     for by in range(1, fsdp):
         sent = joint_grad_terms(
@@ -1077,19 +1077,22 @@
         got = shift(order.done(sent), "fsdp", by)
         arrived = got if arrived is None else (arrived.astype(F32) + got.astype(F32))
 
-    line_step(line_three, "down", 0)
-    line_step(line_two, "down", 1)
-    line_start("up", 0)
+    order.pin(gradients["up", 1])
+    line_step(line_three, "down", 1)
+    line_step(line_two, "up", 0)
+    line_start("up", 1)
     wide_small = small_step(*wide_small)
+    order.pin(arrived)
     in_parts = [begin(joint_rows[0], joint_matrices, True, 512)]
     mine = joint_grad_terms(
         ctx_place, [order.ready(x_near[0])] + x_near[1:], x_far, joint_back, (0, share), add=arrived
     )
     order.done(mine)
     in_totals = [middle(*in_parts[0][:2])]
-    line_step(line_three, "down", 1)
-    line_step(line_two, "up", 0)
-    line_start("up", 1)
+    order.pin(gradients["out", 0])
+    line_step(line_three, "up", 0)
+    line_step(line_two, "up", 1)
+    line_start("out", 0)
     wide_small = small_end(*wide_small)
     in_parts.append(begin(joint_rows[1], joint_matrices, True, 512))
     joint_all = from_all(mine)
@@ -1098,14 +1101,11 @@
     late_small = small_start(
         jnp.concatenate([bias_sums[0, :columns], bias_sums[0, 2 * columns :]])
     )
-    line_step(line_three, "up", 0)
-    line_step(line_two, "up", 1)
-    line_start("out", 0)
-    late_small = small_step(*late_small)
     line_step(line_three, "up", 1)
     line_step(line_two, "out", 0)
+    late_small = small_step(*late_small)
+    line_step(line_three, "out", 0)
     late_small = small_end(*late_small)
-    line_step(line_three, "out", 0)
 
     input_low = []
     for r in each:

time: 1030 us -> 965 us (0.937)
  waiting for transfers between devices: 447 us -> 352 us
  starting transfers between devices: 124 us -> 144 us
    ppermute x2, waiting for transfers between devices: 0.01 us -> 61.3 us  [small_start(): return (value, lax.ppermute(value, 'ctx', [(0, 1), (1, 0), (2, 3), (3, 2)]))]
    ppermute x5, waiting for transfers between devices: 60 us -> 4.07 us  [line_one(): return (value, lax.ppermute(value, 'ctx', [(0, 1), (3, 2)]))]
    ppermute x8 -> x7, waiting for transfers between devices: 74.4 us -> 40.9 us  [shift(): lax.ppermute(value, axis, [(i, (i + by) % size) for i in range(size)])]
    ppermute x2, waiting for transfers between devices: 37.5 us -> 9.98 us  [small_step(): return (value, lax.ppermute(value, 'ctx', [(0, 2), (2, 0), (1, 3), (3, 1)]))]
    all_to_all x11 -> x8, waiting for transfers between devices: 95.1 us -> 72.1 us  [swap_ctx(): return lax.all_to_all(value, 'ctx', 0, 0, tiled=True)]
    ppermute x5, waiting for transfers between devices: 59.9 us -> 39.9 us  [line_three(): return (total, lax.ppermute(total, 'ctx', [(1, 0), (2, 3)]))]
    ppermute x2, starting transfers between devices: 7.32 us -> 25.6 us  [small_step(): return (value, lax.ppermute(value, 'ctx', [(0, 2), (2, 0), (1, 3), (3, 1)]))]
    select_n x8 -> x12, other arithmetic: 14.9 us -> 22.5 us  [rotate(): return jnp.where(by == 0, value, swapped)]
  transfers between devices with their start and end apart: 75 -> 76, of which waited for: 32 -> 30; matrix products, arithmetic and copies ran while one was open for 12% -> 14% of each run, Pallas kernels for 26% -> 30%
where the time goes in v3:
time: 965 us; the launch traced here: 958 us
  waiting for transfers between devices  352 us (36%)
  Pallas kernels  292 us (30%)
  starting transfers between devices  144 us (15%)
  other arithmetic  110 us (11%)
  local copies, waits for them, and re-layouts  45.2 us (5%)
  between operations  15.4 us (2%)
    pallas_call x14, Pallas kernels, grid_call(): pl.pallas_call(kernel, grid_spec=pltpu.PrefetchScalarGridSpec(num_scalar_...  116 us
    ppermute x11, waiting for transfers between devices, chip_swap(): return lax.ppermute(value, 'tp', [(i, i ^ 2) for i in range(size)])  105 us
    all_to_all x8, waiting for transfers between devices, swap_ctx(): return lax.all_to_all(value, 'ctx', 0, 0, tiled=True)  72.1 us
    ppermute x2, waiting for transfers between devices, small_start(): return (value, lax.ppermute(value, 'ctx', [(0, 1), (1, 0), (2, 3), (3, 2)]))  61.3 us
    all_to_all x8, starting transfers between devices, swap_ctx(): return lax.all_to_all(value, 'ctx', 0, 0, tiled=True)  45.6 us
    pallas_call x5, Pallas kernels, weight_grad(): pl.pallas_call(functools.partial(grad_kernel, len(pairs)), grid_spec=pltp...  41.4 us
    ppermute x7, waiting for transfers between devices, shift(): lax.ppermute(value, axis, [(i, (i + by) % size) for i in range(size)])  40.9 us
    ppermute x5, waiting for transfers between devices, line_three(): return (total, lax.ppermute(total, 'ctx', [(1, 0), (2, 3)]))  39.9 us
  transfers between devices with their start and end apart: 76, of which 30 were waited for; matrix products, arithmetic and copies ran while one was open for 14% of the time, Pallas kernels for 30%

profile of v3, /device:TPU:0, one launch (start us, length us, event | category | flops | bytes accessed | tf_op | source)
XLA Modules:
  0.0 958.0 jit_solution(13339569486832913487)
XLA Ops:
  24.6 16.1 %collective-permute-done.refs_1_ = bf16[1024,384]{1,0:T(8,128)(2,1)S(1)} collective-permute-done((bf16[1024,384]{1,0:T(8,128)(2,1)S(1)}, bf16[1024,384]{1,0:T(8,128)(2,1)S(1)}, u32[]{:S(2)}, u32[]{:S(2)}) %collective-permute-start) | collective-permute-done | bytes 786464 | tf_op jit(solution)/shard_map/ppermute | solution.py:52
  55.0 16.4 %collective-permute-done.2 = bf16[2,128,2048]{2,1,0:T(8,128)(2,1)S(1)} collective-permute-done((bf16[2,128,2048]{2,1,0:T(8,128)(2,1)}, bf16[2,128,2048]{2,1,0:T(8,128)(2,1)S(1)}, u32[]{:S(2)}, u32[]{:S(2)}) %collective-permute-start.2) | collective-permute-done | bytes 1048608 | tf_op jit(solution)/shard_map/ppermute | solution.py:52
  76.7 16.2 %collective-permute-done.6 = bf16[2,128,2048]{2,1,0:T(8,128)(2,1)S(1)} collective-permute-done((bf16[2,128,2048]{2,1,0:T(8,128)(2,1)S(1)}, bf16[2,128,2048]{2,1,0:T(8,128)(2,1)S(1)}, u32[]{:S(2)}, u32[]{:S(2)}) %collective-permute-start.6) | collective-permute-done | bytes 1048608 | tf_op jit(solution)/shard_map/ppermute | solution.py:47
  120.3 10.1 %collective-permute-done.8 = bf16[2,128,2048]{2,1,0:T(8,128)(2,1)S(1)} collective-permute-done((bf16[2,128,2048]{2,1,0:T(8,128)(2,1)}, bf16[2,128,2048]{2,1,0:T(8,128)(2,1)S(1)}, u32[]{:S(2)}, u32[]{:S(2)}) %collective-permute-start.8) | collective-permute-done | bytes 1048608 | tf_op jit(solution)/shard_map/ppermute | solution.py:47
  145.0 11.9 %attend.2 = (bf16[4,512,128]{2,1,0:T(8,128)(2,1)}, f32[128,2048]{1,0:T(8,128)}, f32[1,2048]{1,0:T(1,128)}) custom-call(s32[2,4]{1,0:T(2,128)} %get-tuple-element.292.live, s32[1]{0:T(128)} %bitcast.4.place_ref, bf16[3,1024,128]{2,1,0:T(8,128)(2,1)} %project.4.refs_0_, bf16[3,1024,128]{2,1,0:T(8,128)(2,1)} %project.5.refs_1_, ...), custom_call_target="tpu_custom_call" | custom-call | flops 8388608 | bytes 8192 | tf_op jit(solution)/shard_map/attend/pallas_call | solution.py:540
  156.8 15.2 %all-to-all-start.1 = ((bf16[4,512,128]{2,1,0:T(8,128)(2,1)}), bf16[4,512,128]{2,1,0:T(8,128)(2,1)S(1)}, u32[]{:S(2)}, u32[]{:S(2)}) async-start(bf16[4,512,128]{2,1,0:T(8,128)(2,1)} %get-tuple-element.140), calls=%async_computation.1 | async-start | bytes 1048576 | tf_op jit(solution)/shard_map/all_to_all | solution.py:777
  172.0 11.9 %attend.3 = (bf16[4,512,128]{2,1,0:T(8,128)(2,1)}, f32[128,2048]{1,0:T(8,128)}, f32[1,2048]{1,0:T(1,128)}) custom-call(s32[2,4]{1,0:T(2,128)} %get-tuple-element.293.live, s32[1]{0:T(128)} %bitcast.4.place_ref, bf16[3,1024,128]{2,1,0:T(8,128)(2,1)} %project.4.refs_0_, bf16[3,1024,128]{2,1,0:T(8,128)(2,1)} %project.5.refs_1_, ...), custom_call_target="tpu_custom_call" | custom-call | flops 8388608 | bytes 8192 | tf_op jit(solution)/shard_map/attend/pallas_call | solution.py:540
  219.0 20.2 %collective-permute-done.12.far = bf16[256,2048]{1,0:T(8,128)(2,1)} collective-permute-done((bf16[256,2048]{1,0:T(8,128)(2,1)S(1)}, bf16[256,2048]{1,0:T(8,128)(2,1)}, u32[]{:S(2)}, u32[]{:S(2)}) %collective-permute-start.12) | collective-permute-done | bytes 1048608 | tf_op jit(solution)/shard_map/ppermute | solution.py:47
  244.1 15.8 %collective-permute-done.13.far = bf16[256,2048]{1,0:T(8,128)(2,1)S(1)} collective-permute-done((bf16[256,2048]{1,0:T(8,128)(2,1)S(1)}, bf16[256,2048]{1,0:T(8,128)(2,1)S(1)}, u32[]{:S(2)}, u32[]{:S(2)}) %collective-permute-start.13) | collective-permute-done | bytes 1048608 | tf_op jit(solution)/shard_map/ppermute | solution.py:47
  267.2 10.9 %up_project.2 = (bf16[512,2048]{1,0:T(8,128)(2,1)}, bf16[512,2048]{1,0:T(8,128)(2,1)}) custom-call(s32[1]{0:T(128)} %bitcast.place_ref, bf16[256,2048]{1,0:T(8,128)(2,1)} %get-tuple-element.212.near.refs_0_, bf16[256,2048]{1,0:T(8,128)(2,1)} %copy-done.10, bf16[2048,2048]{1,0:T(8,128)(2,1)} %all-gather.7.cloned.1.call-done.refs_0_.refs_1_, ...), custom_call_target="tpu_custom_call" | custom-call | flops 16777216 | bytes 57344 | tf_op jit(solution)/shard_map/up_project/pallas_call | solution.py:116
  279.1 10.8 %up_project.3 = (bf16[512,2048]{1,0:T(8,128)(2,1)}, bf16[512,2048]{1,0:T(8,128)(2,1)}) custom-call(s32[1]{0:T(128)} %bitcast.place_ref, bf16[256,2048]{1,0:T(8,128)(2,1)} %get-tuple-element.157.near.refs_4_, bf16[256,2048]{1,0:T(8,128)(2,1)} %copy-done.11, bf16[2048,2048]{1,0:T(8,128)(2,1)} %all-gather.7.cloned.1.call-done.refs_0_.refs_1_, ...), custom_call_target="tpu_custom_call" | custom-call | flops 16777216 | bytes 57344 | tf_op jit(solution)/shard_map/up_project/pallas_call | solution.py:116
  301.8 9.9 %terms.11 = (bf16[256,2048]{1,0:T(8,128)(2,1)}, f32[256,2048]{1,0:T(8,128)}) custom-call(s32[1]{0:T(128)} %bitcast.place_ref, bf16[512,2048]{1,0:T(8,128)(2,1)} %get-tuple-element.158.left_ref.refs_4_.refs_6_, bf16[2048,2048]{1,0:T(8,128)(2,1)} %all-gather.9.cloned.1.call-done.refs_0_.refs_1_, bf16[2048,2048]{1,0:T(8,128)(2,1)} %all-gather.9.cloned.1.call-done.refs_0_.refs_1_), custom_call_target="tpu_custom_call" | custom-call | flops 16777216 | bytes 53248 | tf_op jit(solution)/shard_map/terms/pallas_call | solution.py:116
  316.1 21.5 %collective-permute-done.18.far = bf16[256,2048]{1,0:T(8,128)(2,1)S(1)} collective-permute-done((bf16[256,2048]{1,0:T(8,128)(2,1)S(1)}, bf16[256,2048]{1,0:T(8,128)(2,1)S(1)}, u32[]{:S(2)}, u32[]{:S(2)}) %collective-permute-start.18) | collective-permute-done | bytes 1048608 | tf_op jit(solution)/shard_map/ppermute | solution.py:47
  348.8 9.5 act_back.2
  391.3 10.0 %act_back.3 = (bf16[512,2048]{1,0:T(8,128)(2,1)}, f32[1,2048]{1,0:T(1,128)}) custom-call(s32[1]{0:T(128)} %bitcast.place_ref, bf16[256,2048]{1,0:T(8,128)(2,1)} %get-tuple-element.185.refs_5_.near, bf16[256,2048]{1,0:T(8,128)(2,1)} %copy-done.13, bf16[2048,2048]{1,0:T(8,128)(2,1)} %all-gather.9.cloned.1.call-done.refs_0_.refs_1_, ...), custom_call_target="tpu_custom_call" | custom-call | flops 16777216 | bytes 57344 | tf_op jit(solution)/shard_map/act_back/pallas_call | solution.py:116
  423.4 21.4 %collective-permute-done.26.far = bf16[256,2048]{1,0:T(8,128)(2,1)S(1)} collective-permute-done((bf16[256,2048]{1,0:T(8,128)(2,1)S(1)}, bf16[256,2048]{1,0:T(8,128)(2,1)S(1)}, u32[]{:S(2)}, u32[]{:S(2)}) %collective-permute-start.26) | collective-permute-done | bytes 1048608 | tf_op jit(solution)/shard_map/ppermute | solution.py:47
  479.1 39.2 %all-to-all-done.3.refs_4_ = bf16[4,512,128]{2,1,0:T(8,128)(2,1)S(1)} async-done(((bf16[4,512,128]{2,1,0:T(8,128)(2,1)}), bf16[4,512,128]{2,1,0:T(8,128)(2,1)S(1)}, u32[]{:S(2)}, u32[]{:S(2)}) %all-to-all-start.3) | async-done | bytes 524320 | tf_op jit(solution)/shard_map/all_to_all | solution.py:777
  567.4 18.2 %attend_back.2.refs_0_ = bf16[4,3,512,128]{3,2,1,0:T(8,128)(2,1)} custom-call(s32[2,4]{1,0:T(2,128)} %get-tuple-element.292.live, s32[1]{0:T(128)} %bitcast.4.place_ref, bf16[3,1024,128]{2,1,0:T(8,128)(2,1)} %project.4.refs_0_, bf16[3,1024,128]{2,1,0:T(8,128)(2,1)} %project.5.refs_1_, bf16[3,1024,128]{2,1,0:T(8,128)(2,1)} %project.6.refs_2_, ...), custom_call_target="tpu_custom_call" | custom-call | flops 20971520 | bytes 16384 | tf_op jit(solution)/shard_map/attend_back/pallas_call | solution.py:631
  618.0 17.7 %attend_back.3.refs_1_ = bf16[4,3,512,128]{3,2,1,0:T(8,128)(2,1)} custom-call(s32[2,4]{1,0:T(2,128)} %get-tuple-element.293.live, s32[1]{0:T(128)} %bitcast.4.place_ref, bf16[3,1024,128]{2,1,0:T(8,128)(2,1)} %project.4.refs_0_, bf16[3,1024,128]{2,1,0:T(8,128)(2,1)} %project.5.refs_1_, bf16[3,1024,128]{2,1,0:T(8,128)(2,1)} %project.6.refs_2_, ...), custom_call_target="tpu_custom_call" | custom-call | flops 20971520 | bytes 16384 | tf_op jit(solution)/shard_map/attend_back/pallas_call | solution.py:631
  635.6 9.7 %joint_grad.2 = bf16[1024,384]{1,0:T(8,128)(2,1)} custom-call(s32[1]{0:T(128)} %bitcast.4.place_ref, bf16[4,3,512,128]{3,2,1,0:T(8,128)(2,1)} %attend_back.2.refs_0_, bf16[4,3,512,128]{3,2,1,0:T(8,128)(2,1)} %attend_back.3.refs_1_, bf16[512,2048]{1,0:T(8,128)(2,1)} %bitcast.68, bf16[512,2048]{1,0:T(8,128)(2,1)} %bitcast.54, bf16[512,2048]{1,0:T(8,128)(2,1)} %bitcast.58, ...), custom_call_target="tpu_custom_call" | custom-call | flops 12582912 | bytes 45056 | tf_op jit(solution)/shard_map/joint_grad/pallas_call | solution.py:442
  661.7 15.7 %collective-permute-done.37 = f32[14336]{0:T(1024)S(1)} collective-permute-done((f32[14336]{0:T(1024)S(1)}, f32[14336]{0:T(1024)S(1)}, u32[]{:S(2)}, u32[]{:S(2)}) %collective-permute-start.37) | collective-permute-done | bytes 57376 | tf_op jit(solution)/shard_map/ppermute | solution.py:1026
  688.9 9.3 terms.14
  710.3 10.3 %joint_grad.3 = bf16[1024,384]{1,0:T(8,128)(2,1)} custom-call(s32[1]{0:T(128)} %bitcast.4.place_ref, bf16[4,3,512,128]{3,2,1,0:T(8,128)(2,1)} %attend_back.2.refs_0_, bf16[4,3,512,128]{3,2,1,0:T(8,128)(2,1)} %attend_back.3.refs_1_, bf16[512,2048]{1,0:T(8,128)(2,1)} %bitcast.69, bf16[512,2048]{1,0:T(8,128)(2,1)} %bitcast.55, bf16[512,2048]{1,0:T(8,128)(2,1)} %bitcast.59, ...), custom_call_target="tpu_custom_call" | custom-call | flops 12582912 | bytes 45056 | tf_op jit(solution)/shard_map/joint_grad/pallas_call | solution.py:442
  732.2 13.7 %collective-permute-start.44 = (f32[14336]{0:T(1024)S(1)}, f32[14336]{0:T(1024)S(1)}, u32[]{:S(2)}, u32[]{:S(2)}) collective-permute-start(f32[14336]{0:T(1024)S(1)} %add.158), channel_id=1, source_target_pairs={{0,8},{8,0},{4,12},{12,4},{1,9},{9,1},{5,13},{13,5},{2,10},{10,2},... | collective-permute-start | bytes 172040 | tf_op jit(solution)/shard_map/ppermute | solution.py:1030
  750.3 10.0 %all-to-all-done.6.left_ref = bf16[4,3,512,128]{3,2,1,0:T(8,128)(2,1)} async-done(((bf16[4,3,512,128]{3,2,1,0:T(8,128)(2,1)}), bf16[4,3,512,128]{3,2,1,0:T(8,128)(2,1)}, u32[]{:S(2)}, u32[]{:S(2)}) %all-to-all-start.6) | async-done | bytes 1572896 | tf_op jit(solution)/shard_map/all_to_all | solution.py:777
  770.6 10.0 %collective-permute-done.44 = f32[14336]{0:T(1024)S(1)} collective-permute-done((f32[14336]{0:T(1024)S(1)}, f32[14336]{0:T(1024)S(1)}, u32[]{:S(2)}, u32[]{:S(2)}) %collective-permute-start.44) | collective-permute-done | bytes 57376 | tf_op jit(solution)/shard_map/ppermute | solution.py:1030
  782.7 9.3 terms.15
  794.2 18.0 %collective-permute-done.58 = bf16[1024,1024]{1,0:T(8,128)(2,1)} collective-permute-done((bf16[1024,1024]{1,0:T(8,128)(2,1)}, bf16[1024,1024]{1,0:T(8,128)(2,1)}, u32[]{:S(2)}, u32[]{:S(2)}) %collective-permute-start.58) | collective-permute-done | bytes 2097184 | tf_op jit(solution)/shard_map/ppermute | solution.py:976
  835.8 45.6 %collective-permute-done.51 = f32[1024]{0:T(1024)S(1)} collective-permute-done((f32[1024]{0:T(1024)S(1)}, f32[1024]{0:T(1024)S(1)}, u32[]{:S(2)}, u32[]{:S(2)}) %collective-permute-start.51) | collective-permute-done | bytes 4128 | tf_op jit(solution)/shard_map/ppermute | solution.py:1026
  881.4 12.0 %collective-permute-start.53 = (f32[1024]{0:T(1024)S(1)}, f32[1024]{0:T(1024)S(1)}, u32[]{:S(2)}, u32[]{:S(2)}) collective-permute-start(f32[1024]{0:T(1024)S(1)} %add.172), channel_id=1, source_target_pairs={{0,8},{8,0},{4,12},{12,4},{1,9},{9,1},{5,13},{13,5},{2,10},{10,2},... | collective-permute-start | bytes 12296 | tf_op jit(solution)/shard_map/ppermute | solution.py:1030
  921.6 11.1 %collective-permute-done.56 = bf16[1024,1024]{1,0:T(8,128)(2,1)} collective-permute-done((bf16[1024,1024]{1,0:T(8,128)(2,1)}, bf16[1024,1024]{1,0:T(8,128)(2,1)}, u32[]{:S(2)}, u32[]{:S(2)}) %collective-permute-start.56) | collective-permute-done | bytes 2097184 | tf_op jit(solution)/shard_map/ppermute | solution.py:976
  939.0 10.8 %collective-permute-done.54 = bf16[512,1024]{1,0:T(8,128)(2,1)S(1)} collective-permute-done((bf16[512,1024]{1,0:T(8,128)(2,1)S(1)}, bf16[512,1024]{1,0:T(8,128)(2,1)S(1)}, u32[]{:S(2)}, u32[]{:S(2)}) %collective-permute-start.54) | collective-permute-done | bytes 1048608 | tf_op jit(solution)/shard_map/ppermute | solution.py:976
  (404 shorter events, 454.4 us)
Async XLA Ops:
  14.9 176.1 %all-gather.5.cloned.1.call-start = ((), (), s32[]{:S(2)}) async-start(), calls=%async_computation.13 | async-start | bytes 3145728 | tf_op jit(solution)/shard_map/all_gather | solution.py:838
  45.9 220.3 %all-gather.7.cloned.1.call-start = ((), (), s32[]{:S(2)}) async-start(), calls=%async_computation.14 | async-start | bytes 12582912 | tf_op jit(solution)/shard_map/all_gather | solution.py:838
  46.7 243.1 %all-gather.9.cloned.1.call-start = ((), (), s32[]{:S(2)}) async-start(), calls=%async_computation.15 | async-start | bytes 12582912 | tf_op jit(solution)/shard_map/all_gather | solution.py:838
  191.0 180.0 %all-gather.11.cloned.1.call-start = ((), (), s32[]{:S(2)}) async-start(), calls=%async_computation.16 | async-start | bytes 9437184 | tf_op jit(solution)/shard_map/all_gather | solution.py:838
  217.5 243.1 %reduce-scatter.6.cloned.1.call-start = ((), (), s32[]{:S(2)}) async-start(), calls=%async_computation.17 | async-start | bytes 6291456 | tf_op jit(solution)/shard_map/reduce_scatter | solution.py:963
  391.3 138.3 %reduce-scatter.10.cloned.1.call-start = ((), (), s32[]{:S(2)}) async-start(), calls=%async_computation.19 | async-start | bytes 6291456 | tf_op jit(solution)/shard_map/reduce_scatter | solution.py:963
  419.2 166.4 %reduce-scatter.8.cloned.1.call-start = ((), (), s32[]{:S(2)}) async-start(), calls=%async_computation.18 | async-start | bytes 6291456 | tf_op jit(solution)/shard_map/reduce_scatter | solution.py:963
  460.6 58.5 %collective-permute-start.28 = (bf16[1024,1024]{1,0:T(8,128)(2,1)}, bf16[1024,1024]{1,0:T(8,128)(2,1)}, u32[]{:S(2)}, u32[]{:S(2)}) collective-permute-start(bf16[1024,1024]{1,0:T(8,128)(2,1)} %reduce-scatter.6.cloned.1.call-done), channel_id=1, source_target_pairs={{0,4},{12,8},{1,5},{13,9},{2,6},{14,10},{3,7},{15,11},{16,20},{28,... | collective-permute-start | bytes 6291464 | tf_op jit(solution)/shard_map/ppermute | solution.py:968
  477.6 173.0 %reduce-scatter.12.cloned.1.call-start = ((), (), s32[]{:S(2)}) async-start(), calls=%async_computation.20 | async-start | bytes 6291456 | tf_op jit(solution)/shard_map/reduce_scatter | solution.py:963
  538.7 46.9 %collective-permute-start.33 = (bf16[1024,1024]{1,0:T(8,128)(2,1)S(1)}, bf16[1024,1024]{1,0:T(8,128)(2,1)}, u32[]{:S(2)}, u32[]{:S(2)}) collective-permute-start(bf16[1024,1024]{1,0:T(8,128)(2,1)S(1)} %add_convert_fusion.7), channel_id=1, source_target_pairs={{4,8},{8,4},{5,9},{9,5},{6,10},{10,6},{7,11},{11,7},{20,24},{24,20... | collective-permute-start | bytes 6291464 | tf_op jit(solution)/shard_map/ppermute | solution.py:972
  540.8 52.2 %collective-permute-start.34 = (bf16[1024,1024]{1,0:T(8,128)(2,1)}, bf16[1024,1024]{1,0:T(8,128)(2,1)}, u32[]{:S(2)}, u32[]{:S(2)}) collective-permute-start(bf16[1024,1024]{1,0:T(8,128)(2,1)} %reduce-scatter.10.cloned.1.call-done), channel_id=1, source_target_pairs={{0,4},{12,8},{1,5},{13,9},{2,6},{14,10},{3,7},{15,11},{16,20},{28,... | collective-permute-start | bytes 6291464 | tf_op jit(solution)/shard_map/ppermute | solution.py:968
  547.9 63.6 %collective-permute-start.19 = (bf16[256,2048]{1,0:T(8,128)(2,1)}, bf16[256,2048]{1,0:T(8,128)(2,1)}, u32[]{:S(2)}, u32[]{:S(2)}) collective-permute-start(bf16[256,2048]{1,0:T(8,128)(2,1)} %get-tuple-element.170), channel_id=1, source_target_pairs={{0,1},{1,0},{2,3},{3,2},{4,5},{5,4},{6,7},{7,6},{8,9},{9,8},{10,11... | collective-permute-start | bytes 3145736 | tf_op jit(solution)/shard_map/ppermute | solution.py:42
  557.4 49.0 %all-to-all-start.4 = ((bf16[4,512,128]{2,1,0:T(8,128)(2,1)}), bf16[4,512,128]{2,1,0:T(8,128)(2,1)S(1)}, u32[]{:S(2)}, u32[]{:S(2)}) async-start(bf16[4,512,128]{2,1,0:T(8,128)(2,1)} %head_back.3), calls=%async_computation.7 | async-start | bytes 1048576 | tf_op jit(solution)/shard_map/all_to_all | solution.py:777
  596.8 53.9 %collective-permute-start.35 = (bf16[1024,1024]{1,0:T(8,128)(2,1)}, bf16[1024,1024]{1,0:T(8,128)(2,1)}, u32[]{:S(2)}, u32[]{:S(2)}) collective-permute-start(bf16[1024,1024]{1,0:T(8,128)(2,1)} %add_convert_fusion.5), channel_id=1, source_target_pairs={{4,8},{8,4},{5,9},{9,5},{6,10},{10,6},{7,11},{11,7},{20,24},{24,20... | collective-permute-start | bytes 6291464 | tf_op jit(solution)/shard_map/ppermute | solution.py:972
  599.0 56.2 %collective-permute-start.36 = (bf16[1024,1024]{1,0:T(8,128)(2,1)}, bf16[1024,1024]{1,0:T(8,128)(2,1)}, u32[]{:S(2)}, u32[]{:S(2)}) collective-permute-start(bf16[1024,1024]{1,0:T(8,128)(2,1)} %reduce-scatter.8.cloned.1.call-done), channel_id=1, source_target_pairs={{0,4},{12,8},{1,5},{13,9},{2,6},{14,10},{3,7},{15,11},{16,20},{28,... | collective-permute-start | bytes 6291464 | tf_op jit(solution)/shard_map/ppermute | solution.py:968
  606.4 78.1 %all-to-all-start.5 = ((bf16[4,3,512,128]{3,2,1,0:T(8,128)(2,1)}), bf16[4,3,512,128]{3,2,1,0:T(8,128)(2,1)}, u32[]{:S(2)}, u32[]{:S(2)}) async-start(bf16[4,3,512,128]{3,2,1,0:T(8,128)(2,1)} %attend_back.2.refs_0_), calls=%async_computation.9 | async-start | bytes 3145728 | tf_op jit(solution)/shard_map/all_to_all | solution.py:777
  610.8 115.9 %reduce-scatter.14.cloned.1.call-start = ((), (), s32[]{:S(2)}) async-start(), calls=%async_computation.21 | async-start | bytes 3145728 | tf_op jit(solution)/shard_map/reduce_scatter | solution.py:963
  649.4 74.0 %collective-permute-start.57 = (bf16[1024,1024]{1,0:T(8,128)(2,1)S(1)}, bf16[1024,1024]{1,0:T(8,128)(2,1)}, u32[]{:S(2)}, u32[]{:S(2)}) collective-permute-start(bf16[1024,1024]{1,0:T(8,128)(2,1)S(1)} %add_convert_fusion.6), channel_id=1, source_target_pairs={{4,0},{8,12},{5,1},{9,13},{6,2},{10,14},{7,3},{11,15},{20,16},{24,... | collective-permute-start | bytes 6291464 | tf_op jit(solution)/shard_map/ppermute | solution.py:976
  659.7 72.4 %collective-permute-start.42 = (bf16[1024,1024]{1,0:T(8,128)(2,1)}, bf16[1024,1024]{1,0:T(8,128)(2,1)}, u32[]{:S(2)}, u32[]{:S(2)}) collective-permute-start(bf16[1024,1024]{1,0:T(8,128)(2,1)} %add_convert_fusion.3), channel_id=1, source_target_pairs={{4,8},{8,4},{5,9},{9,5},{6,10},{10,6},{7,11},{11,7},{20,24},{24,20... | collective-permute-start | bytes 6291464 | tf_op jit(solution)/shard_map/ppermute | solution.py:972
  684.5 75.9 %all-to-all-start.6 = ((bf16[4,3,512,128]{3,2,1,0:T(8,128)(2,1)}), bf16[4,3,512,128]{3,2,1,0:T(8,128)(2,1)}, u32[]{:S(2)}, u32[]{:S(2)}) async-start(bf16[4,3,512,128]{3,2,1,0:T(8,128)(2,1)} %attend_back.3.refs_1_), calls=%async_computation.11 | async-start | bytes 3145728 | tf_op jit(solution)/shard_map/all_to_all | solution.py:777
  698.2 67.9 %collective-permute-start.43 = (bf16[1024,1024]{1,0:T(8,128)(2,1)}, bf16[1024,1024]{1,0:T(8,128)(2,1)}, u32[]{:S(2)}, u32[]{:S(2)}) collective-permute-start(bf16[1024,1024]{1,0:T(8,128)(2,1)} %reduce-scatter.12.cloned.1.call-done), channel_id=1, source_target_pairs={{0,4},{12,8},{1,5},{13,9},{2,6},{14,10},{3,7},{15,11},{16,20},{28,... | collective-permute-start | bytes 6291464 | tf_op jit(solution)/shard_map/ppermute | solution.py:968
  708.9 103.3 %collective-permute-start.58 = (bf16[1024,1024]{1,0:T(8,128)(2,1)}, bf16[1024,1024]{1,0:T(8,128)(2,1)}, u32[]{:S(2)}, u32[]{:S(2)}) collective-permute-start(bf16[1024,1024]{1,0:T(8,128)(2,1)} %add_convert_fusion.4), channel_id=1, source_target_pairs={{4,0},{8,12},{5,1},{9,13},{6,2},{10,14},{7,3},{11,15},{20,16},{24,... | collective-permute-start | bytes 6291464 | tf_op jit(solution)/shard_map/ppermute | solution.py:976
  721.9 70.1 %collective-permute-start.40 = (bf16[256,2048]{1,0:T(8,128)(2,1)}, bf16[256,2048]{1,0:T(8,128)(2,1)}, u32[]{:S(2)}, u32[]{:S(2)}) collective-permute-start(bf16[256,2048]{1,0:T(8,128)(2,1)} %add_convert_fusion.13), channel_id=1, source_target_pairs={{0,2},{1,3},{2,0},{3,1},{4,6},{5,7},{6,4},{7,5},{8,10},{9,11},{10,... | collective-permute-start | bytes 3145736 | tf_op jit(solution)/shard_map/ppermute | solution.py:47
  726.6 104.8 %collective-permute-start.50 = (bf16[512,1024]{1,0:T(8,128)(2,1)}, bf16[512,1024]{1,0:T(8,128)(2,1)}, u32[]{:S(2)}, u32[]{:S(2)}) collective-permute-start(bf16[512,1024]{1,0:T(8,128)(2,1)} %reduce-scatter.14.cloned.1.call-done), channel_id=1, source_target_pairs={{0,4},{12,8},{1,5},{13,9},{2,6},{14,10},{3,7},{15,11},{16,20},{28,... | collective-permute-start | bytes 3145736 | tf_op jit(solution)/shard_map/ppermute | solution.py:968
  732.2 48.4 %collective-permute-start.44 = (f32[14336]{0:T(1024)S(1)}, f32[14336]{0:T(1024)S(1)}, u32[]{:S(2)}, u32[]{:S(2)}) collective-permute-start(f32[14336]{0:T(1024)S(1)} %add.158), channel_id=1, source_target_pairs={{0,8},{8,0},{4,12},{12,4},{1,9},{9,1},{5,13},{13,5},{2,10},{10,2},... | collective-permute-start | bytes 172040 | tf_op jit(solution)/shard_map/ppermute | solution.py:1030
  762.4 136.1 %all-to-all-start.7 = ((bf16[4,1024,384]{1,2,0:T(8,128)(2,1)}), bf16[4,1024,384]{1,2,0:T(8,128)(2,1)S(1)}, u32[]{:S(2)}, u32[]{:S(2)}) async-start(bf16[4,1024,384]{1,2,0:T(8,128)(2,1)} %broadcast_in_dim.23), calls=%async_computation.12 | async-start | bytes 6291456 | tf_op jit(solution)/shard_map/all_to_all | solution.py:777
  766.1 128.8 %collective-permute-start.55 = (bf16[1024,1024]{1,0:T(8,128)(2,1)}, bf16[1024,1024]{1,0:T(8,128)(2,1)}, u32[]{:S(2)}, u32[]{:S(2)}) collective-permute-start(bf16[1024,1024]{1,0:T(8,128)(2,1)} %add_convert_fusion.2), channel_id=1, source_target_pairs={{4,0},{8,12},{5,1},{9,13},{6,2},{10,14},{7,3},{11,15},{20,16},{24,... | collective-permute-start | bytes 6291464 | tf_op jit(solution)/shard_map/ppermute | solution.py:976
  780.6 45.4 %collective-permute-start.49 = (bf16[1024,1024]{1,0:T(8,128)(2,1)S(1)}, bf16[1024,1024]{1,0:T(8,128)(2,1)}, u32[]{:S(2)}, u32[]{:S(2)}) collective-permute-start(bf16[1024,1024]{1,0:T(8,128)(2,1)S(1)} %add_convert_fusion.1), channel_id=1, source_target_pairs={{4,8},{8,4},{5,9},{9,5},{6,10},{10,6},{7,11},{11,7},{20,24},{24,20... | collective-permute-start | bytes 6291464 | tf_op jit(solution)/shard_map/ppermute | solution.py:972
  822.9 70.5 %collective-permute-start.46 = (bf16[256,2048]{1,0:T(8,128)(2,1)S(1)}, bf16[256,2048]{1,0:T(8,128)(2,1)S(1)}, u32[]{:S(2)}, u32[]{:S(2)}) collective-permute-start(bf16[256,2048]{1,0:T(8,128)(2,1)S(1)} %add_convert_fusion.11), channel_id=1, source_target_pairs={{0,2},{1,3},{2,0},{3,1},{4,6},{5,7},{6,4},{7,5},{8,10},{9,11},{10,... | collective-permute-start | bytes 3145736 | tf_op jit(solution)/shard_map/ppermute | solution.py:47
  824.4 57.0 %collective-permute-start.51 = (f32[1024]{0:T(1024)S(1)}, f32[1024]{0:T(1024)S(1)}, u32[]{:S(2)}, u32[]{:S(2)}) collective-permute-start(f32[1024]{0:T(1024)S(1)} %fusion.21), channel_id=1, source_target_pairs={{0,4},{4,0},{8,12},{12,8},{1,5},{5,1},{9,13},{13,9},{2,6},{6,2},{1... | collective-permute-start | bytes 12296 | tf_op jit(solution)/shard_map/ppermute | solution.py:1026
  830.0 102.7 %collective-permute-start.56 = (bf16[1024,1024]{1,0:T(8,128)(2,1)}, bf16[1024,1024]{1,0:T(8,128)(2,1)}, u32[]{:S(2)}, u32[]{:S(2)}) collective-permute-start(bf16[1024,1024]{1,0:T(8,128)(2,1)} %add_convert_fusion), channel_id=1, source_target_pairs={{4,0},{8,12},{5,1},{9,13},{6,2},{10,14},{7,3},{11,15},{20,16},{24,... | collective-permute-start | bytes 6291464 | tf_op jit(solution)/shard_map/ppermute | solution.py:976
  834.1 75.1 %collective-permute-start.52 = (bf16[512,1024]{1,0:T(8,128)(2,1)}, bf16[512,1024]{1,0:T(8,128)(2,1)}, u32[]{:S(2)}, u32[]{:S(2)}) collective-permute-start(bf16[512,1024]{1,0:T(8,128)(2,1)} %add_convert_fusion.9), channel_id=1, source_target_pairs={{4,8},{8,4},{5,9},{9,5},{6,10},{10,6},{7,11},{11,7},{20,24},{24,20... | collective-permute-start | bytes 3145736 | tf_op jit(solution)/shard_map/ppermute | solution.py:972
  (112 other events, 1519.6 us)
Sparse Core Ops, SparseCore 0:
  46.0 31.3 all-gather.4
  78.9 103.9 all-gather.6
  184.5 104.0 all-gather.8
  290.7 80.2 all-gather.10
  391.4 54.3 reduce-scatter.5
  448.6 54.2 reduce-scatter.9
  505.7 54.3 reduce-scatter.7
  563.1 54.2 reduce-scatter.11
  619.6 33.6 reduce-scatter.13

commit v4 on v3

--- a/solution.py
+++ b/solution.py
@@ -713,9 +713,9 @@
 
 def by_tokens(kernel, name, inputs, vectors, outs, sums=0):
     tokens, width = inputs[0][0].shape
-    tile = tokens // 4
+    tile = tokens // 2
     specs = [
-        pl.BlockSpec((tile, v.shape[1]), lambda i, a=at: (a * 4 + i, 0)) for v, at in inputs
+        pl.BlockSpec((tile, v.shape[1]), lambda i, a=at: (a * 2 + i, 0)) for v, at in inputs
     ]
     out_specs = [pl.BlockSpec((tile, columns), lambda i: (i, 0)) for columns, _ in outs]
     out_shape = [like((tokens, columns), dtype) for columns, dtype in outs]
@@ -724,7 +724,7 @@
         out_shape.append(like((sums, width), F32))
     return pl.pallas_call(
         kernel,
-        grid=(4,),
+        grid=(2,),
         in_specs=specs + [pl.BlockSpec(vectors.shape, lambda i: (0, 0))],
         out_specs=out_specs,
         out_shape=out_shape,
@@ -815,8 +815,8 @@
         return value.reshape(rows * half, width)
 
     x_near, x_far = [flat(x_rows[:, :half])], [flat(x_rows[:, half:])]
-    quarter, seg = lax.optimization_barrier((quarter, seg))
     first_quarter = shift(quarter, "ctx", 1)
+    first_quarter, seg = lax.optimization_barrier((first_quarter, seg))
     heads_all = [project(x_near[0], x_far[0], rows, head_weight, head_bias)]
     second_quarter = shift(first_quarter, "ctx", 1)
     x_near.append(joined(first_quarter, chip_swap(first_quarter)))
@@ -826,7 +826,7 @@
     x_near.append(joined(second_quarter, chip_swap(second_quarter)))
     x_far.append(core_swap(x_near[2]))
     heads_all.append(project(x_near[2], x_far[2], rows, head_weight, head_bias))
-    third_other = chip_swap(after(third_quarter, heads_all[0], x_near[2]))
+    third_other = chip_swap(after(third_quarter, heads_all[0]))
     third_quarter = after(third_quarter, heads_all[1], heads_all[2])
     x_near.append(joined(third_quarter, third_other))
     x_far.append(core_swap(x_near[3]))
@@ -882,6 +882,7 @@
     totals = [middle(*parts[r][:2]) for r in each]
 
     normal_one, inverse_one, norm_low = [], [], []
+    act_low, slopes = [], []
     for r in each:
         near, far = totals[r]
         normal, inverse, low = by_tokens(
@@ -895,11 +896,8 @@
         normal_one.append(normal)
         inverse_one.append(inverse)
         norm_low.append(both(low))
-
-    act_low, slopes = [], []
-    for r in each:
         near, far = norm_low[r]
-        act, slope = up_project(fsdp_place, order.ready(near), far, up_full, up_bias[None])
+        act, slope = up_project(order.ready(fsdp_place), near, far, up_full, up_bias[None])
         order.done(act)
         act_low.append(act)
         slopes.append(slope)

time: 965 us -> 957 us (level)
  blocking collectives: 0 us -> 22.1 us
  waiting for transfers between devices: 352 us -> 336 us
  starting transfers between devices: 144 us -> 130 us
    all_to_all x0 -> x1, blocking collectives: none -> 22.1 us  [swap_ctx(): return lax.all_to_all(value, 'ctx', 0, 0, tiled=True)]
    ppermute x7, waiting for transfers between devices: 40.9 us -> 20.9 us  [shift(): lax.ppermute(value, axis, [(i, (i + by) % size) for i in range(size)])]
    all_to_all x8 -> x7, starting transfers between devices: 45.6 us -> 27.4 us  [swap_ctx(): return lax.all_to_all(value, 'ctx', 0, 0, tiled=True)]
    unnamed x138 -> x136, local copies, waits for them, and re-layouts: 24.9 us -> 21.1 us
    all_to_all x8 -> x7, waiting for transfers between devices: 72.1 us -> 72.6 us  [swap_ctx(): return lax.all_to_all(value, 'ctx', 0, 0, tiled=True)]
  transfers between devices with their start and end apart: 76 -> 75, of which waited for: 30 -> 29; matrix products, arithmetic and copies ran while one was open for 14% -> 15% of each run, Pallas kernels for 30% -> 29%
where the time goes in v4:
time: 957 us; the launch traced here: 951 us
  waiting for transfers between devices  336 us (35%)
  Pallas kernels  288 us (30%)
  starting transfers between devices  130 us (14%)
  other arithmetic  115 us (12%)
  local copies, waits for them, and re-layouts  44.1 us (5%)
  blocking collectives  22.1 us (2%)
  between operations  15.4 us (2%)
    pallas_call x14, Pallas kernels, grid_call(): pl.pallas_call(kernel, grid_spec=pltpu.PrefetchScalarGridSpec(num_scalar_...  116 us
    ppermute x11, waiting for transfers between devices, chip_swap(): return lax.ppermute(value, 'tp', [(i, i ^ 2) for i in range(size)])  96.5 us
    all_to_all x7, waiting for transfers between devices, swap_ctx(): return lax.all_to_all(value, 'ctx', 0, 0, tiled=True)  72.6 us
    ppermute x2, waiting for transfers between devices, small_start(): return (value, lax.ppermute(value, 'ctx', [(0, 1), (1, 0), (2, 3), (3, 2)]))  63 us
    pallas_call x5, Pallas kernels, weight_grad(): pl.pallas_call(functools.partial(grad_kernel, len(pairs)), grid_spec=pltp...  42.5 us
    ppermute x5, waiting for transfers between devices, line_three(): return (total, lax.ppermute(total, 'ctx', [(1, 0), (2, 3)]))  35.8 us
    pallas_call x2, Pallas kernels, attend_back(): pl.pallas_call(functools.partial(attend_back_kernel, parts, query_block,...  35 us
    ppermute x5, starting transfers between devices, line_one(): return (value, lax.ppermute(value, 'ctx', [(0, 1), (3, 2)]))  30.9 us
  transfers between devices with their start and end apart: 75, of which 29 were waited for; matrix products, arithmetic and copies ran while one was open for 15% of the time, Pallas kernels for 29%

profile of v4, /device:TPU:0, one launch (start us, length us, event | category | flops | bytes accessed | tf_op | source)
XLA Modules:
  0.0 950.6 jit_solution(2959017099906122210)
XLA Ops:
  15.5 22.1 %all_to_all.40 = s32[4,2,512]{2,1,0:T(2,128)S(1)} all-to-all(s32[4,2,512]{2,1,0:T(2,128)S(1)} %broadcast_in_dim.17), channel_id=1, replica_groups=mesh['fsdp'=2,'ctx'=4,'tp'=4] {'ctx'}, dimensions={0} | all-to-all | bytes 32768 | tf_op jit(solution)/shard_map/all_to_all | solution.py:777
  47.1 17.6 %collective-permute-done.2 = bf16[2,128,2048]{2,1,0:T(8,128)(2,1)S(1)} collective-permute-done((bf16[2,128,2048]{2,1,0:T(8,128)(2,1)}, bf16[2,128,2048]{2,1,0:T(8,128)(2,1)S(1)}, u32[]{:S(2)}, u32[]{:S(2)}) %collective-permute-start.2) | collective-permute-done | bytes 1048608 | tf_op jit(solution)/shard_map/ppermute | solution.py:52
  69.6 18.5 %collective-permute-done.6 = bf16[2,128,2048]{2,1,0:T(8,128)(2,1)} collective-permute-done((bf16[2,128,2048]{2,1,0:T(8,128)(2,1)S(1)}, bf16[2,128,2048]{2,1,0:T(8,128)(2,1)}, u32[]{:S(2)}, u32[]{:S(2)}) %collective-permute-start.6) | collective-permute-done | bytes 1048608 | tf_op jit(solution)/shard_map/ppermute | solution.py:47
  117.8 13.4 %collective-permute-done.8 = bf16[2,128,2048]{2,1,0:T(8,128)(2,1)S(1)} collective-permute-done((bf16[2,128,2048]{2,1,0:T(8,128)(2,1)}, bf16[2,128,2048]{2,1,0:T(8,128)(2,1)S(1)}, u32[]{:S(2)}, u32[]{:S(2)}) %collective-permute-start.8) | collective-permute-done | bytes 1048608 | tf_op jit(solution)/shard_map/ppermute | solution.py:47
  145.6 11.9 %attend.2 = (bf16[4,512,128]{2,1,0:T(8,128)(2,1)}, f32[128,2048]{1,0:T(8,128)}, f32[1,2048]{1,0:T(1,128)}) custom-call(s32[2,4]{1,0:T(2,128)} %get-tuple-element.292.live, s32[1]{0:T(128)} %bitcast.4.place_ref, bf16[3,1024,128]{2,1,0:T(8,128)(2,1)} %project.4.refs_0_, bf16[3,1024,128]{2,1,0:T(8,128)(2,1)} %project.5.refs_1_, ...), custom_call_target="tpu_custom_call" | custom-call | flops 8388608 | bytes 8192 | tf_op jit(solution)/shard_map/attend/pallas_call | solution.py:540
  161.1 11.9 %attend.3 = (bf16[4,512,128]{2,1,0:T(8,128)(2,1)}, f32[128,2048]{1,0:T(8,128)}, f32[1,2048]{1,0:T(1,128)}) custom-call(s32[2,4]{1,0:T(2,128)} %get-tuple-element.293.live, s32[1]{0:T(128)} %bitcast.4.place_ref, bf16[3,1024,128]{2,1,0:T(8,128)(2,1)} %project.4.refs_0_, bf16[3,1024,128]{2,1,0:T(8,128)(2,1)} %project.5.refs_1_, ...), custom_call_target="tpu_custom_call" | custom-call | flops 8388608 | bytes 8192 | tf_op jit(solution)/shard_map/attend/pallas_call | solution.py:540
  185.3 15.3 %all-to-all-done.2.left_ref = bf16[4,512,128]{2,1,0:T(8,128)(2,1)S(1)} async-done(((bf16[4,512,128]{2,1,0:T(8,128)(2,1)}), bf16[4,512,128]{2,1,0:T(8,128)(2,1)S(1)}, u32[]{:S(2)}, u32[]{:S(2)}) %all-to-all-start.2) | async-done | bytes 524320 | tf_op jit(solution)/shard_map/all_to_all | solution.py:777
  214.7 19.4 %collective-permute-done.12.far = bf16[256,2048]{1,0:T(8,128)(2,1)} collective-permute-done((bf16[256,2048]{1,0:T(8,128)(2,1)S(1)}, bf16[256,2048]{1,0:T(8,128)(2,1)}, u32[]{:S(2)}, u32[]{:S(2)}) %collective-permute-start.12) | collective-permute-done | bytes 1048608 | tf_op jit(solution)/shard_map/ppermute | solution.py:47
  242.6 10.8 %up_project.2 = (bf16[512,2048]{1,0:T(8,128)(2,1)}, bf16[512,2048]{1,0:T(8,128)(2,1)}) custom-call(s32[1]{0:T(128)} %bitcast.place_ref, bf16[256,2048]{1,0:T(8,128)(2,1)} %get-tuple-element.212.near.refs_0_, bf16[256,2048]{1,0:T(8,128)(2,1)} %copy-done.7, bf16[2048,2048]{1,0:T(8,128)(2,1)} %all-gather.7.cloned.1.call-done.refs_0_.refs_1_, ...), custom_call_target="tpu_custom_call" | custom-call | flops 16777216 | bytes 57344 | tf_op jit(solution)/shard_map/up_project/pallas_call | solution.py:116
  264.0 10.8 %up_project.3 = (bf16[512,2048]{1,0:T(8,128)(2,1)}, bf16[512,2048]{1,0:T(8,128)(2,1)}) custom-call(s32[1]{0:T(128)} %bitcast.place_ref, bf16[256,2048]{1,0:T(8,128)(2,1)} %get-tuple-element.156.near.refs_4_, bf16[256,2048]{1,0:T(8,128)(2,1)} %copy-done.8, bf16[2048,2048]{1,0:T(8,128)(2,1)} %all-gather.7.cloned.1.call-done.refs_0_.refs_1_, ...), custom_call_target="tpu_custom_call" | custom-call | flops 16777216 | bytes 57344 | tf_op jit(solution)/shard_map/up_project/pallas_call | solution.py:116
  292.9 9.9 %terms.11 = (bf16[256,2048]{1,0:T(8,128)(2,1)}, f32[256,2048]{1,0:T(8,128)}) custom-call(s32[1]{0:T(128)} %bitcast.place_ref, bf16[512,2048]{1,0:T(8,128)(2,1)} %get-tuple-element.158.left_ref.refs_4_.refs_6_, bf16[2048,2048]{1,0:T(8,128)(2,1)} %all-gather.9.cloned.1.call-done.refs_0_.refs_1_, bf16[2048,2048]{1,0:T(8,128)(2,1)} %all-gather.9.cloned.1.call-done.refs_0_.refs_1_), custom_call_target="tpu_custom_call" | custom-call | flops 16777216 | bytes 53248 | tf_op jit(solution)/shard_map/terms/pallas_call | solution.py:116
  307.6 21.1 %collective-permute-done.18.far = bf16[256,2048]{1,0:T(8,128)(2,1)S(1)} collective-permute-done((bf16[256,2048]{1,0:T(8,128)(2,1)S(1)}, bf16[256,2048]{1,0:T(8,128)(2,1)S(1)}, u32[]{:S(2)}, u32[]{:S(2)}) %collective-permute-start.18) | collective-permute-done | bytes 1048608 | tf_op jit(solution)/shard_map/ppermute | solution.py:47
  339.5 9.6 %act_back.2 = (bf16[512,2048]{1,0:T(8,128)(2,1)}, f32[1,2048]{1,0:T(1,128)}) custom-call(s32[1]{0:T(128)} %bitcast.place_ref, bf16[256,2048]{1,0:T(8,128)(2,1)} %get-tuple-element.172.near.refs_1_, bf16[256,2048]{1,0:T(8,128)(2,1)} %copy-done.9, bf16[2048,2048]{1,0:T(8,128)(2,1)} %all-gather.9.cloned.1.call-done.refs_0_.refs_1_, ...), custom_call_target="tpu_custom_call" | custom-call | flops 16777216 | bytes 57344 | tf_op jit(solution)/shard_map/act_back/pallas_call | solution.py:116
  349.0 9.6 %terms.12 = (bf16[256,2048]{1,0:T(8,128)(2,1)}, f32[256,2048]{1,0:T(8,128)}) custom-call(s32[1]{0:T(128)} %bitcast.place_ref, bf16[512,2048]{1,0:T(8,128)(2,1)} %get-tuple-element.174.left_ref.refs_1_.refs_3_, bf16[2048,2048]{1,0:T(8,128)(2,1)} %all-gather.7.cloned.1.call-done.refs_0_.refs_1_, bf16[2048,2048]{1,0:T(8,128)(2,1)} %all-gather.7.cloned.1.call-done.refs_0_.refs_1_), custom_call_target="tpu_custom_call" | custom-call | flops 16777216 | bytes 53248 | tf_op jit(solution)/shard_map/terms/pallas_call | solution.py:116
  383.2 10.0 %act_back.3 = (bf16[512,2048]{1,0:T(8,128)(2,1)}, f32[1,2048]{1,0:T(1,128)}) custom-call(s32[1]{0:T(128)} %bitcast.place_ref, bf16[256,2048]{1,0:T(8,128)(2,1)} %get-tuple-element.185.refs_5_.near, bf16[256,2048]{1,0:T(8,128)(2,1)} %copy-done.10, bf16[2048,2048]{1,0:T(8,128)(2,1)} %all-gather.9.cloned.1.call-done.refs_0_.refs_1_, ...), custom_call_target="tpu_custom_call" | custom-call | flops 16777216 | bytes 57344 | tf_op jit(solution)/shard_map/act_back/pallas_call | solution.py:116
  415.4 21.4 %collective-permute-done.26.far = bf16[256,2048]{1,0:T(8,128)(2,1)S(1)} collective-permute-done((bf16[256,2048]{1,0:T(8,128)(2,1)S(1)}, bf16[256,2048]{1,0:T(8,128)(2,1)S(1)}, u32[]{:S(2)}, u32[]{:S(2)}) %collective-permute-start.26) | collective-permute-done | bytes 1048608 | tf_op jit(solution)/shard_map/ppermute | solution.py:47
  442.8 9.6 %weight_grad.7 = bf16[2048,1024]{1,0:T(8,128)(2,1)} custom-call(s32[1]{0:T(128)} %bitcast.place_ref, bf16[256,2048]{1,0:T(8,128)(2,1)} %get-tuple-element.212.near.refs_0_, bf16[512,2048]{1,0:T(8,128)(2,1)} %get-tuple-element.174.left_ref.refs_1_.refs_3_, bf16[256,2048]{1,0:T(8,128)(2,1)} %copy-done.7, ...), custom_call_target="tpu_custom_call" | custom-call | flops 16777216 | bytes 40960 | tf_op jit(solution)/shard_map/weight_grad/pallas_call | solution.py:383
  471.2 38.6 %all-to-all-done.3.refs_4_ = bf16[4,512,128]{2,1,0:T(8,128)(2,1)S(1)} async-done(((bf16[4,512,128]{2,1,0:T(8,128)(2,1)}), bf16[4,512,128]{2,1,0:T(8,128)(2,1)S(1)}, u32[]{:S(2)}, u32[]{:S(2)}) %all-to-all-start.3) | async-done | bytes 524320 | tf_op jit(solution)/shard_map/all_to_all | solution.py:777
  519.9 9.6 %weight_grad.8 = bf16[2048,1024]{1,0:T(8,128)(2,1)} custom-call(s32[1]{0:T(128)} %bitcast.place_ref, bf16[256,2048]{1,0:T(8,128)(2,1)} %get-tuple-element.212.near.refs_0_, bf16[512,2048]{1,0:T(8,128)(2,1)} %get-tuple-element.174.left_ref.refs_1_.refs_3_, bf16[256,2048]{1,0:T(8,128)(2,1)} %copy-done.7, ...), custom_call_target="tpu_custom_call" | custom-call | flops 16777216 | bytes 40960 | tf_op jit(solution)/shard_map/weight_grad/pallas_call | solution.py:383
  557.8 17.5 %attend_back.2.refs_0_ = bf16[4,3,512,128]{3,2,1,0:T(8,128)(2,1)} custom-call(s32[2,4]{1,0:T(2,128)} %get-tuple-element.292.live, s32[1]{0:T(128)} %bitcast.4.place_ref, bf16[3,1024,128]{2,1,0:T(8,128)(2,1)} %project.4.refs_0_, bf16[3,1024,128]{2,1,0:T(8,128)(2,1)} %project.5.refs_1_, bf16[3,1024,128]{2,1,0:T(8,128)(2,1)} %project.6.refs_2_, ...), custom_call_target="tpu_custom_call" | custom-call | flops 20971520 | bytes 16384 | tf_op jit(solution)/shard_map/attend_back/pallas_call | solution.py:631
  609.2 17.4 %attend_back.3.refs_1_ = bf16[4,3,512,128]{3,2,1,0:T(8,128)(2,1)} custom-call(s32[2,4]{1,0:T(2,128)} %get-tuple-element.293.live, s32[1]{0:T(128)} %bitcast.4.place_ref, bf16[3,1024,128]{2,1,0:T(8,128)(2,1)} %project.4.refs_0_, bf16[3,1024,128]{2,1,0:T(8,128)(2,1)} %project.5.refs_1_, bf16[3,1024,128]{2,1,0:T(8,128)(2,1)} %project.6.refs_2_, ...), custom_call_target="tpu_custom_call" | custom-call | flops 20971520 | bytes 16384 | tf_op jit(solution)/shard_map/attend_back/pallas_call | solution.py:631
  626.6 9.7 %joint_grad.2 = bf16[1024,384]{1,0:T(8,128)(2,1)} custom-call(s32[1]{0:T(128)} %bitcast.4.place_ref, bf16[4,3,512,128]{3,2,1,0:T(8,128)(2,1)} %attend_back.2.refs_0_, bf16[4,3,512,128]{3,2,1,0:T(8,128)(2,1)} %attend_back.3.refs_1_, bf16[512,2048]{1,0:T(8,128)(2,1)} %bitcast.64, bf16[512,2048]{1,0:T(8,128)(2,1)} %bitcast.54, ...), custom_call_target="tpu_custom_call" | custom-call | flops 12582912 | bytes 45056 | tf_op jit(solution)/shard_map/joint_grad/pallas_call | solution.py:442
  652.7 15.6 %collective-permute-done.37 = f32[14336]{0:T(1024)S(1)} collective-permute-done((f32[14336]{0:T(1024)S(1)}, f32[14336]{0:T(1024)S(1)}, u32[]{:S(2)}, u32[]{:S(2)}) %collective-permute-start.37) | collective-permute-done | bytes 57376 | tf_op jit(solution)/shard_map/ppermute | solution.py:1024
  700.7 9.9 %joint_grad.3 = bf16[1024,384]{1,0:T(8,128)(2,1)} custom-call(s32[1]{0:T(128)} %bitcast.4.place_ref, bf16[4,3,512,128]{3,2,1,0:T(8,128)(2,1)} %attend_back.2.refs_0_, bf16[4,3,512,128]{3,2,1,0:T(8,128)(2,1)} %attend_back.3.refs_1_, bf16[512,2048]{1,0:T(8,128)(2,1)} %bitcast.65, bf16[512,2048]{1,0:T(8,128)(2,1)} %bitcast.55, ...), custom_call_target="tpu_custom_call" | custom-call | flops 12582912 | bytes 45056 | tf_op jit(solution)/shard_map/joint_grad/pallas_call | solution.py:442
  722.1 13.7 %collective-permute-start.44 = (f32[14336]{0:T(1024)S(1)}, f32[14336]{0:T(1024)S(1)}, u32[]{:S(2)}, u32[]{:S(2)}) collective-permute-start(f32[14336]{0:T(1024)S(1)} %add.158), channel_id=1, source_target_pairs={{0,8},{8,0},{4,12},{12,4},{1,9},{9,1},{5,13},{13,5},{2,10},{10,2},... | collective-permute-start | bytes 172040 | tf_op jit(solution)/shard_map/ppermute | solution.py:1028
  740.3 9.4 all-to-all-done.6.left_ref
  760.0 13.7 %collective-permute-done.44 = f32[14336]{0:T(1024)S(1)} collective-permute-done((f32[14336]{0:T(1024)S(1)}, f32[14336]{0:T(1024)S(1)}, u32[]{:S(2)}, u32[]{:S(2)}) %collective-permute-start.44) | collective-permute-done | bytes 57376 | tf_op jit(solution)/shard_map/ppermute | solution.py:1028
  787.4 12.0 %collective-permute-done.58 = bf16[1024,1024]{1,0:T(8,128)(2,1)} collective-permute-done((bf16[1024,1024]{1,0:T(8,128)(2,1)}, bf16[1024,1024]{1,0:T(8,128)(2,1)}, u32[]{:S(2)}, u32[]{:S(2)}) %collective-permute-start.58) | collective-permute-done | bytes 2097184 | tf_op jit(solution)/shard_map/ppermute | solution.py:974
  823.0 47.4 %collective-permute-done.51 = f32[1024]{0:T(1024)S(1)} collective-permute-done((f32[1024]{0:T(1024)S(1)}, f32[1024]{0:T(1024)S(1)}, u32[]{:S(2)}, u32[]{:S(2)}) %collective-permute-start.51) | collective-permute-done | bytes 4128 | tf_op jit(solution)/shard_map/ppermute | solution.py:1024
  870.5 13.8 %collective-permute-start.53 = (f32[1024]{0:T(1024)S(1)}, f32[1024]{0:T(1024)S(1)}, u32[]{:S(2)}, u32[]{:S(2)}) collective-permute-start(f32[1024]{0:T(1024)S(1)} %add.172), channel_id=1, source_target_pairs={{0,8},{8,0},{4,12},{12,4},{1,9},{9,1},{5,13},{13,5},{2,10},{10,2},... | collective-permute-start | bytes 12296 | tf_op jit(solution)/shard_map/ppermute | solution.py:1028
  912.4 11.3 %collective-permute-done.56 = bf16[1024,1024]{1,0:T(8,128)(2,1)} collective-permute-done((bf16[1024,1024]{1,0:T(8,128)(2,1)}, bf16[1024,1024]{1,0:T(8,128)(2,1)}, u32[]{:S(2)}, u32[]{:S(2)}) %collective-permute-start.56) | collective-permute-done | bytes 2097184 | tf_op jit(solution)/shard_map/ppermute | solution.py:974
  929.9 12.5 %collective-permute-done.54 = bf16[512,1024]{1,0:T(8,128)(2,1)S(1)} collective-permute-done((bf16[512,1024]{1,0:T(8,128)(2,1)S(1)}, bf16[512,1024]{1,0:T(8,128)(2,1)S(1)}, u32[]{:S(2)}, u32[]{:S(2)}) %collective-permute-start.54) | collective-permute-done | bytes 1048608 | tf_op jit(solution)/shard_map/ppermute | solution.py:974
  (401 shorter events, 440.2 us)
Async XLA Ops:
  7.2 165.8 %all-gather.5.cloned.1.call-start = ((), (), s32[]{:S(2)}) async-start(), calls=%async_computation.13 | async-start | bytes 3145728 | tf_op jit(solution)/shard_map/all_gather | solution.py:838
  37.6 204.0 %all-gather.7.cloned.1.call-start = ((), (), s32[]{:S(2)}) async-start(), calls=%async_computation.14 | async-start | bytes 12582912 | tf_op jit(solution)/shard_map/all_gather | solution.py:838
  38.5 242.9 %all-gather.9.cloned.1.call-start = ((), (), s32[]{:S(2)}) async-start(), calls=%async_computation.15 | async-start | bytes 12582912 | tf_op jit(solution)/shard_map/all_gather | solution.py:838
  185.2 178.5 %all-gather.11.cloned.1.call-start = ((), (), s32[]{:S(2)}) async-start(), calls=%async_computation.16 | async-start | bytes 9437184 | tf_op jit(solution)/shard_map/all_gather | solution.py:838
  240.3 212.2 %reduce-scatter.6.cloned.1.call-start = ((), (), s32[]{:S(2)}) async-start(), calls=%async_computation.17 | async-start | bytes 6291456 | tf_op jit(solution)/shard_map/reduce_scatter | solution.py:961
  383.2 136.7 %reduce-scatter.10.cloned.1.call-start = ((), (), s32[]{:S(2)}) async-start(), calls=%async_computation.19 | async-start | bytes 6291456 | tf_op jit(solution)/shard_map/reduce_scatter | solution.py:961
  411.1 164.2 %reduce-scatter.8.cloned.1.call-start = ((), (), s32[]{:S(2)}) async-start(), calls=%async_computation.18 | async-start | bytes 6291456 | tf_op jit(solution)/shard_map/reduce_scatter | solution.py:961
  452.5 58.1 %collective-permute-start.28 = (bf16[1024,1024]{1,0:T(8,128)(2,1)}, bf16[1024,1024]{1,0:T(8,128)(2,1)}, u32[]{:S(2)}, u32[]{:S(2)}) collective-permute-start(bf16[1024,1024]{1,0:T(8,128)(2,1)} %reduce-scatter.6.cloned.1.call-done), channel_id=1, source_target_pairs={{0,4},{12,8},{1,5},{13,9},{2,6},{14,10},{3,7},{15,11},{16,20},{28,... | collective-permute-start | bytes 6291464 | tf_op jit(solution)/shard_map/ppermute | solution.py:966
  469.7 172.0 %reduce-scatter.12.cloned.1.call-start = ((), (), s32[]{:S(2)}) async-start(), calls=%async_computation.20 | async-start | bytes 6291456 | tf_op jit(solution)/shard_map/reduce_scatter | solution.py:961
  469.7 44.1 %collective-permute-start.29 = (bf16[256,2048]{1,0:T(8,128)(2,1)}, bf16[256,2048]{1,0:T(8,128)(2,1)S(1)}, u32[]{:S(2)}, u32[]{:S(2)}) collective-permute-start(bf16[256,2048]{1,0:T(8,128)(2,1)} %add_convert_fusion.14.near), channel_id=1, source_target_pairs={{0,2},{1,3},{2,0},{3,1},{4,6},{5,7},{6,4},{7,5},{8,10},{9,11},{10,... | collective-permute-start | bytes 3145736 | tf_op jit(solution)/shard_map/ppermute | solution.py:47
  529.5 45.9 %collective-permute-start.33 = (bf16[1024,1024]{1,0:T(8,128)(2,1)S(1)}, bf16[1024,1024]{1,0:T(8,128)(2,1)}, u32[]{:S(2)}, u32[]{:S(2)}) collective-permute-start(bf16[1024,1024]{1,0:T(8,128)(2,1)S(1)} %add_convert_fusion.7), channel_id=1, source_target_pairs={{4,8},{8,4},{5,9},{9,5},{6,10},{10,6},{7,11},{11,7},{20,24},{24,20... | collective-permute-start | bytes 6291464 | tf_op jit(solution)/shard_map/ppermute | solution.py:970
  531.6 51.7 %collective-permute-start.34 = (bf16[1024,1024]{1,0:T(8,128)(2,1)}, bf16[1024,1024]{1,0:T(8,128)(2,1)}, u32[]{:S(2)}, u32[]{:S(2)}) collective-permute-start(bf16[1024,1024]{1,0:T(8,128)(2,1)} %reduce-scatter.10.cloned.1.call-done), channel_id=1, source_target_pairs={{0,4},{12,8},{1,5},{13,9},{2,6},{14,10},{3,7},{15,11},{16,20},{28,... | collective-permute-start | bytes 6291464 | tf_op jit(solution)/shard_map/ppermute | solution.py:966
  538.3 64.4 %collective-permute-start.19 = (bf16[256,2048]{1,0:T(8,128)(2,1)}, bf16[256,2048]{1,0:T(8,128)(2,1)}, u32[]{:S(2)}, u32[]{:S(2)}) collective-permute-start(bf16[256,2048]{1,0:T(8,128)(2,1)} %get-tuple-element.170), channel_id=1, source_target_pairs={{0,1},{1,0},{2,3},{3,2},{4,5},{5,4},{6,7},{7,6},{8,9},{9,8},{10,11... | collective-permute-start | bytes 3145736 | tf_op jit(solution)/shard_map/ppermute | solution.py:42
  547.7 49.6 %all-to-all-start.4 = ((bf16[4,512,128]{2,1,0:T(8,128)(2,1)}), bf16[4,512,128]{2,1,0:T(8,128)(2,1)S(1)}, u32[]{:S(2)}, u32[]{:S(2)}) async-start(bf16[4,512,128]{2,1,0:T(8,128)(2,1)} %head_back.3), calls=%async_computation.7 | async-start | bytes 1048576 | tf_op jit(solution)/shard_map/all_to_all | solution.py:777
  587.2 54.5 %collective-permute-start.35 = (bf16[1024,1024]{1,0:T(8,128)(2,1)}, bf16[1024,1024]{1,0:T(8,128)(2,1)}, u32[]{:S(2)}, u32[]{:S(2)}) collective-permute-start(bf16[1024,1024]{1,0:T(8,128)(2,1)} %add_convert_fusion.5), channel_id=1, source_target_pairs={{4,8},{8,4},{5,9},{9,5},{6,10},{10,6},{7,11},{11,7},{20,24},{24,20... | collective-permute-start | bytes 6291464 | tf_op jit(solution)/shard_map/ppermute | solution.py:970
  589.4 56.8 %collective-permute-start.36 = (bf16[1024,1024]{1,0:T(8,128)(2,1)}, bf16[1024,1024]{1,0:T(8,128)(2,1)}, u32[]{:S(2)}, u32[]{:S(2)}) collective-permute-start(bf16[1024,1024]{1,0:T(8,128)(2,1)} %reduce-scatter.8.cloned.1.call-done), channel_id=1, source_target_pairs={{0,4},{12,8},{1,5},{13,9},{2,6},{14,10},{3,7},{15,11},{16,20},{28,... | collective-permute-start | bytes 6291464 | tf_op jit(solution)/shard_map/ppermute | solution.py:966
  597.4 77.1 %all-to-all-start.5 = ((bf16[4,3,512,128]{3,2,1,0:T(8,128)(2,1)}), bf16[4,3,512,128]{3,2,1,0:T(8,128)(2,1)}, u32[]{:S(2)}, u32[]{:S(2)}) async-start(bf16[4,3,512,128]{3,2,1,0:T(8,128)(2,1)} %attend_back.2.refs_0_), calls=%async_computation.9 | async-start | bytes 3145728 | tf_op jit(solution)/shard_map/all_to_all | solution.py:777
  602.0 114.6 %reduce-scatter.14.cloned.1.call-start = ((), (), s32[]{:S(2)}) async-start(), calls=%async_computation.21 | async-start | bytes 3145728 | tf_op jit(solution)/shard_map/reduce_scatter | solution.py:961
  640.4 72.9 %collective-permute-start.57 = (bf16[1024,1024]{1,0:T(8,128)(2,1)S(1)}, bf16[1024,1024]{1,0:T(8,128)(2,1)}, u32[]{:S(2)}, u32[]{:S(2)}) collective-permute-start(bf16[1024,1024]{1,0:T(8,128)(2,1)S(1)} %add_convert_fusion.6), channel_id=1, source_target_pairs={{4,0},{8,12},{5,1},{9,13},{6,2},{10,14},{7,3},{11,15},{20,16},{24,... | collective-permute-start | bytes 6291464 | tf_op jit(solution)/shard_map/ppermute | solution.py:974
  650.8 71.3 %collective-permute-start.42 = (bf16[1024,1024]{1,0:T(8,128)(2,1)}, bf16[1024,1024]{1,0:T(8,128)(2,1)}, u32[]{:S(2)}, u32[]{:S(2)}) collective-permute-start(bf16[1024,1024]{1,0:T(8,128)(2,1)} %add_convert_fusion.3), channel_id=1, source_target_pairs={{4,8},{8,4},{5,9},{9,5},{6,10},{10,6},{7,11},{11,7},{20,24},{24,20... | collective-permute-start | bytes 6291464 | tf_op jit(solution)/shard_map/ppermute | solution.py:970
  674.5 75.2 %all-to-all-start.6 = ((bf16[4,3,512,128]{3,2,1,0:T(8,128)(2,1)}), bf16[4,3,512,128]{3,2,1,0:T(8,128)(2,1)}, u32[]{:S(2)}, u32[]{:S(2)}) async-start(bf16[4,3,512,128]{3,2,1,0:T(8,128)(2,1)} %attend_back.3.refs_1_), calls=%async_computation.11 | async-start | bytes 3145728 | tf_op jit(solution)/shard_map/all_to_all | solution.py:777
  688.2 67.3 %collective-permute-start.43 = (bf16[1024,1024]{1,0:T(8,128)(2,1)}, bf16[1024,1024]{1,0:T(8,128)(2,1)}, u32[]{:S(2)}, u32[]{:S(2)}) collective-permute-start(bf16[1024,1024]{1,0:T(8,128)(2,1)} %reduce-scatter.12.cloned.1.call-done), channel_id=1, source_target_pairs={{0,4},{12,8},{1,5},{13,9},{2,6},{14,10},{3,7},{15,11},{16,20},{28,... | collective-permute-start | bytes 6291464 | tf_op jit(solution)/shard_map/ppermute | solution.py:966
  699.3 100.2 %collective-permute-start.58 = (bf16[1024,1024]{1,0:T(8,128)(2,1)}, bf16[1024,1024]{1,0:T(8,128)(2,1)}, u32[]{:S(2)}, u32[]{:S(2)}) collective-permute-start(bf16[1024,1024]{1,0:T(8,128)(2,1)} %add_convert_fusion.4), channel_id=1, source_target_pairs={{4,0},{8,12},{5,1},{9,13},{6,2},{10,14},{7,3},{11,15},{20,16},{24,... | collective-permute-start | bytes 6291464 | tf_op jit(solution)/shard_map/ppermute | solution.py:974
  711.9 73.4 %collective-permute-start.40 = (bf16[256,2048]{1,0:T(8,128)(2,1)}, bf16[256,2048]{1,0:T(8,128)(2,1)}, u32[]{:S(2)}, u32[]{:S(2)}) collective-permute-start(bf16[256,2048]{1,0:T(8,128)(2,1)} %add_convert_fusion.13), channel_id=1, source_target_pairs={{0,2},{1,3},{2,0},{3,1},{4,6},{5,7},{6,4},{7,5},{8,10},{9,11},{10,... | collective-permute-start | bytes 3145736 | tf_op jit(solution)/shard_map/ppermute | solution.py:47
  716.5 102.2 %collective-permute-start.50 = (bf16[512,1024]{1,0:T(8,128)(2,1)}, bf16[512,1024]{1,0:T(8,128)(2,1)}, u32[]{:S(2)}, u32[]{:S(2)}) collective-permute-start(bf16[512,1024]{1,0:T(8,128)(2,1)} %reduce-scatter.14.cloned.1.call-done), channel_id=1, source_target_pairs={{0,4},{12,8},{1,5},{13,9},{2,6},{14,10},{3,7},{15,11},{16,20},{28,... | collective-permute-start | bytes 3145736 | tf_op jit(solution)/shard_map/ppermute | solution.py:966
  722.1 51.6 %collective-permute-start.44 = (f32[14336]{0:T(1024)S(1)}, f32[14336]{0:T(1024)S(1)}, u32[]{:S(2)}, u32[]{:S(2)}) collective-permute-start(f32[14336]{0:T(1024)S(1)} %add.158), channel_id=1, source_target_pairs={{0,8},{8,0},{4,12},{12,4},{1,9},{9,1},{5,13},{13,5},{2,10},{10,2},... | collective-permute-start | bytes 172040 | tf_op jit(solution)/shard_map/ppermute | solution.py:1028
  751.8 137.6 %all-to-all-start.7 = ((bf16[4,1024,384]{1,2,0:T(8,128)(2,1)}), bf16[4,1024,384]{1,2,0:T(8,128)(2,1)S(1)}, u32[]{:S(2)}, u32[]{:S(2)}) async-start(bf16[4,1024,384]{1,2,0:T(8,128)(2,1)} %broadcast_in_dim.23), calls=%async_computation.12 | async-start | bytes 6291456 | tf_op jit(solution)/shard_map/all_to_all | solution.py:777
  755.5 130.3 %collective-permute-start.55 = (bf16[1024,1024]{1,0:T(8,128)(2,1)}, bf16[1024,1024]{1,0:T(8,128)(2,1)}, u32[]{:S(2)}, u32[]{:S(2)}) collective-permute-start(bf16[1024,1024]{1,0:T(8,128)(2,1)} %add_convert_fusion.2), channel_id=1, source_target_pairs={{4,0},{8,12},{5,1},{9,13},{6,2},{10,14},{7,3},{11,15},{20,16},{24,... | collective-permute-start | bytes 6291464 | tf_op jit(solution)/shard_map/ppermute | solution.py:974
  810.2 74.0 %collective-permute-start.46 = (bf16[256,2048]{1,0:T(8,128)(2,1)S(1)}, bf16[256,2048]{1,0:T(8,128)(2,1)S(1)}, u32[]{:S(2)}, u32[]{:S(2)}) collective-permute-start(bf16[256,2048]{1,0:T(8,128)(2,1)S(1)} %add_convert_fusion.11), channel_id=1, source_target_pairs={{0,2},{1,3},{2,0},{3,1},{4,6},{5,7},{6,4},{7,5},{8,10},{9,11},{10,... | collective-permute-start | bytes 3145736 | tf_op jit(solution)/shard_map/ppermute | solution.py:47
  811.7 58.8 %collective-permute-start.51 = (f32[1024]{0:T(1024)S(1)}, f32[1024]{0:T(1024)S(1)}, u32[]{:S(2)}, u32[]{:S(2)}) collective-permute-start(f32[1024]{0:T(1024)S(1)} %fusion.21), channel_id=1, source_target_pairs={{0,4},{4,0},{8,12},{12,8},{1,5},{5,1},{9,13},{13,9},{2,6},{6,2},{1... | collective-permute-start | bytes 12296 | tf_op jit(solution)/shard_map/ppermute | solution.py:1024
  817.3 106.3 %collective-permute-start.56 = (bf16[1024,1024]{1,0:T(8,128)(2,1)}, bf16[1024,1024]{1,0:T(8,128)(2,1)}, u32[]{:S(2)}, u32[]{:S(2)}) collective-permute-start(bf16[1024,1024]{1,0:T(8,128)(2,1)} %add_convert_fusion), channel_id=1, source_target_pairs={{4,0},{8,12},{5,1},{9,13},{6,2},{10,14},{7,3},{11,15},{20,16},{24,... | collective-permute-start | bytes 6291464 | tf_op jit(solution)/shard_map/ppermute | solution.py:974
  821.4 78.5 %collective-permute-start.52 = (bf16[512,1024]{1,0:T(8,128)(2,1)}, bf16[512,1024]{1,0:T(8,128)(2,1)}, u32[]{:S(2)}, u32[]{:S(2)}) collective-permute-start(bf16[512,1024]{1,0:T(8,128)(2,1)} %add_convert_fusion.9), channel_id=1, source_target_pairs={{4,8},{8,4},{5,9},{9,5},{6,10},{10,6},{7,11},{11,7},{20,24},{24,20... | collective-permute-start | bytes 3145736 | tf_op jit(solution)/shard_map/ppermute | solution.py:970
  (110 other events, 1497.3 us)
Sparse Core Ops, SparseCore 0:
  37.7 32.4 all-gather.4
  71.8 103.9 all-gather.6
  177.3 103.9 all-gather.8
  283.4 80.3 all-gather.10
  383.3 54.2 reduce-scatter.5
  440.5 54.3 reduce-scatter.9
  497.7 54.2 reduce-scatter.7
  555.0 54.3 reduce-scatter.11
  611.6 34.5 reduce-scatter.13
